TPU v7x, 32 devices: a whole 2x2x4 slice. The times are simulated.
32 devices in a mesh: row: 4 (over y, x), col: 8 (over z, core).
Axes of the slice: x: 2, y: 2, z: 4, core: 2. Of those that a mesh axis runs over, the one named last changes fastest.
Arguments:
- objects: float32 [4, 2048, 4096], P(None, 'row', 'col'), may hold values from -5 to 5
- illumination: float32 [2, 256, 256], replicated, may hold values from -5 to 5
- propagator_phase: float32 [256, 256], replicated, may hold values from -3.140625 to 3.140625
- intensity: bfloat16 [384, 256, 256], P(('row', 'col')), may hold values from 0 to 2
- offsets: int32 [384, 2], P(('row', 'col')), may hold values from -1 to 3, as said below
- counts: int32 [32], P(('row', 'col')), may hold values from 0 to 12, as said below
Outputs:
- gradient: float32 [4, 2048, 4096], P(None, 'row', 'col')
Inputs may be any that keep to these rules, and one draw needn't show every extreme that they name: `counts`: for every device, its count plus the count of the device 8 // 2 further along col (cyclically, same row) is at most 12; some device has exactly 12; every device at row index 0 has a live slot. `offsets`: the first slot of every device has column offset 512 // 128 - 1.
All inputs are finite; a program needn't handle non-finite values.
Results may differ from a plain program's by a relative error of at most 0.015.
Values may be sent and summed in bfloat16 or wider, within the bound.
No kernel may reach another device: no remote copies, remote signals or barrier semaphores. Data moves between devices by JAX's collectives and lax.ppermute only.
A program may use at most 128 MiB of HBM per device.

v0:
```python
import functools
import math

import jax
import jax.numpy as jnp
import numpy as np
from jax import lax
from jax.experimental import pallas as pl
from jax.experimental.pallas import tpu as pltpu
from jax.sharding import PartitionSpec as P


HALF = jnp.bfloat16
FULL = jnp.float32


def from_behind(x, axis, by):
    size = lax.axis_size(axis)
    pairs = [(i, i + by) for i in range(size) if 0 <= i + by < size]
    return lax.ppermute(x, axis, pairs)


def half_tables(extent):
    half = extent // 2
    number = np.arange(extent, dtype=np.int64)
    turns = (number[:, None] * number[None, :]) % extent
    angle = turns.astype(np.float32) * np.float32(2.0 * math.pi / extent)
    scale = np.float32(1.0 / math.sqrt(extent))
    cosine, sine = np.cos(angle) * scale, np.sin(angle) * scale
    tables = []
    for parity in range(2):
        c, s = cosine[parity::2, :half], sine[parity::2, :half]
        block = np.block([[c, s], [-s, c]])
        tables += [block, block.T]
    pick = np.zeros((extent, extent), np.float32)
    pick[number, np.concatenate([number[0::2], number[1::2]])] = 1.0
    tables += [pick, pick.T]
    return np.stack(tables).astype(HALF)


EVEN, EVEN_T, ODD, ODD_T, PICK, PICK_T = range(6)


def dot(left, right):
    return jnp.dot(left, right, preferred_element_type=FULL)


def beside(*parts):
    return jnp.concatenate(parts, axis=1)


def above(*parts):
    return jnp.concatenate(parts, axis=0)


def butterfly(x, n):
    top, bottom = x[:n] + x[n:], x[:n] - x[n:]
    return [
        beside(y[:, :n] + y[:, n:], y[:, :n] - y[:, n:]).astype(HALF) for y in (top, bottom)
    ]


def paired(first, second, side, n):
    cols = slice(side * n, side * n + n)
    return above(
        beside(first[:n, cols], first[n:, cols]), beside(second[:n, cols], second[n:, cols])
    )


def forward(real, imag, tab, n):
    even_real, odd_real = butterfly(real, n)
    even_imag, odd_imag = butterfly(imag, n)
    yield
    even = dot(tab[EVEN], above(even_real, even_imag)).astype(HALF)
    odd = dot(tab[ODD], above(odd_real, odd_imag)).astype(HALF)
    result = (
        dot(paired(even, odd, 0, n), tab[EVEN_T]),
        dot(paired(even, odd, 1, n), tab[ODD_T]),
    )
    yield
    return result


def inverse(even_cols, odd_cols, tab, n):
    yield

    def left(rows, table):
        stacked = above(
            beside(even_cols[rows, :n], odd_cols[rows, :n]),
            beside(even_cols[rows, n:], odd_cols[rows, n:]),
        )
        return dot(tab[table], stacked).astype(HALF)

    first, second = left(slice(0, n), EVEN_T), left(slice(n, 2 * n), ODD_T)
    even = dot(paired(first, second, 0, n), tab[EVEN])
    odd = dot(paired(first, second, 1, n), tab[ODD])
    yield
    low, high = [above(y[:n] + y[n:], y[:n] - y[n:]) for y in (even + odd, even - odd)]
    return beside(low[:, :n], high[:, :n]), beside(low[:, n:], high[:, n:])


def slot_steps(light, spread, plane, measured, tab, put, n):
    def turned(y, col, sign):
        h_real, h_imag = spread(0, col), sign * spread(1, col)
        real, imag = y[:, :n], y[:, n:]
        return beside(
            (h_real * real - h_imag * imag).astype(HALF),
            (h_real * imag + h_imag * real).astype(HALF),
        )

    def pull(y, level):
        real, imag = y[:, :n], y[:, n:]
        misfit = real * real + imag * imag - level
        return beside((misfit * real).astype(HALF), (misfit * imag).astype(HALF))

    p_real, p_imag = light(0), light(1)
    o_real, o_imag = plane(0), plane(1)
    even, odd = yield from forward(
        p_real * o_real - p_imag * o_imag, p_real * o_imag + p_imag * o_real, tab, n
    )
    passed_real, passed_imag = yield from inverse(turned(even, 0, 1.0), turned(odd, n, 1.0), tab, n)
    o_real, o_imag = plane(2), plane(3)
    even, odd = yield from forward(
        passed_real * o_real - passed_imag * o_imag,
        passed_real * o_imag + passed_imag * o_real,
        tab,
        n,
    )
    level = dot(dot(tab[PICK], measured()).astype(HALF), tab[PICK_T])
    back_real, back_imag = yield from inverse(
        pull(even, level[:, :n]), pull(odd, level[:, n:]), tab, n
    )
    put(2, passed_real * back_real + passed_imag * back_imag)
    put(3, passed_real * back_imag - passed_imag * back_real)
    o_real, o_imag = plane(2), plane(3)
    even, odd = yield from forward(
        o_real * back_real + o_imag * back_imag, o_real * back_imag - o_imag * back_real, tab, n
    )
    start_real, start_imag = yield from inverse(
        turned(even, 0, -1.0), turned(odd, n, -1.0), tab, n
    )
    p_real, p_imag = light(0), light(1)
    put(0, p_real * start_real + p_imag * start_imag)
    put(1, p_real * start_imag - p_imag * start_real)


def alternate(generators):
    waiting = list(generators)
    while waiting:
        waiting = [g for g in waiting if next(g, waiting) is not waiting]


def selected(x, tab):
    result = None
    for _ in range(3):
        part = x.astype(HALF)
        x = x - part.astype(FULL)
        moved = dot(dot(tab[PICK], part).astype(HALF), tab[PICK_T])
        result = moved if result is None else result + moved
    return result


INSIDE, BESIDE, OVER, CORNER = range(4)
VMEM = pl.BlockSpec(memory_space=pltpu.VMEM)
SMEM = pl.BlockSpec(memory_space=pltpu.SMEM)
ANYWHERE = pl.BlockSpec(memory_space=pl.ANY)


def run_copies(moves, sems):
    copies = [
        pltpu.make_async_copy(source, target, sems.at[i])
        for i, (source, target) in enumerate(moves)
    ]
    for copy in copies:
        copy.start()
    for copy in copies:
        copy.wait()


def strips_kernel(first, last, top, bottom):
    top[...] = first[...].astype(HALF)
    bottom[...] = last[...].astype(HALF)


def strips(objects, n):
    planes, rows, cols = objects.shape
    block = (1, n, cols)
    out = jax.ShapeDtypeStruct((planes, n, cols), HALF)
    return pl.pallas_call(
        strips_kernel,
        grid=(planes,),
        in_specs=[
            pl.BlockSpec(block, lambda k: (k, 0, 0)),
            pl.BlockSpec(block, lambda k: (k, rows // n - 1, 0)),
        ],
        out_specs=[pl.BlockSpec(block, lambda k: (k, 0, 0))] * 2,
        out_shape=[out, out],
        compiler_params=pltpu.CompilerParams(vmem_limit_bytes=60 << 20),
        name="strips",
    )(objects, objects)


def prepare_kernel(n, objects, window, left, right):
    planes, tile = objects.shape[:2]
    for k in range(planes):
        plane = objects[k].astype(HALF)
        window[k, n : n + tile, n : n + tile] = plane
        left[k] = plane[:, :n]
        right[k] = plane[:, tile - n :]


def prepare(objects, n):
    planes, tile = objects.shape[:2]
    side = jax.ShapeDtypeStruct((planes, tile, n), HALF)
    return pl.pallas_call(
        functools.partial(prepare_kernel, n),
        in_specs=[VMEM],
        out_specs=[VMEM] * 3,
        out_shape=[
            jax.ShapeDtypeStruct((planes, tile + 2 * n, tile + 2 * n), HALF),
            side,
            side,
        ],
        compiler_params=pltpu.CompilerParams(vmem_limit_bytes=16 << 20),
        name="prepare",
    )(objects)


def slots_kernel(mode, offsets, counts, tab, light, spread, measured, *refs):
    order, sems = refs[-2:]
    slot_count, extent = measured.shape[:2]
    n = extent // 2
    if mode == INSIDE:
        window, total, spread_out = refs[:3]
    else:
        sources, (window, total), outs = refs[:2], refs[4:6], refs[6:-2]
    tile = window.shape[1] - 2 * n
    inner, first, last = pl.ds(n, tile), pl.ds(0, n), pl.ds(n + tile, n)

    if mode == INSIDE:

        def clear(i, carry):
            at = pl.ds(pl.multiple_of(32 * i, 32), 32)
            total[:, at] = jnp.zeros((4, 32, total.shape[2]), FULL)
            return carry

        lax.fori_loop(0, total.shape[1] // 32, clear, 0)
        phase = spread[...]
        spread_out[0] = selected(jnp.cos(phase), tab)
        spread_out[1] = selected(jnp.sin(phase), tab)
        spread = spread_out
    else:
        one, two = sources
        if mode == BESIDE:
            moves = [(one, (inner, first)), (two, (inner, last))]
        elif mode == OVER:
            moves = [(one, (first, inner)), (two, (last, inner))]
        else:
            moves = [
                (side.at[:, pl.ds(at, n)], (rows, cols))
                for side, cols in ((one, first), (two, last))
                for at, rows in ((0, first), (n, last))
            ]
        run_copies([(source, window.at[(slice(None), *at)]) for source, at in moves], sems)

    def within(at):
        return (at >= 0) & ((at + 2) * n <= tile)

    def choose(j, found):
        row_in, col_in = within(offsets[0, j]), within(offsets[1, j])
        wanted = j < counts[0]
        wanted &= row_in if mode in (INSIDE, BESIDE) else jnp.logical_not(row_in)
        wanted &= col_in if mode in (INSIDE, OVER) else jnp.logical_not(col_in)

        @pl.when(wanted)
        def _():
            order[found] = j

        return found + wanted.astype(jnp.int32)

    found = lax.fori_loop(0, slot_count, choose, jnp.int32(0))

    def steps(at):
        slot = order[at]
        row = pl.multiple_of((offsets[0, slot] + 1) * n, n)
        col = pl.multiple_of((offsets[1, slot] + 1) * n, n)
        here = (pl.ds(row, extent), pl.ds(col, extent))

        def put(k, value):
            total[(k, *here)] += value

        return slot_steps(
            lambda k: light[k],
            lambda k, at: spread[k, :, at : at + n],
            lambda k: window[(k, *here)].astype(FULL),
            lambda: measured[slot],
            tab,
            put,
            n,
        )

    def both(i, carry):
        alternate([steps(2 * i), steps(2 * i + 1)])
        return carry

    lax.fori_loop(0, found // 2, both, 0)

    @pl.when(found % 2 == 1)
    def _():
        alternate([steps(found - 1)])

    if mode == BESIDE:
        outs[0][...] = total[0, :8, :128]
    if mode == OVER:
        for k in range(4):
            for d, rows in enumerate((first, last)):
                outs[d][k] = total[k, rows, pl.ds(2 * n, tile - 2 * n)].astype(HALF)
    if mode == CORNER:
        ends, edge = outs[:2], outs[2]
        for k in range(4):
            for e, (cols, edge_cols) in enumerate(((first, pl.ds(n, n)), (last, pl.ds(tile, n)))):
                for d, rows in enumerate((first, last)):
                    ends[e][d, k] = total[k, rows, cols].astype(HALF)
                    edge[d, e, k] = total[k, rows, edge_cols]


def run_slots(mode, scalars, constants, window, total=None, sources=()):
    _, _, _, measured = constants
    slot_count, extent = measured.shape[:2]
    n = extent // 2
    tile = window.shape[1] - 2 * n
    square = (4, n, n)
    outs = {
        INSIDE: [(window.shape, FULL), ((2, extent, extent), FULL)],
        BESIDE: [((8, 128), FULL)],
        OVER: [((4, n, tile - 2 * n), HALF)] * 2,
        CORNER: [((2, *square), HALF)] * 2 + [((2, 2, *square), FULL)],
    }[mode]
    operands = [*scalars, *constants]
    specs = [SMEM, SMEM, VMEM, VMEM, VMEM, VMEM]
    aliases = {}
    if mode == INSIDE:
        operands += [window]
        specs += [VMEM]
    else:
        operands += [*sources, window, total]
        specs += [ANYWHERE, ANYWHERE, VMEM, VMEM]
        aliases = {8: 0, 9: 1}
        outs = [(window.shape, HALF), (total.shape, FULL)] + outs
    return pl.pallas_call(
        functools.partial(slots_kernel, mode),
        out_shape=[jax.ShapeDtypeStruct(*out) for out in outs],
        in_specs=specs,
        out_specs=[VMEM] * len(outs),
        scratch_shapes=[pltpu.SMEM((slot_count,), jnp.int32), pltpu.SemaphoreType.DMA((4,))],
        input_output_aliases=aliases,
        compiler_params=pltpu.CompilerParams(vmem_limit_bytes=24 << 20),
        cost_estimate=pl.CostEstimate(
            flops=3 * 52 * extent**3, bytes_accessed=0, transcendentals=0
        ),
    )(*operands)


def turn_kernel(n, over, below, token, to_left, to_right):
    tile = over.shape[2]
    for d, band in enumerate((over, below)):
        to_left[:, d * n : (d + 1) * n] = band[:, :, :n]
        to_right[:, d * n : (d + 1) * n] = band[:, :, tile - n :]


def turn(over, below, token):
    planes, n, _ = over.shape
    out = jax.ShapeDtypeStruct((planes, 2 * n, n), HALF)
    return pl.pallas_call(
        functools.partial(turn_kernel, n),
        out_shape=[out, out],
        in_specs=[VMEM] * 3,
        out_specs=[VMEM] * 2,
        compiler_params=pltpu.CompilerParams(vmem_limit_bytes=8 << 20),
        name="turn",
    )(over, below, token)


def sides_kernel(n, total, token, left, right):
    tile = left.shape[1]
    for k in range(left.shape[0]):
        left[k] = total[k, pl.ds(n, tile), pl.ds(0, n)].astype(HALF)
        right[k] = total[k, pl.ds(n, tile), pl.ds(n + tile, n)].astype(HALF)


def sides(total, token, n):
    out = jax.ShapeDtypeStruct((total.shape[0], total.shape[1] - 2 * n, n), HALF)
    return pl.pallas_call(
        functools.partial(sides_kernel, n),
        out_shape=[out, out],
        in_specs=[VMEM] * 2,
        out_specs=[VMEM] * 2,
        compiler_params=pltpu.CompilerParams(vmem_limit_bytes=8 << 20),
        name="sides",
    )(total, token)


def join_kernel(edge, from_left, from_right, up, down):
    for d, out in enumerate((up, down)):
        out[0] = (edge[d, 0] + from_left[d].astype(FULL)).astype(HALF)
        out[1] = (edge[d, 1] + from_right[d].astype(FULL)).astype(HALF)


def join(edge, from_left, from_right):
    out = jax.ShapeDtypeStruct(edge.shape[1:], HALF)
    return pl.pallas_call(
        join_kernel,
        out_shape=[out, out],
        in_specs=[VMEM] * 3,
        out_specs=[VMEM] * 2,
        compiler_params=pltpu.CompilerParams(vmem_limit_bytes=8 << 20),
        name="join",
    )(edge, from_left, from_right)


def settle_kernel(n, from_left, from_right, total_in, total, out, sems):
    tile = out.shape[1]
    inner = pl.ds(n, tile)
    for k in range(4):
        total[k, inner, pl.ds(n, n)] += from_left[k].astype(FULL)
        total[k, inner, pl.ds(tile, n)] += from_right[k].astype(FULL)
    rows = tile - 2 * n
    run_copies([(total.at[:, pl.ds(2 * n, rows), inner], out.at[:, pl.ds(n, rows)])], sems)


def settle(total, from_left, from_right, n):
    planes, tile = from_left.shape[:2]
    return pl.pallas_call(
        functools.partial(settle_kernel, n),
        out_shape=[
            jax.ShapeDtypeStruct(total.shape, FULL),
            jax.ShapeDtypeStruct((planes, tile, tile), FULL),
        ],
        in_specs=[VMEM] * 3,
        out_specs=[VMEM, ANYWHERE],
        scratch_shapes=[pltpu.SemaphoreType.DMA((1,))],
        input_output_aliases={2: 0},
        compiler_params=pltpu.CompilerParams(vmem_limit_bytes=16 << 20),
        name="settle",
    )(from_left, from_right, total)


def finish_kernel(n, core_over, core_below, edge_over, edge_below, total, out_in, out, band, sems):
    tile = out.shape[1]
    copies = []
    for d, (core, edge, at, to) in enumerate(
        ((core_over, edge_over, n, 0), (core_below, edge_below, tile, tile - n))
    ):
        rows = pl.ds(at, n)
        for k in range(4):
            band[d, k, :, :n] = total[k, rows, pl.ds(n, n)] + edge[0, k].astype(FULL)
            band[d, k, :, n : tile - n] = total[k, rows, pl.ds(2 * n, tile - 2 * n)] + core[
                k
            ].astype(FULL)
            band[d, k, :, tile - n :] = total[k, rows, pl.ds(tile, n)] + edge[1, k].astype(FULL)
        copies.append(pltpu.make_async_copy(band.at[d], out.at[:, pl.ds(to, n)], sems.at[d]))
        copies[-1].start()
    for copy in copies:
        copy.wait()


def finish(total, out, cores, edges, n):
    planes, tile = out.shape[:2]
    return pl.pallas_call(
        functools.partial(finish_kernel, n),
        out_shape=jax.ShapeDtypeStruct(out.shape, FULL),
        in_specs=[VMEM] * 5 + [ANYWHERE],
        out_specs=ANYWHERE,
        scratch_shapes=[pltpu.VMEM((2, planes, n, tile), FULL), pltpu.SemaphoreType.DMA((2,))],
        input_output_aliases={5: 0},
        compiler_params=pltpu.CompilerParams(vmem_limit_bytes=16 << 20),
        name="finish",
    )(*cores, *edges, total, out)


def per_device(objects, illumination, propagator_phase, intensity, offsets, counts):
    extent = intensity.shape[1]
    n = extent // 2
    scalars = (offsets.T, counts)
    top, bottom = strips(objects, n)
    from_above = from_behind(bottom, "row", 1)
    from_below = from_behind(top, "row", -1)
    window, left, right = prepare(objects, n)
    from_left = from_behind(right, "col", 1)
    from_right = from_behind(left, "col", -1)
    constants = [jnp.asarray(half_tables(extent)), illumination, propagator_phase, intensity]
    total, constants[2] = run_slots(INSIDE, scalars, constants, window)
    window, total, token = run_slots(
        BESIDE, scalars, constants, window, total, (from_left, from_right)
    )
    to_left, to_right = turn(from_above, from_below, token)
    corner_left = from_behind(to_right, "col", 1)
    corner_right = from_behind(to_left, "col", -1)
    window, total, core_up, core_down = run_slots(
        OVER, scalars, constants, window, total, (from_above, from_below)
    )
    core_below = from_behind(core_up, "row", -1)
    core_over = from_behind(core_down, "row", 1)
    _, total, ends_left, ends_right, edge = run_slots(
        CORNER, scalars, constants, window, total, (corner_left, corner_right)
    )
    ends_from_right = from_behind(ends_left, "col", -1)
    ends_from_left = from_behind(ends_right, "col", 1)
    edge_up, edge_down = join(edge, ends_from_left, ends_from_right)
    edge_below = from_behind(edge_up, "row", -1)
    edge_over = from_behind(edge_down, "row", 1)
    side_left, side_right = sides(total, edge_up, n)
    side_from_right = from_behind(side_left, "col", -1)
    side_from_left = from_behind(side_right, "col", 1)
    total, out = settle(total, side_from_left, side_from_right, n)
    return finish(total, out, (core_over, core_below), (edge_over, edge_below), n)


def solution(mesh):
    placed = (
        P(None, "row", "col"),
        P(),
        P(),
        P(("row", "col"), None, None),
        P(("row", "col"), None),
        P(("row", "col")),
    )
    return jax.shard_map(
        per_device, mesh=mesh, in_specs=placed, out_specs=P(None, "row", "col"), check_vma=False
    )
```

profile of v0, /device:TPU:9, one launch (start us, length us, event | category | flops | bytes accessed | tf_op | source)
XLA Modules:
  0.0 106.2 jit_solution(2738789355773614251)
XLA Ops:
  0.0 2.2 %copy-done.2 = f32[4,512,512]{2,1,0:T(8,128)S(1)} copy-done((f32[4,512,512]{2,1,0:T(8,128)S(1)}, f32[4,512,512]{2,1,0:T(8,128)}, u32[]{:S(2)}) %copy-start.2) | copy-done | bytes 4194328
  2.2 1.3 %prepare.1 = (bf16[4,768,768]{2,1,0:T(8,128)(2,1)S(1)}, bf16[4,512,128]{2,1,0:T(8,128)(2,1)}, bf16[4,512,128]{2,1,0:T(8,128)(2,1)}) custom-call(f32[4,512,512]{2,1,0:T(8,128)S(1)} %copy-done.2), custom_call_target="tpu_custom_call" | custom-call | tf_op jit(solution)/shard_map/prepare/pallas_call | solution.py:215
  3.5 2.2 %copy-done = bf16[4,768,768]{2,1,0:T(8,128)(2,1)} copy-done((bf16[4,768,768]{2,1,0:T(8,128)(2,1)}, bf16[4,768,768]{2,1,0:T(8,128)(2,1)S(1)}, u32[]{:S(2)}) %copy-start) | copy-done | bytes 4718616
  5.7 4.0 %collective-permute-start.2 = (bf16[4,512,128]{2,1,0:T(8,128)(2,1)}, bf16[4,512,128]{2,1,0:T(8,128)(2,1)S(1)}, u32[]{:S(2)}, u32[]{:S(2)}) collective-permute-start(bf16[4,512,128]{2,1,0:T(8,128)(2,1)} %get-tuple-element.35), channel_id=1, source_target_pairs={{0,1},{1,2},{2,3},{3,4},{4,5},{5,6},{6,7},{8,9},{9,10},{10,11},{11... | collective-permute-start | bytes 1572872 | tf_op jit(solution)/shard_map/ppermute | solution.py:20
  9.7 1.9 %collective-permute-start.3 = (bf16[4,512,128]{2,1,0:T(8,128)(2,1)}, bf16[4,512,128]{2,1,0:T(8,128)(2,1)S(1)}, u32[]{:S(2)}, u32[]{:S(2)}) collective-permute-start(bf16[4,512,128]{2,1,0:T(8,128)(2,1)} %get-tuple-element.36), channel_id=1, source_target_pairs={{1,0},{2,1},{3,2},{4,3},{5,4},{6,5},{7,6},{9,8},{10,9},{11,10},{12... | collective-permute-start | bytes 1572872 | tf_op jit(solution)/shard_map/ppermute | solution.py:20
  11.6 3.6 %strips.1 = (bf16[4,128,512]{2,1,0:T(8,128)(2,1)}, bf16[4,128,512]{2,1,0:T(8,128)(2,1)}) custom-call(f32[4,512,512]{2,1,0:T(8,128)} %last.1, f32[4,512,512]{2,1,0:T(8,128)} %last.1), custom_call_target="tpu_custom_call" | custom-call | tf_op jit(solution)/shard_map/strips/pallas_call | solution.py:189
  15.2 3.1 %collective-permute-start = (bf16[4,128,512]{2,1,0:T(8,128)(2,1)}, bf16[4,128,512]{2,1,0:T(8,128)(2,1)S(1)}, u32[]{:S(2)}, u32[]{:S(2)}) collective-permute-start(bf16[4,128,512]{2,1,0:T(8,128)(2,1)} %get-tuple-element.33), channel_id=1, source_target_pairs={{0,8},{8,16},{16,24},{1,9},{9,17},{17,25},{2,10},{10,18},{18,26},{... | collective-permute-start | bytes 1572872 | tf_op jit(solution)/shard_map/ppermute | solution.py:20
  18.4 1.3 %collective-permute-start.1 = (bf16[4,128,512]{2,1,0:T(8,128)(2,1)}, bf16[4,128,512]{2,1,0:T(8,128)(2,1)S(1)}, u32[]{:S(2)}, u32[]{:S(2)}) collective-permute-start(bf16[4,128,512]{2,1,0:T(8,128)(2,1)} %get-tuple-element.34), channel_id=1, source_target_pairs={{8,0},{16,8},{24,16},{9,1},{17,9},{25,17},{10,2},{18,10},{26,18},{... | collective-permute-start | bytes 1572872 | tf_op jit(solution)/shard_map/ppermute | solution.py:20
  20.3 0.0 copy-done.3
  20.3 0.0 copy-done.4
  20.3 0.0 copy-done.5
  20.3 0.0 copy-done.6
  20.3 0.0 copy-start.1
  20.3 2.3 %copy-done.1 = bf16[4,768,768]{2,1,0:T(8,128)(2,1)S(1)} copy-done((bf16[4,768,768]{2,1,0:T(8,128)(2,1)S(1)}, bf16[4,768,768]{2,1,0:T(8,128)(2,1)}, u32[]{:S(2)}) %copy-start.1) | copy-done | bytes 4718616
  22.7 0.9 copy-done.7
  23.6 3.1 %shard_map.73 = (f32[4,768,768]{2,1,0:T(8,128)S(1)}, f32[2,256,256]{2,1,0:T(8,128)S(1)}) custom-call(s32[2,12]{1,0:T(2,128)S(1)} %bitcast.1, s32[1]{0:T(128)S(6)} %copy.24.counts, bf16[6,256,256]{2,1,0:T(8,128)(2,1)S(1)} %copy-done.4, f32[2,256,256]{2,1,0:T(8,128)S(1)} %copy-done.5, f32[256,256]{1,0:T(8,128)S(1)} %copy-done.7, ...), custom_call_target="tpu_custom_call" | custom-call | flops 2617245696 | tf_op jit(solution)/shard_map/pallas_call | solution.py:350
  26.7 0.0 collective-permute-done.2.refs_0_
  26.7 0.0 collective-permute-done.3.refs_1_
  26.7 4.0 %shard_map.74 = (bf16[4,768,768]{2,1,0:T(8,128)(2,1)S(1)}, f32[4,768,768]{2,1,0:T(8,128)S(1)}, f32[8,128]{1,0:T(8,128)S(1)}) custom-call(s32[2,12]{1,0:T(2,128)S(1)} %bitcast.2, s32[1]{0:T(128)S(6)} %copy.24.counts, bf16[6,256,256]{2,1,0:T(8,128)(2,1)S(1)} %copy-done.4, f32[2,256,256]{2,1,0:T(8,128)S(1)} %copy-done.5, ...), custom_call_target="tpu_custom_call", output_to_operand_aliasing={{0}: (8, {}), {1}: (9, {})} | custom-call | flops 2617245696 | tf_op jit(solution)/shard_map/pallas_call | solution.py:350
  30.8 0.0 collective-permute-done.refs_0_.over
  30.8 11.7 %collective-permute-done.1.refs_1_.below = bf16[4,128,512]{2,1,0:T(8,128)(2,1)S(1)} collective-permute-done((bf16[4,128,512]{2,1,0:T(8,128)(2,1)}, bf16[4,128,512]{2,1,0:T(8,128)(2,1)S(1)}, u32[]{:S(2)}, u32[]{:S(2)}) %collective-permute-start.1) | collective-permute-done | bytes 524320 | tf_op jit(solution)/shard_map/ppermute | solution.py:20
  42.4 0.1 turn.1
  42.5 4.5 %collective-permute-start.6 = (bf16[4,256,128]{2,1,0:T(8,128)(2,1)S(1)}, bf16[4,256,128]{2,1,0:T(8,128)(2,1)S(1)}, u32[]{:S(2)}, u32[]{:S(2)}) collective-permute-start(bf16[4,256,128]{2,1,0:T(8,128)(2,1)S(1)} %get-tuple-element.43), channel_id=1, source_target_pairs={{0,1},{1,2},{2,3},{3,4},{4,5},{5,6},{6,7},{8,9},{9,10},{10,11},{11... | collective-permute-start | bytes 786440 | tf_op jit(solution)/shard_map/ppermute | solution.py:20
  47.0 1.9 %collective-permute-start.7 = (bf16[4,256,128]{2,1,0:T(8,128)(2,1)S(1)}, bf16[4,256,128]{2,1,0:T(8,128)(2,1)S(1)}, u32[]{:S(2)}, u32[]{:S(2)}) collective-permute-start(bf16[4,256,128]{2,1,0:T(8,128)(2,1)S(1)} %get-tuple-element.44), channel_id=1, source_target_pairs={{1,0},{2,1},{3,2},{4,3},{5,4},{6,5},{7,6},{9,8},{10,9},{11,10},{12... | collective-permute-start | bytes 786440 | tf_op jit(solution)/shard_map/ppermute | solution.py:20
  49.0 0.9 shard_map.75
  49.9 0.4 collective-permute-done.6.refs_0_
  50.3 4.4 %collective-permute-done.7.refs_1_ = bf16[4,256,128]{2,1,0:T(8,128)(2,1)S(1)} collective-permute-done((bf16[4,256,128]{2,1,0:T(8,128)(2,1)S(1)}, bf16[4,256,128]{2,1,0:T(8,128)(2,1)S(1)}, u32[]{:S(2)}, u32[]{:S(2)}) %collective-permute-start.7) | collective-permute-done | bytes 262176 | tf_op jit(solution)/shard_map/ppermute | solution.py:20
  54.7 1.2 %shard_map.76 = (bf16[4,768,768]{2,1,0:T(8,128)(2,1)S(1)}, f32[4,768,768]{2,1,0:T(8,128)S(1)}, bf16[2,4,128,128]{3,2,1,0:T(8,128)(2,1)S(1)}, bf16[2,4,128,128]{3...) custom-call(s32[2,12]{1,0:T(2,128)S(1)} %bitcast.4, ...), custom_call_target="tpu_custom_call", output_to_operand_aliasing={{0}: (8, {}), {1}: (9, {})} | custom-call | flops 2617245696 | tf_op jit(solution)/shard_map/pallas_call | solution.py:350
  55.9 4.6 %collective-permute-start.8 = (bf16[2,4,128,128]{3,2,1,0:T(8,128)(2,1)S(1)}, bf16[2,4,128,128]{3,2,1,0:T(8,128)(2,1)S(1)}, u32[]{:S(2)}, u32[]{:S(2)}) collective-permute-start(bf16[2,4,128,128]{3,2,1,0:T(8,128)(2,1)S(1)} %get-tuple-element.48), channel_id=1, source_target_pairs={{0,1},{1,2},{2,3},{3,4},{4,5},{5,6},{6,7},{8,9},{9,10},{10,11},{11... | collective-permute-start | bytes 786440 | tf_op jit(solution)/shard_map/ppermute | solution.py:20
  60.6 1.9 %collective-permute-start.9 = (bf16[2,4,128,128]{3,2,1,0:T(8,128)(2,1)S(1)}, bf16[2,4,128,128]{3,2,1,0:T(8,128)(2,1)S(1)}, u32[]{:S(2)}, u32[]{:S(2)}) collective-permute-start(bf16[2,4,128,128]{3,2,1,0:T(8,128)(2,1)S(1)} %get-tuple-element.49), channel_id=1, source_target_pairs={{1,0},{2,1},{3,2},{4,3},{5,4},{6,5},{7,6},{9,8},{10,9},{11,10},{12... | collective-permute-start | bytes 786440 | tf_op jit(solution)/shard_map/ppermute | solution.py:20
  62.5 1.4 %collective-permute-done.8.from_left = bf16[2,4,128,128]{3,2,1,0:T(8,128)(2,1)S(1)} collective-permute-done((bf16[2,4,128,128]{3,2,1,0:T(8,128)(2,1)S(1)}, bf16[2,4,128,128]{3,2,1,0:T(8,128)(2,1)S(1)}, u32[]{:S(2)}, u32[]{:S(2)}) %collective-permute-start.8) | collective-permute-done | bytes 262176 | tf_op jit(solution)/shard_map/ppermute | solution.py:20
  63.9 4.4 %collective-permute-done.9.from_right = bf16[2,4,128,128]{3,2,1,0:T(8,128)(2,1)S(1)} collective-permute-done((bf16[2,4,128,128]{3,2,1,0:T(8,128)(2,1)S(1)}, bf16[2,4,128,128]{3,2,1,0:T(8,128)(2,1)S(1)}, u32[]{:S(2)}, u32[]{:S(2)}) %collective-permute-start.9) | collective-permute-done | bytes 262176 | tf_op jit(solution)/shard_map/ppermute | solution.py:20
  68.3 0.1 join.1
  68.4 0.1 sides.1
  68.5 1.9 %collective-permute-start.12 = (bf16[4,512,128]{2,1,0:T(8,128)(2,1)S(1)}, bf16[4,512,128]{2,1,0:T(8,128)(2,1)S(1)}, u32[]{:S(2)}, u32[]{:S(2)}) collective-permute-start(bf16[4,512,128]{2,1,0:T(8,128)(2,1)S(1)} %get-tuple-element.53), channel_id=1, source_target_pairs={{0,1},{1,2},{2,3},{3,4},{4,5},{5,6},{6,7},{8,9},{9,10},{10,11},{11... | collective-permute-start | bytes 1572872 | tf_op jit(solution)/shard_map/ppermute | solution.py:20
  70.4 2.4 %collective-permute-start.13 = (bf16[4,512,128]{2,1,0:T(8,128)(2,1)S(1)}, bf16[4,512,128]{2,1,0:T(8,128)(2,1)S(1)}, u32[]{:S(2)}, u32[]{:S(2)}) collective-permute-start(bf16[4,512,128]{2,1,0:T(8,128)(2,1)S(1)} %get-tuple-element.54), channel_id=1, source_target_pairs={{1,0},{2,1},{3,2},{4,3},{5,4},{6,5},{7,6},{9,8},{10,9},{11,10},{12... | collective-permute-start | bytes 1572872 | tf_op jit(solution)/shard_map/ppermute | solution.py:20
  72.8 8.2 %collective-permute-start.4 = (bf16[4,128,256]{2,1,0:T(8,128)(2,1)S(1)}, bf16[4,128,256]{2,1,0:T(8,128)(2,1)S(1)}, u32[]{:S(2)}, u32[]{:S(2)}) collective-permute-start(bf16[4,128,256]{2,1,0:T(8,128)(2,1)S(1)} %get-tuple-element.40), channel_id=1, source_target_pairs={{0,8},{8,16},{16,24},{1,9},{9,17},{17,25},{2,10},{10,18},{18,26},{... | collective-permute-start | bytes 786440 | tf_op jit(solution)/shard_map/ppermute | solution.py:20
  81.1 1.3 %collective-permute-start.5 = (bf16[4,128,256]{2,1,0:T(8,128)(2,1)S(1)}, bf16[4,128,256]{2,1,0:T(8,128)(2,1)S(1)}, u32[]{:S(2)}, u32[]{:S(2)}) collective-permute-start(bf16[4,128,256]{2,1,0:T(8,128)(2,1)S(1)} %get-tuple-element.41), channel_id=1, source_target_pairs={{8,0},{16,8},{24,16},{9,1},{17,9},{25,17},{10,2},{18,10},{26,18},{... | collective-permute-start | bytes 786440 | tf_op jit(solution)/shard_map/ppermute | solution.py:20
  82.4 4.0 %collective-permute-start.10 = (bf16[2,4,128,128]{3,2,1,0:T(8,128)(2,1)S(1)}, bf16[2,4,128,128]{3,2,1,0:T(8,128)(2,1)S(1)}, u32[]{:S(2)}, u32[]{:S(2)}) collective-permute-start(bf16[2,4,128,128]{3,2,1,0:T(8,128)(2,1)S(1)} %get-tuple-element.50), channel_id=1, source_target_pairs={{0,8},{8,16},{16,24},{1,9},{9,17},{17,25},{2,10},{10,18},{18,26},{... | collective-permute-start | bytes 786440 | tf_op jit(solution)/shard_map/ppermute | solution.py:20
  86.4 0.0 collective-permute-done.12.from_left
  86.4 1.3 %collective-permute-start.11 = (bf16[2,4,128,128]{3,2,1,0:T(8,128)(2,1)S(1)}, bf16[2,4,128,128]{3,2,1,0:T(8,128)(2,1)S(1)}, u32[]{:S(2)}, u32[]{:S(2)}) collective-permute-start(bf16[2,4,128,128]{3,2,1,0:T(8,128)(2,1)S(1)} %get-tuple-element.51.token), channel_id=1, source_target_pairs={{8,0},{16,8},{24,16},{9,1},{17,9},{25,17},{10,2},{18,10},{26,18},{... | collective-permute-start | bytes 786440 | tf_op jit(solution)/shard_map/ppermute | solution.py:20
  87.7 0.0 collective-permute-done.13.from_right
  87.7 1.6 %settle.1 = (f32[4,768,768]{2,1,0:T(8,128)S(1)}, f32[4,512,512]{2,1,0:T(8,128)}) custom-call(bf16[4,512,128]{2,1,0:T(8,128)(2,1)S(1)} %collective-permute-done.12.from_left, bf16[4,512,128]{2,1,0:T(8,128)(2,1)S(1)} %collective-permute-done.13.from_right, f32[4,768,768]{2,1,0:T(8,128)S(1)} %get-tuple-element.52.total.total_in), custom_call_target="tpu_custom_call", output_to_operand_aliasing={{0}: (2, {})} | custom-call | tf_op jit(solution)/shard_map/settle/pallas_call | solution.py:433
  89.3 0.0 collective-permute-done.4.core_over
  89.3 4.0 %collective-permute-done.5.core_below = bf16[4,128,256]{2,1,0:T(8,128)(2,1)S(1)} collective-permute-done((bf16[4,128,256]{2,1,0:T(8,128)(2,1)S(1)}, bf16[4,128,256]{2,1,0:T(8,128)(2,1)S(1)}, u32[]{:S(2)}, u32[]{:S(2)}) %collective-permute-start.5) | collective-permute-done | bytes 262176 | tf_op jit(solution)/shard_map/ppermute | solution.py:20
  93.3 0.0 collective-permute-done.10.edge_over
  93.3 11.2 %collective-permute-done.11.edge_below = bf16[2,4,128,128]{3,2,1,0:T(8,128)(2,1)S(1)} collective-permute-done((bf16[2,4,128,128]{3,2,1,0:T(8,128)(2,1)S(1)}, bf16[2,4,128,128]{3,2,1,0:T(8,128)(2,1)S(1)}, u32[]{:S(2)}, u32[]{:S(2)}) %collective-permute-start.11) | collective-permute-done | bytes 262176 | tf_op jit(solution)/shard_map/ppermute | solution.py:20
  104.6 1.5 %finish.1 = f32[4,512,512]{2,1,0:T(8,128)} custom-call(bf16[4,128,256]{2,1,0:T(8,128)(2,1)S(1)} %collective-permute-done.4.core_over, bf16[4,128,256]{2,1,0:T(8,128)(2,1)S(1)} %collective-permute-done.5.core_below, bf16[2,4,128,128]{3,2,1,0:T(8,128)(2,1)S(1)} %collective-permute-done.10.edge_over, ...), custom_call_target="tpu_custom_call", output_to_operand_aliasing={{}: (5, {})} | custom-call | tf_op jit(solution)/shard_map/finish/pallas_call | solution.py:469
  (7 shorter events, 0.0 us)
Async XLA Ops:
  0.0 2.2 %copy-start.2 = (f32[4,512,512]{2,1,0:T(8,128)S(1)}, f32[4,512,512]{2,1,0:T(8,128)}, u32[]{:S(2)}) copy-start(f32[4,512,512]{2,1,0:T(8,128)} %last.1) | copy-start | bytes 12582916
  3.5 2.2 %copy-start = (bf16[4,768,768]{2,1,0:T(8,128)(2,1)}, bf16[4,768,768]{2,1,0:T(8,128)(2,1)S(1)}, u32[]{:S(2)}) copy-start(bf16[4,768,768]{2,1,0:T(8,128)(2,1)S(1)} %get-tuple-element.31.refs_0_.refs_2_) | copy-start | bytes 14155780
  5.7 14.6 %copy-start.3 = (bf16[12,256,256]{2,1,0:T(8,128)(2,1)S(1)}, bf16[12,256,256]{2,1,0:T(8,128)(2,1)}, u32[]{:S(2)}) copy-start(bf16[12,256,256]{2,1,0:T(8,128)(2,1)} %measured.7) | copy-start | bytes 4718596
  5.7 14.6 %copy-start.4 = (bf16[6,256,256]{2,1,0:T(8,128)(2,1)S(1)}, bf16[6,256,256]{2,1,0:T(8,128)(2,1)}, u32[]{:S(2)}) copy-start(bf16[6,256,256]{2,1,0:T(8,128)(2,1)} %constant.2.clone.tab) | copy-start | bytes 2359300
  5.7 14.6 %copy-start.5 = (f32[2,256,256]{2,1,0:T(8,128)S(1)}, f32[2,256,256]{2,1,0:T(8,128)}, u32[]{:S(2)}) copy-start(f32[2,256,256]{2,1,0:T(8,128)} %light.7) | copy-start | bytes 1572868
  5.7 14.7 %copy-start.6 = (s32[12,2]{0,1:T(2,128)S(1)}, s32[12,2]{0,1:T(2,128)}, u32[]{:S(2)}) copy-start(s32[12,2]{0,1:T(2,128)} %param.11) | copy-start | bytes 292
  5.7 21.0 %collective-permute-start.2 = (bf16[4,512,128]{2,1,0:T(8,128)(2,1)}, bf16[4,512,128]{2,1,0:T(8,128)(2,1)S(1)}, u32[]{:S(2)}, u32[]{:S(2)}) collective-permute-start(bf16[4,512,128]{2,1,0:T(8,128)(2,1)} %get-tuple-element.35), channel_id=1, source_target_pairs={{0,1},{1,2},{2,3},{3,4},{4,5},{5,6},{6,7},{8,9},{9,10},{10,11},{11... | collective-permute-start | bytes 1572872 | tf_op jit(solution)/shard_map/ppermute | solution.py:20
  9.7 17.0 %collective-permute-start.3 = (bf16[4,512,128]{2,1,0:T(8,128)(2,1)}, bf16[4,512,128]{2,1,0:T(8,128)(2,1)S(1)}, u32[]{:S(2)}, u32[]{:S(2)}) collective-permute-start(bf16[4,512,128]{2,1,0:T(8,128)(2,1)} %get-tuple-element.36), channel_id=1, source_target_pairs={{1,0},{2,1},{3,2},{4,3},{5,4},{6,5},{7,6},{9,8},{10,9},{11,10},{12... | collective-permute-start | bytes 1572872 | tf_op jit(solution)/shard_map/ppermute | solution.py:20
  15.2 15.6 %collective-permute-start = (bf16[4,128,512]{2,1,0:T(8,128)(2,1)}, bf16[4,128,512]{2,1,0:T(8,128)(2,1)S(1)}, u32[]{:S(2)}, u32[]{:S(2)}) collective-permute-start(bf16[4,128,512]{2,1,0:T(8,128)(2,1)} %get-tuple-element.33), channel_id=1, source_target_pairs={{0,8},{8,16},{16,24},{1,9},{9,17},{17,25},{2,10},{10,18},{18,26},{... | collective-permute-start | bytes 1572872 | tf_op jit(solution)/shard_map/ppermute | solution.py:20
  18.4 24.1 %collective-permute-start.1 = (bf16[4,128,512]{2,1,0:T(8,128)(2,1)}, bf16[4,128,512]{2,1,0:T(8,128)(2,1)S(1)}, u32[]{:S(2)}, u32[]{:S(2)}) collective-permute-start(bf16[4,128,512]{2,1,0:T(8,128)(2,1)} %get-tuple-element.34), channel_id=1, source_target_pairs={{8,0},{16,8},{24,16},{9,1},{17,9},{25,17},{10,2},{18,10},{26,18},{... | collective-permute-start | bytes 1572872 | tf_op jit(solution)/shard_map/ppermute | solution.py:20
  20.3 2.3 %copy-start.1 = (bf16[4,768,768]{2,1,0:T(8,128)(2,1)S(1)}, bf16[4,768,768]{2,1,0:T(8,128)(2,1)}, u32[]{:S(2)}) copy-start(bf16[4,768,768]{2,1,0:T(8,128)(2,1)} %copy-done) | copy-start | bytes 14155780
  22.7 0.9 copy-start.7
  42.5 7.8 %collective-permute-start.6 = (bf16[4,256,128]{2,1,0:T(8,128)(2,1)S(1)}, bf16[4,256,128]{2,1,0:T(8,128)(2,1)S(1)}, u32[]{:S(2)}, u32[]{:S(2)}) collective-permute-start(bf16[4,256,128]{2,1,0:T(8,128)(2,1)S(1)} %get-tuple-element.43), channel_id=1, source_target_pairs={{0,1},{1,2},{2,3},{3,4},{4,5},{5,6},{6,7},{8,9},{9,10},{10,11},{11... | collective-permute-start | bytes 786440 | tf_op jit(solution)/shard_map/ppermute | solution.py:20
  47.0 7.7 %collective-permute-start.7 = (bf16[4,256,128]{2,1,0:T(8,128)(2,1)S(1)}, bf16[4,256,128]{2,1,0:T(8,128)(2,1)S(1)}, u32[]{:S(2)}, u32[]{:S(2)}) collective-permute-start(bf16[4,256,128]{2,1,0:T(8,128)(2,1)S(1)} %get-tuple-element.44), channel_id=1, source_target_pairs={{1,0},{2,1},{3,2},{4,3},{5,4},{6,5},{7,6},{9,8},{10,9},{11,10},{12... | collective-permute-start | bytes 786440 | tf_op jit(solution)/shard_map/ppermute | solution.py:20
  55.9 7.9 %collective-permute-start.8 = (bf16[2,4,128,128]{3,2,1,0:T(8,128)(2,1)S(1)}, bf16[2,4,128,128]{3,2,1,0:T(8,128)(2,1)S(1)}, u32[]{:S(2)}, u32[]{:S(2)}) collective-permute-start(bf16[2,4,128,128]{3,2,1,0:T(8,128)(2,1)S(1)} %get-tuple-element.48), channel_id=1, source_target_pairs={{0,1},{1,2},{2,3},{3,4},{4,5},{5,6},{6,7},{8,9},{9,10},{10,11},{11... | collective-permute-start | bytes 786440 | tf_op jit(solution)/shard_map/ppermute | solution.py:20
  60.6 7.7 %collective-permute-start.9 = (bf16[2,4,128,128]{3,2,1,0:T(8,128)(2,1)S(1)}, bf16[2,4,128,128]{3,2,1,0:T(8,128)(2,1)S(1)}, u32[]{:S(2)}, u32[]{:S(2)}) collective-permute-start(bf16[2,4,128,128]{3,2,1,0:T(8,128)(2,1)S(1)} %get-tuple-element.49), channel_id=1, source_target_pairs={{1,0},{2,1},{3,2},{4,3},{5,4},{6,5},{7,6},{9,8},{10,9},{11,10},{12... | collective-permute-start | bytes 786440 | tf_op jit(solution)/shard_map/ppermute | solution.py:20
  68.5 17.9 %collective-permute-start.12 = (bf16[4,512,128]{2,1,0:T(8,128)(2,1)S(1)}, bf16[4,512,128]{2,1,0:T(8,128)(2,1)S(1)}, u32[]{:S(2)}, u32[]{:S(2)}) collective-permute-start(bf16[4,512,128]{2,1,0:T(8,128)(2,1)S(1)} %get-tuple-element.53), channel_id=1, source_target_pairs={{0,1},{1,2},{2,3},{3,4},{4,5},{5,6},{6,7},{8,9},{9,10},{10,11},{11... | collective-permute-start | bytes 1572872 | tf_op jit(solution)/shard_map/ppermute | solution.py:20
  70.4 17.3 %collective-permute-start.13 = (bf16[4,512,128]{2,1,0:T(8,128)(2,1)S(1)}, bf16[4,512,128]{2,1,0:T(8,128)(2,1)S(1)}, u32[]{:S(2)}, u32[]{:S(2)}) collective-permute-start(bf16[4,512,128]{2,1,0:T(8,128)(2,1)S(1)} %get-tuple-element.54), channel_id=1, source_target_pairs={{1,0},{2,1},{3,2},{4,3},{5,4},{6,5},{7,6},{9,8},{10,9},{11,10},{12... | collective-permute-start | bytes 1572872 | tf_op jit(solution)/shard_map/ppermute | solution.py:20
  72.8 16.4 %collective-permute-start.4 = (bf16[4,128,256]{2,1,0:T(8,128)(2,1)S(1)}, bf16[4,128,256]{2,1,0:T(8,128)(2,1)S(1)}, u32[]{:S(2)}, u32[]{:S(2)}) collective-permute-start(bf16[4,128,256]{2,1,0:T(8,128)(2,1)S(1)} %get-tuple-element.40), channel_id=1, source_target_pairs={{0,8},{8,16},{16,24},{1,9},{9,17},{17,25},{2,10},{10,18},{18,26},{... | collective-permute-start | bytes 786440 | tf_op jit(solution)/shard_map/ppermute | solution.py:20
  81.1 12.3 %collective-permute-start.5 = (bf16[4,128,256]{2,1,0:T(8,128)(2,1)S(1)}, bf16[4,128,256]{2,1,0:T(8,128)(2,1)S(1)}, u32[]{:S(2)}, u32[]{:S(2)}) collective-permute-start(bf16[4,128,256]{2,1,0:T(8,128)(2,1)S(1)} %get-tuple-element.41), channel_id=1, source_target_pairs={{8,0},{16,8},{24,16},{9,1},{17,9},{25,17},{10,2},{18,10},{26,18},{... | collective-permute-start | bytes 786440 | tf_op jit(solution)/shard_map/ppermute | solution.py:20
  82.4 11.0 %collective-permute-start.10 = (bf16[2,4,128,128]{3,2,1,0:T(8,128)(2,1)S(1)}, bf16[2,4,128,128]{3,2,1,0:T(8,128)(2,1)S(1)}, u32[]{:S(2)}, u32[]{:S(2)}) collective-permute-start(bf16[2,4,128,128]{3,2,1,0:T(8,128)(2,1)S(1)} %get-tuple-element.50), channel_id=1, source_target_pairs={{0,8},{8,16},{16,24},{1,9},{9,17},{17,25},{2,10},{10,18},{18,26},{... | collective-permute-start | bytes 786440 | tf_op jit(solution)/shard_map/ppermute | solution.py:20
  86.4 18.2 %collective-permute-start.11 = (bf16[2,4,128,128]{3,2,1,0:T(8,128)(2,1)S(1)}, bf16[2,4,128,128]{3,2,1,0:T(8,128)(2,1)S(1)}, u32[]{:S(2)}, u32[]{:S(2)}) collective-permute-start(bf16[2,4,128,128]{3,2,1,0:T(8,128)(2,1)S(1)} %get-tuple-element.51.token), channel_id=1, source_target_pairs={{8,0},{16,8},{24,16},{9,1},{17,9},{25,17},{10,2},{18,10},{26,18},{... | collective-permute-start | bytes 786440 | tf_op jit(solution)/shard_map/ppermute | solution.py:20
where the time goes:
time: 107 us; the launch traced here: 106 us
  starting transfers between devices  42.5 us (40%)
  waiting for transfers between devices  37.5 us (35%)
  Pallas kernels  17.5 us (16%)
  local copies, waits for them, and re-layouts  7.64 us (7%)
  between operations  1.09 us (1%)
    ppermute x14, starting transfers between devices, from_behind(): return lax.ppermute(x, axis, pairs)  42.5 us
    ppermute x14, waiting for transfers between devices, from_behind(): return lax.ppermute(x, axis, pairs)  37.5 us
    pallas_call x4, Pallas kernels, run_slots(): pl.pallas_call(functools.partial(slots_kernel, mode), out_shape=[jax.Shap...  9.25 us
    unnamed x16, local copies, waits for them, and re-layouts  7.64 us
    pallas_call x1, Pallas kernels, strips(): pl.pallas_call(strips_kernel, grid=(planes,), in_specs=[pl.BlockSpec(bloc...  3.57 us
  transfers between devices with their start and end apart: 14, of which 7 were waited for; matrix products, arithmetic and copies ran while one was open for 0% of the time, Pallas kernels for 12%

commit v1 on v0

--- a/solution.py
+++ b/solution.py
@@ -14,10 +14,19 @@
 FULL = jnp.float32
 
 
-def from_behind(x, axis, by):
+def exchange(x, axis, turn):
     size = lax.axis_size(axis)
-    pairs = [(i, i + by) for i in range(size) if 0 <= i + by < size]
-    return lax.ppermute(x, axis, pairs)
+    pairs = [(i, i + 1) for i in range(turn, size - 1, 2)]
+    return lax.ppermute(x, axis, pairs + [(j, i) for i, j in pairs])
+
+
+def ahead(axis, turn):
+    odd = lax.axis_index(axis) % 2
+    return odd if turn == 0 else 1 - odd
+
+
+def pick(side, low, high, size):
+    return pl.ds(pl.multiple_of(high - side * (high - low), size), size)
 
 
 def half_tables(extent):
@@ -177,51 +186,32 @@
         copy.wait()
 
 
-def strips_kernel(first, last, top, bottom):
-    top[...] = first[...].astype(HALF)
-    bottom[...] = last[...].astype(HALF)
-
-
-def strips(objects, n):
-    planes, rows, cols = objects.shape
-    block = (1, n, cols)
-    out = jax.ShapeDtypeStruct((planes, n, cols), HALF)
-    return pl.pallas_call(
-        strips_kernel,
-        grid=(planes,),
-        in_specs=[
-            pl.BlockSpec(block, lambda k: (k, 0, 0)),
-            pl.BlockSpec(block, lambda k: (k, rows // n - 1, 0)),
-        ],
-        out_specs=[pl.BlockSpec(block, lambda k: (k, 0, 0))] * 2,
-        out_shape=[out, out],
-        compiler_params=pltpu.CompilerParams(vmem_limit_bytes=60 << 20),
-        name="strips",
-    )(objects, objects)
-
-
-def prepare_kernel(n, objects, window, left, right):
+def prepare_kernel(n, objects, window, *strips):
     planes, tile = objects.shape[:2]
     for k in range(planes):
-        plane = objects[k].astype(HALF)
-        window[k, n : n + tile, n : n + tile] = plane
-        left[k] = plane[:, :n]
-        right[k] = plane[:, tile - n :]
+        window[k, n : n + tile, n : n + tile] = objects[k].astype(HALF)
+    for turn in range(2):
+        rows = pick(ahead("row", turn), 0, tile - n, n)
+        cols = pick(ahead("col", turn), 0, tile - n, n)
+        for k in range(planes):
+            strips[turn][k] = objects[k, rows, :].astype(HALF)
+            strips[2 + turn][k] = objects[k, :, cols].astype(HALF)
 
 
 def prepare(objects, n):
     planes, tile = objects.shape[:2]
-    side = jax.ShapeDtypeStruct((planes, tile, n), HALF)
+    flat = jax.ShapeDtypeStruct((planes, n, tile), HALF)
+    tall = jax.ShapeDtypeStruct((planes, tile, n), HALF)
+    whole = jax.ShapeDtypeStruct((planes, tile + 2 * n, tile + 2 * n), HALF)
     return pl.pallas_call(
         functools.partial(prepare_kernel, n),
         in_specs=[VMEM],
-        out_specs=[VMEM] * 3,
-        out_shape=[
-            jax.ShapeDtypeStruct((planes, tile + 2 * n, tile + 2 * n), HALF),
-            side,
-            side,
-        ],
+        out_specs=[VMEM] * 5,
+        out_shape=[whole, flat, flat, tall, tall],
         compiler_params=pltpu.CompilerParams(vmem_limit_bytes=16 << 20),
+        cost_estimate=pl.CostEstimate(
+            flops=2000 * objects.size, bytes_accessed=6 * objects.size, transcendentals=0
+        ),
         name="prepare",
     )(objects)
 
@@ -235,7 +225,10 @@
     else:
         sources, (window, total), outs = refs[:2], refs[4:6], refs[6:-2]
     tile = window.shape[1] - 2 * n
-    inner, first, last = pl.ds(n, tile), pl.ds(0, n), pl.ds(n + tile, n)
+    inner = pl.ds(n, tile)
+    row_halo = [pick(ahead("row", turn), 0, n + tile, n) for turn in range(2)]
+    col_halo = [pick(ahead("col", turn), 0, n + tile, n) for turn in range(2)]
+    col_edge = [pick(ahead("col", turn), n, tile, n) for turn in range(2)]
 
     if mode == INSIDE:
 
@@ -250,35 +243,47 @@
         spread_out[1] = selected(jnp.sin(phase), tab)
         spread = spread_out
     else:
-        one, two = sources
         if mode == BESIDE:
-            moves = [(one, (inner, first)), (two, (inner, last))]
+            moves = [(sources[turn], (inner, col_halo[turn])) for turn in range(2)]
         elif mode == OVER:
-            moves = [(one, (first, inner)), (two, (last, inner))]
+            moves = [(sources[turn], (row_halo[turn], inner)) for turn in range(2)]
         else:
             moves = [
-                (side.at[:, pl.ds(at, n)], (rows, cols))
-                for side, cols in ((one, first), (two, last))
-                for at, rows in ((0, first), (n, last))
+                (sources[turn].at[d], (row_halo[d], col_halo[turn]))
+                for turn in range(2)
+                for d in range(2)
             ]
         run_copies([(source, window.at[(slice(None), *at)]) for source, at in moves], sems)
 
-    def within(at):
+    def inside(at):
         return (at >= 0) & ((at + 2) * n <= tile)
 
-    def choose(j, found):
-        row_in, col_in = within(offsets[0, j]), within(offsets[1, j])
-        wanted = j < counts[0]
-        wanted &= row_in if mode in (INSIDE, BESIDE) else jnp.logical_not(row_in)
-        wanted &= col_in if mode in (INSIDE, OVER) else jnp.logical_not(col_in)
-
-        @pl.when(wanted)
+    def listed(kind, found):
+        def choose(j, found):
+            row_in, col_in = inside(offsets[0, j]), inside(offsets[1, j])
+            wanted = j < counts[0]
+            wanted &= row_in if kind in (INSIDE, BESIDE) else jnp.logical_not(row_in)
+            wanted &= col_in if kind in (INSIDE, OVER) else jnp.logical_not(col_in)
+
+            @pl.when(wanted)
+            def _():
+                order[found] = j
+
+            return found + wanted.astype(jnp.int32)
+
+        return lax.fori_loop(0, slot_count, choose, found)
+
+    found = jnp.int32(0)
+    for kind in range(min(mode, OVER) if mode != CORNER else 0):
+        found = listed(kind, found)
+        odd = found % 2
+
+        @pl.when(odd == 1)
         def _():
-            order[found] = j
-
-        return found + wanted.astype(jnp.int32)
-
-    found = lax.fori_loop(0, slot_count, choose, jnp.int32(0))
+            order[0] = order[found - 1]
+
+        found = odd
+    found = listed(mode, found)
 
     def steps(at):
         slot = order[at]
@@ -305,23 +310,25 @@
 
     lax.fori_loop(0, found // 2, both, 0)
 
-    @pl.when(found % 2 == 1)
-    def _():
-        alternate([steps(found - 1)])
+    if mode in (OVER, CORNER):
+
+        @pl.when(found % 2 == 1)
+        def _():
+            alternate([steps(found - 1)])
 
     if mode == BESIDE:
         outs[0][...] = total[0, :8, :128]
     if mode == OVER:
-        for k in range(4):
-            for d, rows in enumerate((first, last)):
-                outs[d][k] = total[k, rows, pl.ds(2 * n, tile - 2 * n)].astype(HALF)
+        for turn in range(2):
+            for k in range(4):
+                outs[turn][k] = total[k, row_halo[turn], pl.ds(2 * n, tile - 2 * n)].astype(HALF)
     if mode == CORNER:
         ends, edge = outs[:2], outs[2]
-        for k in range(4):
-            for e, (cols, edge_cols) in enumerate(((first, pl.ds(n, n)), (last, pl.ds(tile, n)))):
-                for d, rows in enumerate((first, last)):
-                    ends[e][d, k] = total[k, rows, cols].astype(HALF)
-                    edge[d, e, k] = total[k, rows, edge_cols]
+        for turn in range(2):
+            for d in range(2):
+                for k in range(4):
+                    ends[turn][d, k] = total[k, row_halo[d], col_halo[turn]].astype(HALF)
+                    edge[d, turn, k] = total[k, row_halo[d], col_edge[turn]]
 
 
 def run_slots(mode, scalars, constants, window, total=None, sources=()):
@@ -361,16 +368,18 @@
     )(*operands)
 
 
-def turn_kernel(n, over, below, token, to_left, to_right):
-    tile = over.shape[2]
-    for d, band in enumerate((over, below)):
-        to_left[:, d * n : (d + 1) * n] = band[:, :, :n]
-        to_right[:, d * n : (d + 1) * n] = band[:, :, tile - n :]
-
-
-def turn(over, below, token):
-    planes, n, _ = over.shape
-    out = jax.ShapeDtypeStruct((planes, 2 * n, n), HALF)
+def turn_kernel(n, first, second, token, *outs):
+    planes, _, tile = first.shape
+    for turn in range(2):
+        cols = pick(ahead("col", turn), 0, tile - n, n)
+        for d, band in enumerate((first, second)):
+            for k in range(planes):
+                outs[turn][d, k] = band[k, :, cols]
+
+
+def turn_ends(first, second, token):
+    planes, n, _ = first.shape
+    out = jax.ShapeDtypeStruct((2, planes, n, n), HALF)
     return pl.pallas_call(
         functools.partial(turn_kernel, n),
         out_shape=[out, out],
@@ -378,14 +387,15 @@
         out_specs=[VMEM] * 2,
         compiler_params=pltpu.CompilerParams(vmem_limit_bytes=8 << 20),
         name="turn",
-    )(over, below, token)
-
-
-def sides_kernel(n, total, token, left, right):
-    tile = left.shape[1]
-    for k in range(left.shape[0]):
-        left[k] = total[k, pl.ds(n, tile), pl.ds(0, n)].astype(HALF)
-        right[k] = total[k, pl.ds(n, tile), pl.ds(n + tile, n)].astype(HALF)
+    )(first, second, token)
+
+
+def sides_kernel(n, total, token, *outs):
+    planes, tile = outs[0].shape[:2]
+    for turn in range(2):
+        cols = pick(ahead("col", turn), 0, n + tile, n)
+        for k in range(planes):
+            outs[turn][k] = total[k, pl.ds(n, tile), cols].astype(HALF)
 
 
 def sides(total, token, n):
@@ -400,13 +410,13 @@
     )(total, token)
 
 
-def join_kernel(edge, from_left, from_right, up, down):
-    for d, out in enumerate((up, down)):
-        out[0] = (edge[d, 0] + from_left[d].astype(FULL)).astype(HALF)
-        out[1] = (edge[d, 1] + from_right[d].astype(FULL)).astype(HALF)
-
-
-def join(edge, from_left, from_right):
+def join_kernel(edge, first, second, *outs):
+    for d, out in enumerate(outs):
+        out[0] = (edge[d, 0] + first[d].astype(FULL)).astype(HALF)
+        out[1] = (edge[d, 1] + second[d].astype(FULL)).astype(HALF)
+
+
+def join(edge, first, second):
     out = jax.ShapeDtypeStruct(edge.shape[1:], HALF)
     return pl.pallas_call(
         join_kernel,
@@ -415,21 +425,21 @@
         out_specs=[VMEM] * 2,
         compiler_params=pltpu.CompilerParams(vmem_limit_bytes=8 << 20),
         name="join",
-    )(edge, from_left, from_right)
-
-
-def settle_kernel(n, from_left, from_right, total_in, total, out, sems):
+    )(edge, first, second)
+
+
+def settle_kernel(n, first, second, total_in, total, out, sems):
     tile = out.shape[1]
-    inner = pl.ds(n, tile)
-    for k in range(4):
-        total[k, inner, pl.ds(n, n)] += from_left[k].astype(FULL)
-        total[k, inner, pl.ds(tile, n)] += from_right[k].astype(FULL)
+    for turn, side in enumerate((first, second)):
+        cols = pick(ahead("col", turn), n, tile, n)
+        for k in range(out.shape[0]):
+            total[k, pl.ds(n, tile), cols] += side[k].astype(FULL)
     rows = tile - 2 * n
-    run_copies([(total.at[:, pl.ds(2 * n, rows), inner], out.at[:, pl.ds(n, rows)])], sems)
-
-
-def settle(total, from_left, from_right, n):
-    planes, tile = from_left.shape[:2]
+    run_copies([(total.at[:, pl.ds(2 * n, rows), pl.ds(n, tile)], out.at[:, pl.ds(n, rows)])], sems)
+
+
+def settle(total, first, second, n):
+    planes, tile = first.shape[:2]
     return pl.pallas_call(
         functools.partial(settle_kernel, n),
         out_shape=[
@@ -442,23 +452,22 @@
         input_output_aliases={2: 0},
         compiler_params=pltpu.CompilerParams(vmem_limit_bytes=16 << 20),
         name="settle",
-    )(from_left, from_right, total)
-
-
-def finish_kernel(n, core_over, core_below, edge_over, edge_below, total, out_in, out, band, sems):
-    tile = out.shape[1]
+    )(first, second, total)
+
+
+def finish_kernel(n, core_0, core_1, edge_0, edge_1, total, out_in, out, band, sems):
+    planes, tile = out.shape[:2]
     copies = []
-    for d, (core, edge, at, to) in enumerate(
-        ((core_over, edge_over, n, 0), (core_below, edge_below, tile, tile - n))
-    ):
-        rows = pl.ds(at, n)
-        for k in range(4):
-            band[d, k, :, :n] = total[k, rows, pl.ds(n, n)] + edge[0, k].astype(FULL)
-            band[d, k, :, n : tile - n] = total[k, rows, pl.ds(2 * n, tile - 2 * n)] + core[
-                k
-            ].astype(FULL)
-            band[d, k, :, tile - n :] = total[k, rows, pl.ds(tile, n)] + edge[1, k].astype(FULL)
-        copies.append(pltpu.make_async_copy(band.at[d], out.at[:, pl.ds(to, n)], sems.at[d]))
+    for turn, (core, edge) in enumerate(((core_0, edge_0), (core_1, edge_1))):
+        side = ahead("row", turn)
+        rows = pick(side, n, tile, n)
+        for k in range(planes):
+            band[turn, k] = total[k, rows, pl.ds(n, tile)]
+            band[turn, k, :, pl.ds(n, tile - 2 * n)] += core[k].astype(FULL)
+            for e in range(2):
+                band[turn, k, :, pick(ahead("col", e), 0, tile - n, n)] += edge[e, k].astype(FULL)
+        target = out.at[:, pick(side, 0, tile - n, n)]
+        copies.append(pltpu.make_async_copy(band.at[turn], target, sems.at[turn]))
         copies[-1].start()
     for copy in copies:
         copy.wait()
@@ -478,42 +487,30 @@
     )(*cores, *edges, total, out)
 
 
+def both(parts, axis):
+    return [exchange(part, axis, turn) for turn, part in enumerate(parts)]
+
+
 def per_device(objects, illumination, propagator_phase, intensity, offsets, counts):
     extent = intensity.shape[1]
     n = extent // 2
     scalars = (offsets.T, counts)
-    top, bottom = strips(objects, n)
-    from_above = from_behind(bottom, "row", 1)
-    from_below = from_behind(top, "row", -1)
-    window, left, right = prepare(objects, n)
-    from_left = from_behind(right, "col", 1)
-    from_right = from_behind(left, "col", -1)
+    window, *strips = prepare(objects, n)
+    over = both(strips[:2], "row")
+    beside = both(strips[2:], "col")
     constants = [jnp.asarray(half_tables(extent)), illumination, propagator_phase, intensity]
     total, constants[2] = run_slots(INSIDE, scalars, constants, window)
-    window, total, token = run_slots(
-        BESIDE, scalars, constants, window, total, (from_left, from_right)
-    )
-    to_left, to_right = turn(from_above, from_below, token)
-    corner_left = from_behind(to_right, "col", 1)
-    corner_right = from_behind(to_left, "col", -1)
-    window, total, core_up, core_down = run_slots(
-        OVER, scalars, constants, window, total, (from_above, from_below)
-    )
-    core_below = from_behind(core_up, "row", -1)
-    core_over = from_behind(core_down, "row", 1)
-    _, total, ends_left, ends_right, edge = run_slots(
-        CORNER, scalars, constants, window, total, (corner_left, corner_right)
-    )
-    ends_from_right = from_behind(ends_left, "col", -1)
-    ends_from_left = from_behind(ends_right, "col", 1)
-    edge_up, edge_down = join(edge, ends_from_left, ends_from_right)
-    edge_below = from_behind(edge_up, "row", -1)
-    edge_over = from_behind(edge_down, "row", 1)
-    side_left, side_right = sides(total, edge_up, n)
-    side_from_right = from_behind(side_left, "col", -1)
-    side_from_left = from_behind(side_right, "col", 1)
-    total, out = settle(total, side_from_left, side_from_right, n)
-    return finish(total, out, (core_over, core_below), (edge_over, edge_below), n)
+    window, total, token = run_slots(BESIDE, scalars, constants, window, total, beside)
+    corner = both(turn_ends(*over, token), "col")
+    window, total, *cores = run_slots(OVER, scalars, constants, window, total, over)
+    cores = both(cores, "row")
+    _, total, *ends, edge = run_slots(CORNER, scalars, constants, window, total, corner)
+    ends = both(ends, "col")
+    joined = join(edge, *ends)
+    edges = both(joined, "row")
+    outer = both(sides(total, joined[0], n), "col")
+    total, out = settle(total, *outer, n)
+    return finish(total, out, cores, edges, n)
 
 
 def solution(mesh):

time: 107 us -> 86.9 us (0.81)
  waiting for transfers between devices: 37.5 us -> 24.8 us
  local copies, waits for them, and re-layouts: 7.64 us -> 2.35 us
  Pallas kernels: 17.5 us -> 13.8 us
  starting transfers between devices: 42.5 us -> 44.7 us
    ppermute x14, waiting for transfers between devices: 37.5 us -> 24.8 us  [exchange(): return lax.ppermute(x, axis, pairs + [(j, i) for i, j in pairs])]
    unnamed x16 -> x12, local copies, waits for them, and re-layouts: 7.64 us -> 2.35 us
    pallas_call x2 -> x1, Pallas kernels: 3.66 us -> 0.09 us  [turn_ends(): pl.pallas_call(functools.partial(turn_kernel, n), out_shape=[out, out], i...]
    ppermute x14, starting transfers between devices: 42.5 us -> 44.7 us  [exchange(): return lax.ppermute(x, axis, pairs + [(j, i) for i, j in pairs])]
  transfers between devices with their start and end apart: 14 -> 14, of which waited for: 7 -> 4; matrix products, arithmetic and copies ran while one was open for 0% -> 0% of each run, Pallas kernels for 12% -> 12%
where the time goes in v1:
time: 86.9 us; the launch traced here: 86.7 us
  starting transfers between devices  44.7 us (51%)
  waiting for transfers between devices  24.8 us (29%)
  Pallas kernels  13.8 us (16%)
  local copies, waits for them, and re-layouts  2.35 us (3%)
  between operations  1.07 us (1%)
    ppermute x14, starting transfers between devices, exchange(): return lax.ppermute(x, axis, pairs + [(j, i) for i, j in pairs])  44.7 us
    ppermute x14, waiting for transfers between devices, exchange(): return lax.ppermute(x, axis, pairs + [(j, i) for i, j in pairs])  24.8 us
    pallas_call x4, Pallas kernels, run_slots(): pl.pallas_call(functools.partial(slots_kernel, mode), out_shape=[jax.Shap...  9.7 us
    unnamed x12, local copies, waits for them, and re-layouts  2.35 us
  transfers between devices with their start and end apart: 14, of which 4 were waited for; matrix products, arithmetic and copies ran while one was open for 0% of the time, Pallas kernels for 12%

profile of v1, /device:TPU:9, one launch (start us, length us, event | category | flops | bytes accessed | tf_op | source)
XLA Modules:
  0.0 86.7 jit_solution(7117430453921536642)
XLA Ops:
  0.0 0.0 copy-start.1
  0.0 0.0 copy-start
  0.0 0.0 copy-start.3
  0.0 0.0 copy-start.4
  0.0 2.3 %copy-done.4 = f32[4,512,512]{2,1,0:T(8,128)S(1)} copy-done((f32[4,512,512]{2,1,0:T(8,128)S(1)}, f32[4,512,512]{2,1,0:T(8,128)}, u32[]{:S(2)}) %copy-start.4) | copy-done | bytes 4194328
  2.4 0.6 prepare.1
  2.9 0.8 collective-permute-start.2
  3.7 3.1 %collective-permute-start.3 = (bf16[4,512,128]{2,1,0:T(8,128)(2,1)S(1)}, bf16[4,512,128]{2,1,0:T(8,128)(2,1)S(1)}, u32[]{:S(2)}, u32[]{:S(2)}) collective-permute-start(bf16[4,512,128]{2,1,0:T(8,128)(2,1)S(1)} %get-tuple-element.36), channel_id=1, source_target_pairs={{1,2},{3,4},{5,6},{2,1},{4,3},{6,5},{9,10},{11,12},{13,14},{10,9},... | collective-permute-start | bytes 1572872 | tf_op jit(solution)/shard_map/ppermute | solution.py:20
  6.8 1.3 %collective-permute-start = (bf16[4,128,512]{2,1,0:T(8,128)(2,1)S(1)}, bf16[4,128,512]{2,1,0:T(8,128)(2,1)S(1)}, u32[]{:S(2)}, u32[]{:S(2)}) collective-permute-start(bf16[4,128,512]{2,1,0:T(8,128)(2,1)S(1)} %get-tuple-element.33), channel_id=1, source_target_pairs={{0,8},{16,24},{8,0},{24,16},{1,9},{17,25},{9,1},{25,17},{2,10},{18... | collective-permute-start | bytes 1572872 | tf_op jit(solution)/shard_map/ppermute | solution.py:20
  8.1 0.7 collective-permute-start.1
  9.4 0.0 copy-done.1
  9.4 0.0 copy-done
  9.4 0.0 copy-done.2
  9.4 0.0 copy-done.3
  9.4 0.0 copy-done.5
  9.5 3.1 %shard_map.73 = (f32[4,768,768]{2,1,0:T(8,128)S(1)}, f32[2,256,256]{2,1,0:T(8,128)S(1)}) custom-call(s32[2,12]{1,0:T(2,128)S(1)} %bitcast.1, s32[1]{0:T(128)S(6)} %copy.24.counts, bf16[6,256,256]{2,1,0:T(8,128)(2,1)S(1)} %copy-done.1, f32[2,256,256]{2,1,0:T(8,128)S(1)} %copy-done.2, f32[256,256]{1,0:T(8,128)S(1)} %copy-done.5, ...), custom_call_target="tpu_custom_call" | custom-call | flops 2617245696 | tf_op jit(solution)/shard_map/pallas_call | solution.py:357
  12.5 0.0 collective-permute-done.2.refs_0_
  12.5 1.9 %collective-permute-done.3.refs_1_ = bf16[4,512,128]{2,1,0:T(8,128)(2,1)S(1)} collective-permute-done((bf16[4,512,128]{2,1,0:T(8,128)(2,1)S(1)}, bf16[4,512,128]{2,1,0:T(8,128)(2,1)S(1)}, u32[]{:S(2)}, u32[]{:S(2)}) %collective-permute-start.3) | collective-permute-done | bytes 524320 | tf_op jit(solution)/shard_map/ppermute | solution.py:20
  14.5 1.2 %shard_map.74 = (bf16[4,768,768]{2,1,0:T(8,128)(2,1)S(1)}, f32[4,768,768]{2,1,0:T(8,128)S(1)}, f32[8,128]{1,0:T(8,128)S(1)}) custom-call(s32[2,12]{1,0:T(2,128)S(1)} %bitcast.2, s32[1]{0:T(128)S(6)} %copy.24.counts, bf16[6,256,256]{2,1,0:T(8,128)(2,1)S(1)} %copy-done.1, f32[2,256,256]{2,1,0:T(8,128)S(1)} %copy-done.2, ...), custom_call_target="tpu_custom_call", output_to_operand_aliasing={{0}: (8, {}), {1}: (9, {})} | custom-call | flops 2617245696 | tf_op jit(solution)/shard_map/pallas_call | solution.py:357
  15.6 4.9 %collective-permute-done.refs_0_.first = bf16[4,128,512]{2,1,0:T(8,128)(2,1)S(1)} collective-permute-done((bf16[4,128,512]{2,1,0:T(8,128)(2,1)S(1)}, bf16[4,128,512]{2,1,0:T(8,128)(2,1)S(1)}, u32[]{:S(2)}, u32[]{:S(2)}) %collective-permute-start) | collective-permute-done | bytes 524320 | tf_op jit(solution)/shard_map/ppermute | solution.py:20
  20.5 0.0 collective-permute-done.1.refs_1_.second
  20.5 0.1 turn.1
  20.6 0.1 collective-permute-start.6
  20.7 8.9 %collective-permute-start.7 = (bf16[2,4,128,128]{3,2,1,0:T(8,128)(2,1)S(1)}, bf16[2,4,128,128]{3,2,1,0:T(8,128)(2,1)S(1)}, u32[]{:S(2)}, u32[]{:S(2)}) collective-permute-start(bf16[2,4,128,128]{3,2,1,0:T(8,128)(2,1)S(1)} %get-tuple-element.44), channel_id=1, source_target_pairs={{1,2},{3,4},{5,6},{2,1},{4,3},{6,5},{9,10},{11,12},{13,14},{10,9},... | collective-permute-start | bytes 786440 | tf_op jit(solution)/shard_map/ppermute | solution.py:20
  29.6 4.4 %shard_map.75 = (bf16[4,768,768]{2,1,0:T(8,128)(2,1)S(1)}, f32[4,768,768]{2,1,0:T(8,128)S(1)}, bf16[4,128,256]{2,1,0:T(8,128)(2,1)S(1)}, bf16[4,128,256]{2,1,0:T(8,128)(2,1)S(1)}) custom-call(s32[2,12]{1,0:T(2,128)S(1)} %bitcast.3, s32[1]{0:T(128)S(6)} %copy.24.counts, ...), custom_call_target="tpu_custom_call", output_to_operand_aliasing={{0}: (8, {}), {1}: (9, {})} | custom-call | flops 2617245696 | tf_op jit(solution)/shard_map/pallas_call | solution.py:357
  34.0 0.0 collective-permute-done.6.refs_0_
  34.0 0.0 collective-permute-done.7.refs_1_
  34.0 1.0 %shard_map.76 = (bf16[4,768,768]{2,1,0:T(8,128)(2,1)S(1)}, f32[4,768,768]{2,1,0:T(8,128)S(1)}, bf16[2,4,128,128]{3,2,1,0:T(8,128)(2,1)S(1)}, bf16[2,4,128,128]{3...) custom-call(s32[2,12]{1,0:T(2,128)S(1)} %bitcast.4, ...), custom_call_target="tpu_custom_call", output_to_operand_aliasing={{0}: (8, {}), {1}: (9, {})} | custom-call | flops 2617245696 | tf_op jit(solution)/shard_map/pallas_call | solution.py:357
  35.1 0.1 collective-permute-start.8
  35.2 6.2 %collective-permute-start.9 = (bf16[2,4,128,128]{3,2,1,0:T(8,128)(2,1)S(1)}, bf16[2,4,128,128]{3,2,1,0:T(8,128)(2,1)S(1)}, u32[]{:S(2)}, u32[]{:S(2)}) collective-permute-start(bf16[2,4,128,128]{3,2,1,0:T(8,128)(2,1)S(1)} %get-tuple-element.49), channel_id=1, source_target_pairs={{1,2},{3,4},{5,6},{2,1},{4,3},{6,5},{9,10},{11,12},{13,14},{10,9},... | collective-permute-start | bytes 786440 | tf_op jit(solution)/shard_map/ppermute | solution.py:20
  41.4 0.0 collective-permute-done.8.first
  41.4 4.0 %collective-permute-done.9.second = bf16[2,4,128,128]{3,2,1,0:T(8,128)(2,1)S(1)} collective-permute-done((bf16[2,4,128,128]{3,2,1,0:T(8,128)(2,1)S(1)}, bf16[2,4,128,128]{3,2,1,0:T(8,128)(2,1)S(1)}, u32[]{:S(2)}, u32[]{:S(2)}) %collective-permute-start.9) | collective-permute-done | bytes 262176 | tf_op jit(solution)/shard_map/ppermute | solution.py:20
  45.4 0.1 join.1
  45.5 0.2 sides.1
  45.7 0.1 collective-permute-start.12
  45.8 6.3 %collective-permute-start.13 = (bf16[4,512,128]{2,1,0:T(8,128)(2,1)S(1)}, bf16[4,512,128]{2,1,0:T(8,128)(2,1)S(1)}, u32[]{:S(2)}, u32[]{:S(2)}) collective-permute-start(bf16[4,512,128]{2,1,0:T(8,128)(2,1)S(1)} %get-tuple-element.54), channel_id=1, source_target_pairs={{1,2},{3,4},{5,6},{2,1},{4,3},{6,5},{9,10},{11,12},{13,14},{10,9},... | collective-permute-start | bytes 1572872 | tf_op jit(solution)/shard_map/ppermute | solution.py:20
  52.1 11.0 %collective-permute-start.4 = (bf16[4,128,256]{2,1,0:T(8,128)(2,1)S(1)}, bf16[4,128,256]{2,1,0:T(8,128)(2,1)S(1)}, u32[]{:S(2)}, u32[]{:S(2)}) collective-permute-start(bf16[4,128,256]{2,1,0:T(8,128)(2,1)S(1)} %get-tuple-element.40), channel_id=1, source_target_pairs={{0,8},{16,24},{8,0},{24,16},{1,9},{17,25},{9,1},{25,17},{2,10},{18... | collective-permute-start | bytes 786440 | tf_op jit(solution)/shard_map/ppermute | solution.py:20
  63.0 0.7 collective-permute-start.5
  63.7 0.7 collective-permute-start.11
  64.4 0.0 collective-permute-done.12.first
  64.4 4.9 %collective-permute-start.10 = (bf16[2,4,128,128]{3,2,1,0:T(8,128)(2,1)S(1)}, bf16[2,4,128,128]{3,2,1,0:T(8,128)(2,1)S(1)}, u32[]{:S(2)}, u32[]{:S(2)}) collective-permute-start(bf16[2,4,128,128]{3,2,1,0:T(8,128)(2,1)S(1)} %get-tuple-element.50.token), channel_id=1, source_target_pairs={{0,8},{16,24},{8,0},{24,16},{1,9},{17,25},{9,1},{25,17},{2,10},{18... | collective-permute-start | bytes 786440 | tf_op jit(solution)/shard_map/ppermute | solution.py:20
  69.3 0.0 collective-permute-done.13.second
  69.3 1.6 %settle.1 = (f32[4,768,768]{2,1,0:T(8,128)S(1)}, f32[4,512,512]{2,1,0:T(8,128)}) custom-call(bf16[4,512,128]{2,1,0:T(8,128)(2,1)S(1)} %collective-permute-done.12.first, bf16[4,512,128]{2,1,0:T(8,128)(2,1)S(1)} %collective-permute-done.13.second, f32[4,768,768]{2,1,0:T(8,128)S(1)} %get-tuple-element.52.total.total_in), custom_call_target="tpu_custom_call", output_to_operand_aliasing={{0}: (2, {})} | custom-call | tf_op jit(solution)/shard_map/settle/pallas_call | solution.py:443
  70.9 0.0 collective-permute-done.4.core_0
  70.9 0.0 collective-permute-done.5.core_1
  71.0 0.0 collective-permute-done.11.edge_1
  71.0 14.0 %collective-permute-done.10.edge_0 = bf16[2,4,128,128]{3,2,1,0:T(8,128)(2,1)S(1)} collective-permute-done((bf16[2,4,128,128]{3,2,1,0:T(8,128)(2,1)S(1)}, bf16[2,4,128,128]{3,2,1,0:T(8,128)(2,1)S(1)}, u32[]{:S(2)}, u32[]{:S(2)}) %collective-permute-start.10) | collective-permute-done | bytes 262176 | tf_op jit(solution)/shard_map/ppermute | solution.py:20
  85.0 1.6 %finish.1 = f32[4,512,512]{2,1,0:T(8,128)} custom-call(bf16[4,128,256]{2,1,0:T(8,128)(2,1)S(1)} %collective-permute-done.4.core_0, bf16[4,128,256]{2,1,0:T(8,128)(2,1)S(1)} %collective-permute-done.5.core_1, bf16[2,4,128,128]{3,2,1,0:T(8,128)(2,1)S(1)} %collective-permute-done.10.edge_0, ...), custom_call_target="tpu_custom_call", output_to_operand_aliasing={{}: (5, {})} | custom-call | tf_op jit(solution)/shard_map/finish/pallas_call | solution.py:478
  (2 shorter events, 0.0 us)
Async XLA Ops:
  0.0 9.4 %copy-start.1 = (bf16[6,256,256]{2,1,0:T(8,128)(2,1)S(1)}, bf16[6,256,256]{2,1,0:T(8,128)(2,1)}, u32[]{:S(2)}) copy-start(bf16[6,256,256]{2,1,0:T(8,128)(2,1)} %constant.2.clone.tab) | copy-start | bytes 2359300
  0.0 9.4 %copy-start = (bf16[12,256,256]{2,1,0:T(8,128)(2,1)S(1)}, bf16[12,256,256]{2,1,0:T(8,128)(2,1)}, u32[]{:S(2)}) copy-start(bf16[12,256,256]{2,1,0:T(8,128)(2,1)} %measured.7) | copy-start | bytes 4718596
  0.0 9.4 %copy-start.2 = (f32[2,256,256]{2,1,0:T(8,128)S(1)}, f32[2,256,256]{2,1,0:T(8,128)}, u32[]{:S(2)}) copy-start(f32[2,256,256]{2,1,0:T(8,128)} %light.7) | copy-start | bytes 1572868
  0.0 9.4 %copy-start.3 = (s32[12,2]{0,1:T(2,128)S(1)}, s32[12,2]{0,1:T(2,128)}, u32[]{:S(2)}) copy-start(s32[12,2]{0,1:T(2,128)} %param.11) | copy-start | bytes 292
  0.0 2.3 %copy-start.4 = (f32[4,512,512]{2,1,0:T(8,128)S(1)}, f32[4,512,512]{2,1,0:T(8,128)}, u32[]{:S(2)}) copy-start(f32[4,512,512]{2,1,0:T(8,128)} %objects.1) | copy-start | bytes 12582916
  2.4 7.1 %copy-start.5 = (f32[256,256]{1,0:T(8,128)S(1)}, f32[256,256]{1,0:T(8,128)}, u32[]{:S(2)}) copy-start(f32[256,256]{1,0:T(8,128)} %spread.1) | copy-start | bytes 786436
  2.9 9.6 %collective-permute-start.2 = (bf16[4,512,128]{2,1,0:T(8,128)(2,1)S(1)}, bf16[4,512,128]{2,1,0:T(8,128)(2,1)S(1)}, u32[]{:S(2)}, u32[]{:S(2)}) collective-permute-start(bf16[4,512,128]{2,1,0:T(8,128)(2,1)S(1)} %get-tuple-element.35), channel_id=1, source_target_pairs={{0,1},{2,3},{4,5},{6,7},{1,0},{3,2},{5,4},{7,6},{8,9},{10,11},{12,... | collective-permute-start | bytes 1572872 | tf_op jit(solution)/shard_map/ppermute | solution.py:20
  3.7 10.8 %collective-permute-start.3 = (bf16[4,512,128]{2,1,0:T(8,128)(2,1)S(1)}, bf16[4,512,128]{2,1,0:T(8,128)(2,1)S(1)}, u32[]{:S(2)}, u32[]{:S(2)}) collective-permute-start(bf16[4,512,128]{2,1,0:T(8,128)(2,1)S(1)} %get-tuple-element.36), channel_id=1, source_target_pairs={{1,2},{3,4},{5,6},{2,1},{4,3},{6,5},{9,10},{11,12},{13,14},{10,9},... | collective-permute-start | bytes 1572872 | tf_op jit(solution)/shard_map/ppermute | solution.py:20
  6.8 13.7 %collective-permute-start = (bf16[4,128,512]{2,1,0:T(8,128)(2,1)S(1)}, bf16[4,128,512]{2,1,0:T(8,128)(2,1)S(1)}, u32[]{:S(2)}, u32[]{:S(2)}) collective-permute-start(bf16[4,128,512]{2,1,0:T(8,128)(2,1)S(1)} %get-tuple-element.33), channel_id=1, source_target_pairs={{0,8},{16,24},{8,0},{24,16},{1,9},{17,25},{9,1},{25,17},{2,10},{18... | collective-permute-start | bytes 1572872 | tf_op jit(solution)/shard_map/ppermute | solution.py:20
  8.1 12.4 %collective-permute-start.1 = (bf16[4,128,512]{2,1,0:T(8,128)(2,1)S(1)}, bf16[4,128,512]{2,1,0:T(8,128)(2,1)S(1)}, u32[]{:S(2)}, u32[]{:S(2)}) collective-permute-start(bf16[4,128,512]{2,1,0:T(8,128)(2,1)S(1)} %get-tuple-element.34), channel_id=1, source_target_pairs={{8,16},{16,8},{9,17},{17,9},{10,18},{18,10},{11,19},{19,11},{12,20... | collective-permute-start | bytes 1572872 | tf_op jit(solution)/shard_map/ppermute | solution.py:20
  20.6 13.4 %collective-permute-start.6 = (bf16[2,4,128,128]{3,2,1,0:T(8,128)(2,1)S(1)}, bf16[2,4,128,128]{3,2,1,0:T(8,128)(2,1)S(1)}, u32[]{:S(2)}, u32[]{:S(2)}) collective-permute-start(bf16[2,4,128,128]{3,2,1,0:T(8,128)(2,1)S(1)} %get-tuple-element.43), channel_id=1, source_target_pairs={{0,1},{2,3},{4,5},{6,7},{1,0},{3,2},{5,4},{7,6},{8,9},{10,11},{12,... | collective-permute-start | bytes 786440 | tf_op jit(solution)/shard_map/ppermute | solution.py:20
  20.7 13.4 %collective-permute-start.7 = (bf16[2,4,128,128]{3,2,1,0:T(8,128)(2,1)S(1)}, bf16[2,4,128,128]{3,2,1,0:T(8,128)(2,1)S(1)}, u32[]{:S(2)}, u32[]{:S(2)}) collective-permute-start(bf16[2,4,128,128]{3,2,1,0:T(8,128)(2,1)S(1)} %get-tuple-element.44), channel_id=1, source_target_pairs={{1,2},{3,4},{5,6},{2,1},{4,3},{6,5},{9,10},{11,12},{13,14},{10,9},... | collective-permute-start | bytes 786440 | tf_op jit(solution)/shard_map/ppermute | solution.py:20
  35.1 6.3 %collective-permute-start.8 = (bf16[2,4,128,128]{3,2,1,0:T(8,128)(2,1)S(1)}, bf16[2,4,128,128]{3,2,1,0:T(8,128)(2,1)S(1)}, u32[]{:S(2)}, u32[]{:S(2)}) collective-permute-start(bf16[2,4,128,128]{3,2,1,0:T(8,128)(2,1)S(1)} %get-tuple-element.48), channel_id=1, source_target_pairs={{0,1},{2,3},{4,5},{6,7},{1,0},{3,2},{5,4},{7,6},{8,9},{10,11},{12,... | collective-permute-start | bytes 786440 | tf_op jit(solution)/shard_map/ppermute | solution.py:20
  35.2 10.2 %collective-permute-start.9 = (bf16[2,4,128,128]{3,2,1,0:T(8,128)(2,1)S(1)}, bf16[2,4,128,128]{3,2,1,0:T(8,128)(2,1)S(1)}, u32[]{:S(2)}, u32[]{:S(2)}) collective-permute-start(bf16[2,4,128,128]{3,2,1,0:T(8,128)(2,1)S(1)} %get-tuple-element.49), channel_id=1, source_target_pairs={{1,2},{3,4},{5,6},{2,1},{4,3},{6,5},{9,10},{11,12},{13,14},{10,9},... | collective-permute-start | bytes 786440 | tf_op jit(solution)/shard_map/ppermute | solution.py:20
  45.7 18.7 %collective-permute-start.12 = (bf16[4,512,128]{2,1,0:T(8,128)(2,1)S(1)}, bf16[4,512,128]{2,1,0:T(8,128)(2,1)S(1)}, u32[]{:S(2)}, u32[]{:S(2)}) collective-permute-start(bf16[4,512,128]{2,1,0:T(8,128)(2,1)S(1)} %get-tuple-element.53), channel_id=1, source_target_pairs={{0,1},{2,3},{4,5},{6,7},{1,0},{3,2},{5,4},{7,6},{8,9},{10,11},{12,... | collective-permute-start | bytes 1572872 | tf_op jit(solution)/shard_map/ppermute | solution.py:20
  45.8 23.6 %collective-permute-start.13 = (bf16[4,512,128]{2,1,0:T(8,128)(2,1)S(1)}, bf16[4,512,128]{2,1,0:T(8,128)(2,1)S(1)}, u32[]{:S(2)}, u32[]{:S(2)}) collective-permute-start(bf16[4,512,128]{2,1,0:T(8,128)(2,1)S(1)} %get-tuple-element.54), channel_id=1, source_target_pairs={{1,2},{3,4},{5,6},{2,1},{4,3},{6,5},{9,10},{11,12},{13,14},{10,9},... | collective-permute-start | bytes 1572872 | tf_op jit(solution)/shard_map/ppermute | solution.py:20
  52.1 18.9 %collective-permute-start.4 = (bf16[4,128,256]{2,1,0:T(8,128)(2,1)S(1)}, bf16[4,128,256]{2,1,0:T(8,128)(2,1)S(1)}, u32[]{:S(2)}, u32[]{:S(2)}) collective-permute-start(bf16[4,128,256]{2,1,0:T(8,128)(2,1)S(1)} %get-tuple-element.40), channel_id=1, source_target_pairs={{0,8},{16,24},{8,0},{24,16},{1,9},{17,25},{9,1},{25,17},{2,10},{18... | collective-permute-start | bytes 786440 | tf_op jit(solution)/shard_map/ppermute | solution.py:20
  63.0 7.9 %collective-permute-start.5 = (bf16[4,128,256]{2,1,0:T(8,128)(2,1)S(1)}, bf16[4,128,256]{2,1,0:T(8,128)(2,1)S(1)}, u32[]{:S(2)}, u32[]{:S(2)}) collective-permute-start(bf16[4,128,256]{2,1,0:T(8,128)(2,1)S(1)} %get-tuple-element.41), channel_id=1, source_target_pairs={{8,16},{16,8},{9,17},{17,9},{10,18},{18,10},{11,19},{19,11},{12,20... | collective-permute-start | bytes 786440 | tf_op jit(solution)/shard_map/ppermute | solution.py:20
  63.7 7.2 %collective-permute-start.11 = (bf16[2,4,128,128]{3,2,1,0:T(8,128)(2,1)S(1)}, bf16[2,4,128,128]{3,2,1,0:T(8,128)(2,1)S(1)}, u32[]{:S(2)}, u32[]{:S(2)}) collective-permute-start(bf16[2,4,128,128]{3,2,1,0:T(8,128)(2,1)S(1)} %get-tuple-element.51), channel_id=1, source_target_pairs={{8,16},{16,8},{9,17},{17,9},{10,18},{18,10},{11,19},{19,11},{12,20... | collective-permute-start | bytes 786440 | tf_op jit(solution)/shard_map/ppermute | solution.py:20
  64.4 20.5 %collective-permute-start.10 = (bf16[2,4,128,128]{3,2,1,0:T(8,128)(2,1)S(1)}, bf16[2,4,128,128]{3,2,1,0:T(8,128)(2,1)S(1)}, u32[]{:S(2)}, u32[]{:S(2)}) collective-permute-start(bf16[2,4,128,128]{3,2,1,0:T(8,128)(2,1)S(1)} %get-tuple-element.50.token), channel_id=1, source_target_pairs={{0,8},{16,24},{8,0},{24,16},{1,9},{17,25},{9,1},{25,17},{2,10},{18... | collective-permute-start | bytes 786440 | tf_op jit(solution)/shard_map/ppermute | solution.py:20

commit v2 on v1

--- a/solution.py
+++ b/solution.py
@@ -390,7 +390,7 @@
     )(first, second, token)
 
 
-def sides_kernel(n, total, token, *outs):
+def sides_kernel(n, total, *outs):
     planes, tile = outs[0].shape[:2]
     for turn in range(2):
         cols = pick(ahead("col", turn), 0, n + tile, n)
@@ -398,16 +398,16 @@
             outs[turn][k] = total[k, pl.ds(n, tile), cols].astype(HALF)
 
 
-def sides(total, token, n):
+def sides(total, n):
     out = jax.ShapeDtypeStruct((total.shape[0], total.shape[1] - 2 * n, n), HALF)
     return pl.pallas_call(
         functools.partial(sides_kernel, n),
         out_shape=[out, out],
-        in_specs=[VMEM] * 2,
+        in_specs=[VMEM],
         out_specs=[VMEM] * 2,
         compiler_params=pltpu.CompilerParams(vmem_limit_bytes=8 << 20),
         name="sides",
-    )(total, token)
+    )(total)
 
 
 def join_kernel(edge, first, second, *outs):
@@ -461,14 +461,22 @@
     for turn, (core, edge) in enumerate(((core_0, edge_0), (core_1, edge_1))):
         side = ahead("row", turn)
         rows = pick(side, n, tile, n)
+        to = pick(side, 0, tile - n, n)
         for k in range(planes):
-            band[turn, k] = total[k, rows, pl.ds(n, tile)]
-            band[turn, k, :, pl.ds(n, tile - 2 * n)] += core[k].astype(FULL)
+            band[turn, k, :, pl.ds(n, tile - 2 * n)] = total[
+                k, rows, pl.ds(2 * n, tile - 2 * n)
+            ] + core[k].astype(FULL)
             for e in range(2):
-                band[turn, k, :, pick(ahead("col", e), 0, tile - n, n)] += edge[e, k].astype(FULL)
-        target = out.at[:, pick(side, 0, tile - n, n)]
-        copies.append(pltpu.make_async_copy(band.at[turn], target, sems.at[turn]))
-        copies[-1].start()
+                at = ahead("col", e)
+                band[turn, k, :, pick(at, 0, tile - n, n)] = total[
+                    k, rows, pick(at, n, tile, n)
+                ] + edge[e, k].astype(FULL)
+            copies.append(
+                pltpu.make_async_copy(
+                    band.at[turn, k], out.at[k, to], sems.at[turn * planes + k]
+                )
+            )
+            copies[-1].start()
     for copy in copies:
         copy.wait()
 
@@ -480,7 +488,10 @@
         out_shape=jax.ShapeDtypeStruct(out.shape, FULL),
         in_specs=[VMEM] * 5 + [ANYWHERE],
         out_specs=ANYWHERE,
-        scratch_shapes=[pltpu.VMEM((2, planes, n, tile), FULL), pltpu.SemaphoreType.DMA((2,))],
+        scratch_shapes=[
+            pltpu.VMEM((2, planes, n, tile), FULL),
+            pltpu.SemaphoreType.DMA((2 * planes,)),
+        ],
         input_output_aliases={5: 0},
         compiler_params=pltpu.CompilerParams(vmem_limit_bytes=16 << 20),
         name="finish",
@@ -506,9 +517,8 @@
     cores = both(cores, "row")
     _, total, *ends, edge = run_slots(CORNER, scalars, constants, window, total, corner)
     ends = both(ends, "col")
-    joined = join(edge, *ends)
-    edges = both(joined, "row")
-    outer = both(sides(total, joined[0], n), "col")
+    outer = both(sides(total, n), "col")
+    edges = both(join(edge, *ends), "row")
     total, out = settle(total, *outer, n)
     return finish(total, out, cores, edges, n)
 

time: 86.9 us -> 82.5 us (0.949)
  the two profiles are of different devices: /device:TPU:9 before, /device:TPU:20 now
where the time goes in v2:
time: 82.5 us; the launch traced here: 82.2 us
  waiting for transfers between devices  27.2 us (33%)
  starting transfers between devices  25.8 us (31%)
  Pallas kernels  25.7 us (31%)
  local copies, waits for them, and re-layouts  2.35 us (3%)
  between operations  1.09 us (1%)
    ppermute x14, waiting for transfers between devices, exchange(): return lax.ppermute(x, axis, pairs + [(j, i) for i, j in pairs])  27.2 us
    ppermute x14, starting transfers between devices, exchange(): return lax.ppermute(x, axis, pairs + [(j, i) for i, j in pairs])  25.8 us
    pallas_call x4, Pallas kernels, run_slots(): pl.pallas_call(functools.partial(slots_kernel, mode), out_shape=[jax.Shap...  21.8 us
    unnamed x12, local copies, waits for them, and re-layouts  2.35 us
  transfers between devices with their start and end apart: 14, of which 5 were waited for; matrix products, arithmetic and copies ran while one was open for 0% of the time, Pallas kernels for 22%

profile of v2, /device:TPU:20, one launch (start us, length us, event | category | flops | bytes accessed | tf_op | source)
XLA Modules:
  0.0 82.2 jit_solution(10475191971513077013)
XLA Ops:
  0.0 0.0 copy-start.1
  0.0 0.0 copy-start
  0.0 0.0 copy-start.3
  0.0 0.0 copy-start.4
  0.0 2.3 %copy-done.4 = f32[4,512,512]{2,1,0:T(8,128)S(1)} copy-done((f32[4,512,512]{2,1,0:T(8,128)S(1)}, f32[4,512,512]{2,1,0:T(8,128)}, u32[]{:S(2)}) %copy-start.4) | copy-done | bytes 4194328
  2.4 0.6 prepare.1
  2.9 0.1 collective-permute-start.2
  3.0 2.4 %collective-permute-start.3 = (bf16[4,512,128]{2,1,0:T(8,128)(2,1)S(1)}, bf16[4,512,128]{2,1,0:T(8,128)(2,1)S(1)}, u32[]{:S(2)}, u32[]{:S(2)}) collective-permute-start(bf16[4,512,128]{2,1,0:T(8,128)(2,1)S(1)} %get-tuple-element.36), channel_id=1, source_target_pairs={{1,2},{3,4},{5,6},{2,1},{4,3},{6,5},{9,10},{11,12},{13,14},{10,9},... | collective-permute-start | bytes 1572872 | tf_op jit(solution)/shard_map/ppermute | solution.py:20
  5.5 1.6 %collective-permute-start = (bf16[4,128,512]{2,1,0:T(8,128)(2,1)S(1)}, bf16[4,128,512]{2,1,0:T(8,128)(2,1)S(1)}, u32[]{:S(2)}, u32[]{:S(2)}) collective-permute-start(bf16[4,128,512]{2,1,0:T(8,128)(2,1)S(1)} %get-tuple-element.33), channel_id=1, source_target_pairs={{0,8},{16,24},{8,0},{24,16},{1,9},{17,25},{9,1},{25,17},{2,10},{18... | collective-permute-start | bytes 1572872 | tf_op jit(solution)/shard_map/ppermute | solution.py:20
  7.0 2.4 %collective-permute-start.1 = (bf16[4,128,512]{2,1,0:T(8,128)(2,1)S(1)}, bf16[4,128,512]{2,1,0:T(8,128)(2,1)S(1)}, u32[]{:S(2)}, u32[]{:S(2)}) collective-permute-start(bf16[4,128,512]{2,1,0:T(8,128)(2,1)S(1)} %get-tuple-element.34), channel_id=1, source_target_pairs={{8,16},{16,8},{9,17},{17,9},{10,18},{18,10},{11,19},{19,11},{12,20... | collective-permute-start | bytes 1572872 | tf_op jit(solution)/shard_map/ppermute | solution.py:20
  10.1 0.0 copy-done.1
  10.1 0.0 copy-done
  10.1 0.0 copy-done.2
  10.1 0.0 copy-done.3
  10.1 0.0 copy-done.5
  10.1 7.1 %shard_map.73 = (f32[4,768,768]{2,1,0:T(8,128)S(1)}, f32[2,256,256]{2,1,0:T(8,128)S(1)}) custom-call(s32[2,12]{1,0:T(2,128)S(1)} %bitcast.1, s32[1]{0:T(128)S(6)} %copy.24.counts, bf16[6,256,256]{2,1,0:T(8,128)(2,1)S(1)} %copy-done.1, f32[2,256,256]{2,1,0:T(8,128)S(1)} %copy-done.2, f32[256,256]{1,0:T(8,128)S(1)} %copy-done.5, ...), custom_call_target="tpu_custom_call" | custom-call | flops 2617245696 | tf_op jit(solution)/shard_map/pallas_call | solution.py:357
  17.2 0.0 collective-permute-done.2.refs_0_
  17.2 0.0 collective-permute-done.3.refs_1_
  17.2 5.2 %shard_map.74 = (bf16[4,768,768]{2,1,0:T(8,128)(2,1)S(1)}, f32[4,768,768]{2,1,0:T(8,128)S(1)}, f32[8,128]{1,0:T(8,128)S(1)}) custom-call(s32[2,12]{1,0:T(2,128)S(1)} %bitcast.2, s32[1]{0:T(128)S(6)} %copy.24.counts, bf16[6,256,256]{2,1,0:T(8,128)(2,1)S(1)} %copy-done.1, f32[2,256,256]{2,1,0:T(8,128)S(1)} %copy-done.2, ...), custom_call_target="tpu_custom_call", output_to_operand_aliasing={{0}: (8, {}), {1}: (9, {})} | custom-call | flops 2617245696 | tf_op jit(solution)/shard_map/pallas_call | solution.py:357
  22.5 0.0 collective-permute-done.refs_0_.first
  22.5 8.8 %collective-permute-done.1.refs_1_.second = bf16[4,128,512]{2,1,0:T(8,128)(2,1)S(1)} collective-permute-done((bf16[4,128,512]{2,1,0:T(8,128)(2,1)S(1)}, bf16[4,128,512]{2,1,0:T(8,128)(2,1)S(1)}, u32[]{:S(2)}, u32[]{:S(2)}) %collective-permute-start.1) | collective-permute-done | bytes 524320 | tf_op jit(solution)/shard_map/ppermute | solution.py:20
  31.3 0.1 turn.1
  31.4 0.2 collective-permute-start.6
  31.6 1.9 %collective-permute-start.7 = (bf16[2,4,128,128]{3,2,1,0:T(8,128)(2,1)S(1)}, bf16[2,4,128,128]{3,2,1,0:T(8,128)(2,1)S(1)}, u32[]{:S(2)}, u32[]{:S(2)}) collective-permute-start(bf16[2,4,128,128]{3,2,1,0:T(8,128)(2,1)S(1)} %get-tuple-element.44), channel_id=1, source_target_pairs={{1,2},{3,4},{5,6},{2,1},{4,3},{6,5},{9,10},{11,12},{13,14},{10,9},... | collective-permute-start | bytes 786440 | tf_op jit(solution)/shard_map/ppermute | solution.py:20
  33.5 4.4 %shard_map.75 = (bf16[4,768,768]{2,1,0:T(8,128)(2,1)S(1)}, f32[4,768,768]{2,1,0:T(8,128)S(1)}, bf16[4,128,256]{2,1,0:T(8,128)(2,1)S(1)}, bf16[4,128,256]{2,1,0:T(8,128)(2,1)S(1)}) custom-call(s32[2,12]{1,0:T(2,128)S(1)} %bitcast.3, s32[1]{0:T(128)S(6)} %copy.24.counts, ...), custom_call_target="tpu_custom_call", output_to_operand_aliasing={{0}: (8, {}), {1}: (9, {})} | custom-call | flops 2617245696 | tf_op jit(solution)/shard_map/pallas_call | solution.py:357
  37.9 0.0 collective-permute-done.6.refs_0_
  37.9 1.3 %collective-permute-done.7.refs_1_ = bf16[2,4,128,128]{3,2,1,0:T(8,128)(2,1)S(1)} collective-permute-done((bf16[2,4,128,128]{3,2,1,0:T(8,128)(2,1)S(1)}, bf16[2,4,128,128]{3,2,1,0:T(8,128)(2,1)S(1)}, u32[]{:S(2)}, u32[]{:S(2)}) %collective-permute-start.7) | collective-permute-done | bytes 262176 | tf_op jit(solution)/shard_map/ppermute | solution.py:20
  39.3 5.1 %shard_map.76 = (bf16[4,768,768]{2,1,0:T(8,128)(2,1)S(1)}, f32[4,768,768]{2,1,0:T(8,128)S(1)}, bf16[2,4,128,128]{3,2,1,0:T(8,128)(2,1)S(1)}, bf16[2,4,128,128]{3...) custom-call(s32[2,12]{1,0:T(2,128)S(1)} %bitcast.4, ...), custom_call_target="tpu_custom_call", output_to_operand_aliasing={{0}: (8, {}), {1}: (9, {})} | custom-call | flops 2617245696 | tf_op jit(solution)/shard_map/pallas_call | solution.py:357
  44.4 0.2 sides.1
  44.5 0.1 collective-permute-start.12
  44.6 0.5 collective-permute-start.8
  45.1 4.1 %collective-permute-start.9 = (bf16[2,4,128,128]{3,2,1,0:T(8,128)(2,1)S(1)}, bf16[2,4,128,128]{3,2,1,0:T(8,128)(2,1)S(1)}, u32[]{:S(2)}, u32[]{:S(2)}) collective-permute-start(bf16[2,4,128,128]{3,2,1,0:T(8,128)(2,1)S(1)} %get-tuple-element.49), channel_id=1, source_target_pairs={{1,2},{3,4},{5,6},{2,1},{4,3},{6,5},{9,10},{11,12},{13,14},{10,9},... | collective-permute-start | bytes 786440 | tf_op jit(solution)/shard_map/ppermute | solution.py:20
  49.3 1.9 %collective-permute-start.13 = (bf16[4,512,128]{2,1,0:T(8,128)(2,1)S(1)}, bf16[4,512,128]{2,1,0:T(8,128)(2,1)S(1)}, u32[]{:S(2)}, u32[]{:S(2)}) collective-permute-start(bf16[4,512,128]{2,1,0:T(8,128)(2,1)S(1)} %get-tuple-element.54), channel_id=1, source_target_pairs={{1,2},{3,4},{5,6},{2,1},{4,3},{6,5},{9,10},{11,12},{13,14},{10,9},... | collective-permute-start | bytes 1572872 | tf_op jit(solution)/shard_map/ppermute | solution.py:20
  51.2 0.1 collective-permute-start.4
  51.3 0.0 collective-permute-done.8.first
  51.3 7.9 %collective-permute-start.5 = (bf16[4,128,256]{2,1,0:T(8,128)(2,1)S(1)}, bf16[4,128,256]{2,1,0:T(8,128)(2,1)S(1)}, u32[]{:S(2)}, u32[]{:S(2)}) collective-permute-start(bf16[4,128,256]{2,1,0:T(8,128)(2,1)S(1)} %get-tuple-element.41), channel_id=1, source_target_pairs={{8,16},{16,8},{9,17},{17,9},{10,18},{18,10},{11,19},{19,11},{12,20... | collective-permute-start | bytes 786440 | tf_op jit(solution)/shard_map/ppermute | solution.py:20
  59.2 0.0 collective-permute-done.9.second
  59.2 0.1 join.1
  59.3 0.1 collective-permute-start.10
  59.4 0.0 collective-permute-done.12.first
  59.4 2.6 %collective-permute-start.11 = (bf16[2,4,128,128]{3,2,1,0:T(8,128)(2,1)S(1)}, bf16[2,4,128,128]{3,2,1,0:T(8,128)(2,1)S(1)}, u32[]{:S(2)}, u32[]{:S(2)}) collective-permute-start(bf16[2,4,128,128]{3,2,1,0:T(8,128)(2,1)S(1)} %get-tuple-element.51), channel_id=1, source_target_pairs={{8,16},{16,8},{9,17},{17,9},{10,18},{18,10},{11,19},{19,11},{12,20... | collective-permute-start | bytes 786440 | tf_op jit(solution)/shard_map/ppermute | solution.py:20
  62.0 0.0 collective-permute-done.13.second
  62.0 1.6 %settle.1 = (f32[4,768,768]{2,1,0:T(8,128)S(1)}, f32[4,512,512]{2,1,0:T(8,128)}) custom-call(bf16[4,512,128]{2,1,0:T(8,128)(2,1)S(1)} %collective-permute-done.12.first, bf16[4,512,128]{2,1,0:T(8,128)(2,1)S(1)} %collective-permute-done.13.second, f32[4,768,768]{2,1,0:T(8,128)S(1)} %get-tuple-element.52.total.total_in), custom_call_target="tpu_custom_call", output_to_operand_aliasing={{0}: (2, {})} | custom-call | tf_op jit(solution)/shard_map/settle/pallas_call | solution.py:443
  63.6 0.0 collective-permute-done.4.core_0
  63.6 6.3 %collective-permute-done.5.core_1 = bf16[4,128,256]{2,1,0:T(8,128)(2,1)S(1)} collective-permute-done((bf16[4,128,256]{2,1,0:T(8,128)(2,1)S(1)}, bf16[4,128,256]{2,1,0:T(8,128)(2,1)S(1)}, u32[]{:S(2)}, u32[]{:S(2)}) %collective-permute-start.5) | collective-permute-done | bytes 262176 | tf_op jit(solution)/shard_map/ppermute | solution.py:20
  70.0 1.5 %collective-permute-done.10.edge_0 = bf16[2,4,128,128]{3,2,1,0:T(8,128)(2,1)S(1)} collective-permute-done((bf16[2,4,128,128]{3,2,1,0:T(8,128)(2,1)S(1)}, bf16[2,4,128,128]{3,2,1,0:T(8,128)(2,1)S(1)}, u32[]{:S(2)}, u32[]{:S(2)}) %collective-permute-start.10) | collective-permute-done | bytes 262176 | tf_op jit(solution)/shard_map/ppermute | solution.py:20
  71.5 9.2 %collective-permute-done.11.edge_1 = bf16[2,4,128,128]{3,2,1,0:T(8,128)(2,1)S(1)} collective-permute-done((bf16[2,4,128,128]{3,2,1,0:T(8,128)(2,1)S(1)}, bf16[2,4,128,128]{3,2,1,0:T(8,128)(2,1)S(1)}, u32[]{:S(2)}, u32[]{:S(2)}) %collective-permute-start.11) | collective-permute-done | bytes 262176 | tf_op jit(solution)/shard_map/ppermute | solution.py:20
  80.6 1.4 %finish.1 = f32[4,512,512]{2,1,0:T(8,128)} custom-call(bf16[4,128,256]{2,1,0:T(8,128)(2,1)S(1)} %collective-permute-done.4.core_0, bf16[4,128,256]{2,1,0:T(8,128)(2,1)S(1)} %collective-permute-done.5.core_1, bf16[2,4,128,128]{3,2,1,0:T(8,128)(2,1)S(1)} %collective-permute-done.10.edge_0, ...), custom_call_target="tpu_custom_call", output_to_operand_aliasing={{}: (5, {})} | custom-call | tf_op jit(solution)/shard_map/finish/pallas_call | solution.py:486
  (2 shorter events, 0.0 us)
Async XLA Ops:
  0.0 10.1 %copy-start.1 = (bf16[6,256,256]{2,1,0:T(8,128)(2,1)S(1)}, bf16[6,256,256]{2,1,0:T(8,128)(2,1)}, u32[]{:S(2)}) copy-start(bf16[6,256,256]{2,1,0:T(8,128)(2,1)} %constant.2.clone.tab) | copy-start | bytes 2359300
  0.0 10.1 %copy-start = (bf16[12,256,256]{2,1,0:T(8,128)(2,1)S(1)}, bf16[12,256,256]{2,1,0:T(8,128)(2,1)}, u32[]{:S(2)}) copy-start(bf16[12,256,256]{2,1,0:T(8,128)(2,1)} %measured.7) | copy-start | bytes 4718596
  0.0 10.1 %copy-start.2 = (f32[2,256,256]{2,1,0:T(8,128)S(1)}, f32[2,256,256]{2,1,0:T(8,128)}, u32[]{:S(2)}) copy-start(f32[2,256,256]{2,1,0:T(8,128)} %light.7) | copy-start | bytes 1572868
  0.0 10.1 %copy-start.3 = (s32[12,2]{0,1:T(2,128)S(1)}, s32[12,2]{0,1:T(2,128)}, u32[]{:S(2)}) copy-start(s32[12,2]{0,1:T(2,128)} %param.11) | copy-start | bytes 292
  0.0 2.3 %copy-start.4 = (f32[4,512,512]{2,1,0:T(8,128)S(1)}, f32[4,512,512]{2,1,0:T(8,128)}, u32[]{:S(2)}) copy-start(f32[4,512,512]{2,1,0:T(8,128)} %objects.1) | copy-start | bytes 12582916
  2.4 7.7 %copy-start.5 = (f32[256,256]{1,0:T(8,128)S(1)}, f32[256,256]{1,0:T(8,128)}, u32[]{:S(2)}) copy-start(f32[256,256]{1,0:T(8,128)} %spread.1) | copy-start | bytes 786436
  2.9 14.3 %collective-permute-start.2 = (bf16[4,512,128]{2,1,0:T(8,128)(2,1)S(1)}, bf16[4,512,128]{2,1,0:T(8,128)(2,1)S(1)}, u32[]{:S(2)}, u32[]{:S(2)}) collective-permute-start(bf16[4,512,128]{2,1,0:T(8,128)(2,1)S(1)} %get-tuple-element.35), channel_id=1, source_target_pairs={{0,1},{2,3},{4,5},{6,7},{1,0},{3,2},{5,4},{7,6},{8,9},{10,11},{12,... | collective-permute-start | bytes 1572872 | tf_op jit(solution)/shard_map/ppermute | solution.py:20
  3.0 14.2 %collective-permute-start.3 = (bf16[4,512,128]{2,1,0:T(8,128)(2,1)S(1)}, bf16[4,512,128]{2,1,0:T(8,128)(2,1)S(1)}, u32[]{:S(2)}, u32[]{:S(2)}) collective-permute-start(bf16[4,512,128]{2,1,0:T(8,128)(2,1)S(1)} %get-tuple-element.36), channel_id=1, source_target_pairs={{1,2},{3,4},{5,6},{2,1},{4,3},{6,5},{9,10},{11,12},{13,14},{10,9},... | collective-permute-start | bytes 1572872 | tf_op jit(solution)/shard_map/ppermute | solution.py:20
  5.5 17.0 %collective-permute-start = (bf16[4,128,512]{2,1,0:T(8,128)(2,1)S(1)}, bf16[4,128,512]{2,1,0:T(8,128)(2,1)S(1)}, u32[]{:S(2)}, u32[]{:S(2)}) collective-permute-start(bf16[4,128,512]{2,1,0:T(8,128)(2,1)S(1)} %get-tuple-element.33), channel_id=1, source_target_pairs={{0,8},{16,24},{8,0},{24,16},{1,9},{17,25},{9,1},{25,17},{2,10},{18... | collective-permute-start | bytes 1572872 | tf_op jit(solution)/shard_map/ppermute | solution.py:20
  7.0 24.3 %collective-permute-start.1 = (bf16[4,128,512]{2,1,0:T(8,128)(2,1)S(1)}, bf16[4,128,512]{2,1,0:T(8,128)(2,1)S(1)}, u32[]{:S(2)}, u32[]{:S(2)}) collective-permute-start(bf16[4,128,512]{2,1,0:T(8,128)(2,1)S(1)} %get-tuple-element.34), channel_id=1, source_target_pairs={{8,16},{16,8},{9,17},{17,9},{10,18},{18,10},{11,19},{19,11},{12,20... | collective-permute-start | bytes 1572872 | tf_op jit(solution)/shard_map/ppermute | solution.py:20
  31.4 6.5 %collective-permute-start.6 = (bf16[2,4,128,128]{3,2,1,0:T(8,128)(2,1)S(1)}, bf16[2,4,128,128]{3,2,1,0:T(8,128)(2,1)S(1)}, u32[]{:S(2)}, u32[]{:S(2)}) collective-permute-start(bf16[2,4,128,128]{3,2,1,0:T(8,128)(2,1)S(1)} %get-tuple-element.43), channel_id=1, source_target_pairs={{0,1},{2,3},{4,5},{6,7},{1,0},{3,2},{5,4},{7,6},{8,9},{10,11},{12,... | collective-permute-start | bytes 786440 | tf_op jit(solution)/shard_map/ppermute | solution.py:20
  31.6 7.7 %collective-permute-start.7 = (bf16[2,4,128,128]{3,2,1,0:T(8,128)(2,1)S(1)}, bf16[2,4,128,128]{3,2,1,0:T(8,128)(2,1)S(1)}, u32[]{:S(2)}, u32[]{:S(2)}) collective-permute-start(bf16[2,4,128,128]{3,2,1,0:T(8,128)(2,1)S(1)} %get-tuple-element.44), channel_id=1, source_target_pairs={{1,2},{3,4},{5,6},{2,1},{4,3},{6,5},{9,10},{11,12},{13,14},{10,9},... | collective-permute-start | bytes 786440 | tf_op jit(solution)/shard_map/ppermute | solution.py:20
  44.5 14.8 %collective-permute-start.12 = (bf16[4,512,128]{2,1,0:T(8,128)(2,1)S(1)}, bf16[4,512,128]{2,1,0:T(8,128)(2,1)S(1)}, u32[]{:S(2)}, u32[]{:S(2)}) collective-permute-start(bf16[4,512,128]{2,1,0:T(8,128)(2,1)S(1)} %get-tuple-element.53), channel_id=1, source_target_pairs={{0,1},{2,3},{4,5},{6,7},{1,0},{3,2},{5,4},{7,6},{8,9},{10,11},{12,... | collective-permute-start | bytes 1572872 | tf_op jit(solution)/shard_map/ppermute | solution.py:20
  44.6 6.7 %collective-permute-start.8 = (bf16[2,4,128,128]{3,2,1,0:T(8,128)(2,1)S(1)}, bf16[2,4,128,128]{3,2,1,0:T(8,128)(2,1)S(1)}, u32[]{:S(2)}, u32[]{:S(2)}) collective-permute-start(bf16[2,4,128,128]{3,2,1,0:T(8,128)(2,1)S(1)} %get-tuple-element.48), channel_id=1, source_target_pairs={{0,1},{2,3},{4,5},{6,7},{1,0},{3,2},{5,4},{7,6},{8,9},{10,11},{12,... | collective-permute-start | bytes 786440 | tf_op jit(solution)/shard_map/ppermute | solution.py:20
  45.1 14.1 %collective-permute-start.9 = (bf16[2,4,128,128]{3,2,1,0:T(8,128)(2,1)S(1)}, bf16[2,4,128,128]{3,2,1,0:T(8,128)(2,1)S(1)}, u32[]{:S(2)}, u32[]{:S(2)}) collective-permute-start(bf16[2,4,128,128]{3,2,1,0:T(8,128)(2,1)S(1)} %get-tuple-element.49), channel_id=1, source_target_pairs={{1,2},{3,4},{5,6},{2,1},{4,3},{6,5},{9,10},{11,12},{13,14},{10,9},... | collective-permute-start | bytes 786440 | tf_op jit(solution)/shard_map/ppermute | solution.py:20
  49.3 12.8 %collective-permute-start.13 = (bf16[4,512,128]{2,1,0:T(8,128)(2,1)S(1)}, bf16[4,512,128]{2,1,0:T(8,128)(2,1)S(1)}, u32[]{:S(2)}, u32[]{:S(2)}) collective-permute-start(bf16[4,512,128]{2,1,0:T(8,128)(2,1)S(1)} %get-tuple-element.54), channel_id=1, source_target_pairs={{1,2},{3,4},{5,6},{2,1},{4,3},{6,5},{9,10},{11,12},{13,14},{10,9},... | collective-permute-start | bytes 1572872 | tf_op jit(solution)/shard_map/ppermute | solution.py:20
  51.2 12.5 %collective-permute-start.4 = (bf16[4,128,256]{2,1,0:T(8,128)(2,1)S(1)}, bf16[4,128,256]{2,1,0:T(8,128)(2,1)S(1)}, u32[]{:S(2)}, u32[]{:S(2)}) collective-permute-start(bf16[4,128,256]{2,1,0:T(8,128)(2,1)S(1)} %get-tuple-element.40), channel_id=1, source_target_pairs={{0,8},{16,24},{8,0},{24,16},{1,9},{17,25},{9,1},{25,17},{2,10},{18... | collective-permute-start | bytes 786440 | tf_op jit(solution)/shard_map/ppermute | solution.py:20
  51.3 18.7 %collective-permute-start.5 = (bf16[4,128,256]{2,1,0:T(8,128)(2,1)S(1)}, bf16[4,128,256]{2,1,0:T(8,128)(2,1)S(1)}, u32[]{:S(2)}, u32[]{:S(2)}) collective-permute-start(bf16[4,128,256]{2,1,0:T(8,128)(2,1)S(1)} %get-tuple-element.41), channel_id=1, source_target_pairs={{8,16},{16,8},{9,17},{17,9},{10,18},{18,10},{11,19},{19,11},{12,20... | collective-permute-start | bytes 786440 | tf_op jit(solution)/shard_map/ppermute | solution.py:20
  59.3 12.2 %collective-permute-start.10 = (bf16[2,4,128,128]{3,2,1,0:T(8,128)(2,1)S(1)}, bf16[2,4,128,128]{3,2,1,0:T(8,128)(2,1)S(1)}, u32[]{:S(2)}, u32[]{:S(2)}) collective-permute-start(bf16[2,4,128,128]{3,2,1,0:T(8,128)(2,1)S(1)} %get-tuple-element.50), channel_id=1, source_target_pairs={{0,8},{16,24},{8,0},{24,16},{1,9},{17,25},{9,1},{25,17},{2,10},{18... | collective-permute-start | bytes 786440 | tf_op jit(solution)/shard_map/ppermute | solution.py:20
  59.4 21.2 %collective-permute-start.11 = (bf16[2,4,128,128]{3,2,1,0:T(8,128)(2,1)S(1)}, bf16[2,4,128,128]{3,2,1,0:T(8,128)(2,1)S(1)}, u32[]{:S(2)}, u32[]{:S(2)}) collective-permute-start(bf16[2,4,128,128]{3,2,1,0:T(8,128)(2,1)S(1)} %get-tuple-element.51), channel_id=1, source_target_pairs={{8,16},{16,8},{9,17},{17,9},{10,18},{18,10},{11,19},{19,11},{12,20... | collective-permute-start | bytes 786440 | tf_op jit(solution)/shard_map/ppermute | solution.py:20

commit v3 on v2

--- a/solution.py
+++ b/solution.py
@@ -62,101 +62,99 @@
     return jnp.concatenate(parts, axis=0)
 
 
+def stacked(fields, table):
+    rows = fields[0].shape[0]
+    result = dot(above(*fields) if len(fields) > 1 else fields[0], table)
+    return [result[i * rows : (i + 1) * rows] for i in range(len(fields))]
+
+
+def crossed(fields):
+    return [x.astype(HALF).T for x in fields]
+
+
+def paired(firsts, seconds, side, n):
+    cols = slice(side * n, side * n + n)
+    return [
+        above(beside(x[:n, cols], x[n:, cols]), beside(y[:n, cols], y[n:, cols]))
+        for x, y in zip(firsts, seconds)
+    ]
+
+
 def butterfly(x, n):
-    top, bottom = x[:n] + x[n:], x[:n] - x[n:]
-    return [
-        beside(y[:, :n] + y[:, n:], y[:, :n] - y[:, n:]).astype(HALF) for y in (top, bottom)
-    ]
-
-
-def paired(first, second, side, n):
-    cols = slice(side * n, side * n + n)
-    return above(
-        beside(first[:n, cols], first[n:, cols]), beside(second[:n, cols], second[n:, cols])
+    y = above(x[:n] + x[n:], x[:n] - x[n:])
+    return beside(y[:, :n] + y[:, n:], y[:, :n] - y[:, n:]).astype(HALF)
+
+
+def forward(fields, tab, n):
+    fields = [(butterfly(real, n), butterfly(imag, n)) for real, imag in fields]
+    even = stacked([beside(r[:, :n], i[:, :n]) for r, i in fields], tab[EVEN_T])
+    odd = stacked([beside(r[:, n:], i[:, n:]) for r, i in fields], tab[ODD_T])
+    even, odd = crossed(even), crossed(odd)
+    return (
+        stacked(paired(even, odd, 0, n), tab[EVEN_T]),
+        stacked(paired(even, odd, 1, n), tab[ODD_T]),
     )
 
 
-def forward(real, imag, tab, n):
-    even_real, odd_real = butterfly(real, n)
-    even_imag, odd_imag = butterfly(imag, n)
-    yield
-    even = dot(tab[EVEN], above(even_real, even_imag)).astype(HALF)
-    odd = dot(tab[ODD], above(odd_real, odd_imag)).astype(HALF)
-    result = (
-        dot(paired(even, odd, 0, n), tab[EVEN_T]),
-        dot(paired(even, odd, 1, n), tab[ODD_T]),
+def inverse(even, odd, tab, n):
+    first = crossed(stacked(even, tab[EVEN]))
+    second = crossed(stacked(odd, tab[ODD]))
+    even = stacked(paired(first, second, 0, n), tab[EVEN])
+    odd = stacked(paired(first, second, 1, n), tab[ODD])
+    fields = []
+    for x, y in zip(even, odd):
+        low, high = [above(z[:n] + z[n:], z[:n] - z[n:]) for z in (x + y, x - y)]
+        fields.append((beside(low[:, :n], high[:, :n]), beside(low[:, n:], high[:, n:])))
+    return fields
+
+
+def times(a, b):
+    return a[0] * b[0] - a[1] * b[1], a[0] * b[1] + a[1] * b[0]
+
+
+def times_conjugate(a, b):
+    return a[0] * b[0] + a[1] * b[1], a[0] * b[1] - a[1] * b[0]
+
+
+def slot_group(light, spread, planes, measured, tab, puts, n):
+    def turned(fields, col, product):
+        h = spread(col)
+        pairs = [product(h, (y[:, :n], y[:, n:])) for y in fields]
+        return [beside(real.astype(HALF), imag.astype(HALF)) for real, imag in pairs]
+
+    def pull(fields, levels, col):
+        results = []
+        for y, level in zip(fields, levels):
+            real, imag = y[:, :n], y[:, n:]
+            misfit = real * real + imag * imag - level[:, col : col + n]
+            results.append(beside((misfit * real).astype(HALF), (misfit * imag).astype(HALF)))
+        return results
+
+    even, odd = forward([times(light(), plane(0)) for plane in planes], tab, n)
+    passed = inverse(turned(even, 0, times), turned(odd, n, times), tab, n)
+    even, odd = forward([times(x, plane(2)) for x, plane in zip(passed, planes)], tab, n)
+    levels = crossed(stacked([level() for level in measured], tab[PICK_T]))
+    levels = stacked(levels, tab[PICK_T])
+    back = inverse(pull(even, levels, 0), pull(odd, levels, n), tab, n)
+    for put, x, y in zip(puts, passed, back):
+        put(2, times_conjugate(x, y))
+    even, odd = forward([times_conjugate(plane(2), y) for plane, y in zip(planes, back)], tab, n)
+    start = inverse(
+        turned(even, 0, times_conjugate), turned(odd, n, times_conjugate), tab, n
     )
-    yield
-    return result
-
-
-def inverse(even_cols, odd_cols, tab, n):
-    yield
-
-    def left(rows, table):
-        stacked = above(
-            beside(even_cols[rows, :n], odd_cols[rows, :n]),
-            beside(even_cols[rows, n:], odd_cols[rows, n:]),
-        )
-        return dot(tab[table], stacked).astype(HALF)
-
-    first, second = left(slice(0, n), EVEN_T), left(slice(n, 2 * n), ODD_T)
-    even = dot(paired(first, second, 0, n), tab[EVEN])
-    odd = dot(paired(first, second, 1, n), tab[ODD])
-    yield
-    low, high = [above(y[:n] + y[n:], y[:n] - y[n:]) for y in (even + odd, even - odd)]
-    return beside(low[:, :n], high[:, :n]), beside(low[:, n:], high[:, n:])
-
-
-def slot_steps(light, spread, plane, measured, tab, put, n):
-    def turned(y, col, sign):
-        h_real, h_imag = spread(0, col), sign * spread(1, col)
-        real, imag = y[:, :n], y[:, n:]
-        return beside(
-            (h_real * real - h_imag * imag).astype(HALF),
-            (h_real * imag + h_imag * real).astype(HALF),
-        )
-
-    def pull(y, level):
-        real, imag = y[:, :n], y[:, n:]
-        misfit = real * real + imag * imag - level
-        return beside((misfit * real).astype(HALF), (misfit * imag).astype(HALF))
-
-    p_real, p_imag = light(0), light(1)
-    o_real, o_imag = plane(0), plane(1)
-    even, odd = yield from forward(
-        p_real * o_real - p_imag * o_imag, p_real * o_imag + p_imag * o_real, tab, n
-    )
-    passed_real, passed_imag = yield from inverse(turned(even, 0, 1.0), turned(odd, n, 1.0), tab, n)
-    o_real, o_imag = plane(2), plane(3)
-    even, odd = yield from forward(
-        passed_real * o_real - passed_imag * o_imag,
-        passed_real * o_imag + passed_imag * o_real,
-        tab,
-        n,
-    )
-    level = dot(dot(tab[PICK], measured()).astype(HALF), tab[PICK_T])
-    back_real, back_imag = yield from inverse(
-        pull(even, level[:, :n]), pull(odd, level[:, n:]), tab, n
-    )
-    put(2, passed_real * back_real + passed_imag * back_imag)
-    put(3, passed_real * back_imag - passed_imag * back_real)
-    o_real, o_imag = plane(2), plane(3)
-    even, odd = yield from forward(
-        o_real * back_real + o_imag * back_imag, o_real * back_imag - o_imag * back_real, tab, n
-    )
-    start_real, start_imag = yield from inverse(
-        turned(even, 0, -1.0), turned(odd, n, -1.0), tab, n
-    )
-    p_real, p_imag = light(0), light(1)
-    put(0, p_real * start_real + p_imag * start_imag)
-    put(1, p_real * start_imag - p_imag * start_real)
-
-
-def alternate(generators):
-    waiting = list(generators)
-    while waiting:
-        waiting = [g for g in waiting if next(g, waiting) is not waiting]
+    for put, y in zip(puts, start):
+        put(0, times_conjugate(light(), y))
+
+
+def wave_of(phase):
+    half = phase * 0.5
+    square = half * half
+    sine, cosine = 0.0, 0.0
+    for k in range(6, -1, -1):
+        cosine = cosine * square + (-1.0) ** k / math.factorial(2 * k)
+        sine = sine * square + (-1.0) ** k / math.factorial(2 * k + 1)
+    sine = sine * half
+    return 1.0 - 2.0 * sine * sine, 2.0 * sine * cosine
 
 
 def selected(x, tab):
@@ -217,13 +215,13 @@
 
 
 def slots_kernel(mode, offsets, counts, tab, light, spread, measured, *refs):
-    order, sems = refs[-2:]
+    order = refs[-1]
     slot_count, extent = measured.shape[:2]
     n = extent // 2
     if mode == INSIDE:
         window, total, spread_out = refs[:3]
     else:
-        sources, (window, total), outs = refs[:2], refs[4:6], refs[6:-2]
+        sources, (window, total), outs = refs[:2], refs[4:6], refs[6:-1]
     tile = window.shape[1] - 2 * n
     inner = pl.ds(n, tile)
     row_halo = [pick(ahead("row", turn), 0, n + tile, n) for turn in range(2)]
@@ -238,9 +236,8 @@
             return carry
 
         lax.fori_loop(0, total.shape[1] // 32, clear, 0)
-        phase = spread[...]
-        spread_out[0] = selected(jnp.cos(phase), tab)
-        spread_out[1] = selected(jnp.sin(phase), tab)
+        for k, wave in enumerate(wave_of(spread[...].T)):
+            spread_out[k] = selected(wave, tab)
         spread = spread_out
     else:
         if mode == BESIDE:
@@ -253,7 +250,9 @@
                 for turn in range(2)
                 for d in range(2)
             ]
-        run_copies([(source, window.at[(slice(None), *at)]) for source, at in moves], sems)
+        for source, at in moves:
+            for k in range(4):
+                window[(k, *at)] = source[k]
 
     def inside(at):
         return (at >= 0) & ((at + 2) * n <= tile)
@@ -273,48 +272,61 @@
 
         return lax.fori_loop(0, slot_count, choose, found)
 
+    group = 2 if mode == CORNER else 3
     found = jnp.int32(0)
-    for kind in range(min(mode, OVER) if mode != CORNER else 0):
+    for kind in range(mode if mode != CORNER else 0):
         found = listed(kind, found)
-        odd = found % 2
-
-        @pl.when(odd == 1)
-        def _():
-            order[0] = order[found - 1]
-
-        found = odd
+        left = found % group
+        for i in range(group - 1):
+
+            @pl.when(i < left)
+            def _():
+                order[i] = order[found - left + i]
+
+        found = left
     found = listed(mode, found)
 
-    def steps(at):
-        slot = order[at]
-        row = pl.multiple_of((offsets[0, slot] + 1) * n, n)
-        col = pl.multiple_of((offsets[1, slot] + 1) * n, n)
-        here = (pl.ds(row, extent), pl.ds(col, extent))
-
-        def put(k, value):
-            total[(k, *here)] += value
-
-        return slot_steps(
-            lambda k: light[k],
-            lambda k, at: spread[k, :, at : at + n],
-            lambda k: window[(k, *here)].astype(FULL),
-            lambda: measured[slot],
+    def run(at, size):
+        planes, puts, measures = [], [], []
+        for i in range(size):
+            slot = order[jnp.minimum(at + i, found - 1)]
+            row = pl.multiple_of((offsets[0, slot] + 1) * n, n)
+            col = pl.multiple_of((offsets[1, slot] + 1) * n, n)
+
+            def plane(k, here=(pl.ds(row, extent), pl.ds(col, extent))):
+                return window[(k, *here)].astype(FULL), window[(k + 1, *here)].astype(FULL)
+
+            def put(k, pair, here=(pl.ds(row, extent), pl.ds(col, extent)), i=i):
+                for part in range(2):
+                    value = pair[part]
+                    if mode == OVER and i == size - 1 and size > 1:
+                        value = jnp.where(at + i < found, value, 0.0)
+                    total[(k + part, *here)] += value
+
+            planes.append(plane)
+            puts.append(put)
+            measures.append(lambda slot=slot: measured[slot])
+        slot_group(
+            lambda: (light[0], light[1]),
+            lambda col: (spread[0, :, col : col + n], spread[1, :, col : col + n]),
+            planes,
+            measures,
             tab,
-            put,
+            puts,
             n,
         )
 
-    def both(i, carry):
-        alternate([steps(2 * i), steps(2 * i + 1)])
+    def several(i, carry):
+        run(group * i, group)
         return carry
 
-    lax.fori_loop(0, found // 2, both, 0)
-
+    spare = 1 if mode == OVER else 0
+    lax.fori_loop(0, (found + spare) // group, several, 0)
     if mode in (OVER, CORNER):
 
-        @pl.when(found % 2 == 1)
+        @pl.when(found % group == 1)
         def _():
-            alternate([steps(found - 1)])
+            run(found - 1, 1)
 
     if mode == BESIDE:
         outs[0][...] = total[0, :8, :128]
@@ -351,7 +363,7 @@
         specs += [VMEM]
     else:
         operands += [*sources, window, total]
-        specs += [ANYWHERE, ANYWHERE, VMEM, VMEM]
+        specs += [VMEM] * 4
         aliases = {8: 0, 9: 1}
         outs = [(window.shape, HALF), (total.shape, FULL)] + outs
     return pl.pallas_call(
@@ -359,7 +371,7 @@
         out_shape=[jax.ShapeDtypeStruct(*out) for out in outs],
         in_specs=specs,
         out_specs=[VMEM] * len(outs),
-        scratch_shapes=[pltpu.SMEM((slot_count,), jnp.int32), pltpu.SemaphoreType.DMA((4,))],
+        scratch_shapes=[pltpu.SMEM((slot_count,), jnp.int32)],
         input_output_aliases=aliases,
         compiler_params=pltpu.CompilerParams(vmem_limit_bytes=24 << 20),
         cost_estimate=pl.CostEstimate(

time: 82.5 us -> 82.9 us (level)
  waiting for transfers between devices: 27.2 us -> 29.9 us
  Pallas kernels: 25.7 us -> 23.4 us
    ppermute x14, waiting for transfers between devices: 27.2 us -> 29.9 us  [exchange(): return lax.ppermute(x, axis, pairs + [(j, i) for i, j in pairs])]
    pallas_call x4, Pallas kernels: 21.8 us -> 19.5 us  [run_slots(): pl.pallas_call(functools.partial(slots_kernel, mode), out_shape=[jax.Shap...]
  transfers between devices with their start and end apart: 14 -> 14, of which waited for: 5 -> 6; matrix products, arithmetic and copies ran while one was open for 0% -> 0% of each run, Pallas kernels for 22% -> 20%
where the time goes in v3:
time: 82.9 us; the launch traced here: 81.8 us
  waiting for transfers between devices  29.9 us (36%)
  starting transfers between devices  25.1 us (30%)
  Pallas kernels  23.4 us (28%)
  local copies, waits for them, and re-layouts  2.35 us (3%)
  between operations  1.11 us (1%)
    ppermute x14, waiting for transfers between devices, exchange(): return lax.ppermute(x, axis, pairs + [(j, i) for i, j in pairs])  29.9 us
    ppermute x14, starting transfers between devices, exchange(): return lax.ppermute(x, axis, pairs + [(j, i) for i, j in pairs])  25.1 us
    pallas_call x4, Pallas kernels, run_slots(): pl.pallas_call(functools.partial(slots_kernel, mode), out_shape=[jax.Shap...  19.5 us
    unnamed x12, local copies, waits for them, and re-layouts  2.35 us
  transfers between devices with their start and end apart: 14, of which 6 were waited for; matrix products, arithmetic and copies ran while one was open for 0% of the time, Pallas kernels for 20%

profile of v3, /device:TPU:20, one launch (start us, length us, event | category | flops | bytes accessed | tf_op | source)
XLA Modules:
  0.0 81.8 jit_solution(6296574996543479235)
XLA Ops:
  0.0 0.0 copy-start.1
  0.0 0.0 copy-start
  0.0 0.0 copy-start.3
  0.0 0.0 copy-start.4
  0.0 2.3 %copy-done.4 = f32[4,512,512]{2,1,0:T(8,128)S(1)} copy-done((f32[4,512,512]{2,1,0:T(8,128)S(1)}, f32[4,512,512]{2,1,0:T(8,128)}, u32[]{:S(2)}) %copy-start.4) | copy-done | bytes 4194328
  2.4 0.6 prepare.1
  2.9 0.1 collective-permute-start.2
  3.0 2.4 %collective-permute-start.3 = (bf16[4,512,128]{2,1,0:T(8,128)(2,1)S(1)}, bf16[4,512,128]{2,1,0:T(8,128)(2,1)S(1)}, u32[]{:S(2)}, u32[]{:S(2)}) collective-permute-start(bf16[4,512,128]{2,1,0:T(8,128)(2,1)S(1)} %get-tuple-element.36), channel_id=1, source_target_pairs={{1,2},{3,4},{5,6},{2,1},{4,3},{6,5},{9,10},{11,12},{13,14},{10,9},... | collective-permute-start | bytes 1572872 | tf_op jit(solution)/shard_map/ppermute | solution.py:20
  5.5 1.6 %collective-permute-start = (bf16[4,128,512]{2,1,0:T(8,128)(2,1)S(1)}, bf16[4,128,512]{2,1,0:T(8,128)(2,1)S(1)}, u32[]{:S(2)}, u32[]{:S(2)}) collective-permute-start(bf16[4,128,512]{2,1,0:T(8,128)(2,1)S(1)} %get-tuple-element.33), channel_id=1, source_target_pairs={{0,8},{16,24},{8,0},{24,16},{1,9},{17,25},{9,1},{25,17},{2,10},{18... | collective-permute-start | bytes 1572872 | tf_op jit(solution)/shard_map/ppermute | solution.py:20
  7.0 2.4 %collective-permute-start.1 = (bf16[4,128,512]{2,1,0:T(8,128)(2,1)S(1)}, bf16[4,128,512]{2,1,0:T(8,128)(2,1)S(1)}, u32[]{:S(2)}, u32[]{:S(2)}) collective-permute-start(bf16[4,128,512]{2,1,0:T(8,128)(2,1)S(1)} %get-tuple-element.34), channel_id=1, source_target_pairs={{8,16},{16,8},{9,17},{17,9},{10,18},{18,10},{11,19},{19,11},{12,20... | collective-permute-start | bytes 1572872 | tf_op jit(solution)/shard_map/ppermute | solution.py:20
  10.1 0.0 copy-done.1
  10.1 0.0 copy-done
  10.1 0.0 copy-done.2
  10.1 0.0 copy-done.3
  10.1 0.0 copy-done.5
  10.1 2.5 %shard_map.73 = (f32[4,768,768]{2,1,0:T(8,128)S(1)}, f32[2,256,256]{2,1,0:T(8,128)S(1)}) custom-call(s32[2,12]{1,0:T(2,128)S(1)} %bitcast.1, s32[1]{0:T(128)S(6)} %copy.24.counts, bf16[6,256,256]{2,1,0:T(8,128)(2,1)S(1)} %copy-done.1, f32[2,256,256]{2,1,0:T(8,128)S(1)} %copy-done.2, f32[256,256]{1,0:T(8,128)S(1)} %copy-done.5, ...), custom_call_target="tpu_custom_call" | custom-call | flops 2617245696 | tf_op jit(solution)/shard_map/pallas_call | solution.py:369
  12.6 0.0 collective-permute-done.2.refs_0_
  12.6 0.9 %collective-permute-done.3.refs_1_ = bf16[4,512,128]{2,1,0:T(8,128)(2,1)S(1)} collective-permute-done((bf16[4,512,128]{2,1,0:T(8,128)(2,1)S(1)}, bf16[4,512,128]{2,1,0:T(8,128)(2,1)S(1)}, u32[]{:S(2)}, u32[]{:S(2)}) %collective-permute-start.3) | collective-permute-done | bytes 524320 | tf_op jit(solution)/shard_map/ppermute | solution.py:20
  13.5 5.8 %shard_map.74 = (bf16[4,768,768]{2,1,0:T(8,128)(2,1)S(1)}, f32[4,768,768]{2,1,0:T(8,128)S(1)}, f32[8,128]{1,0:T(8,128)S(1)}) custom-call(s32[2,12]{1,0:T(2,128)S(1)} %bitcast.2, s32[1]{0:T(128)S(6)} %copy.24.counts, bf16[6,256,256]{2,1,0:T(8,128)(2,1)S(1)} %copy-done.1, f32[2,256,256]{2,1,0:T(8,128)S(1)} %copy-done.2, ...), custom_call_target="tpu_custom_call", output_to_operand_aliasing={{0}: (8, {}), {1}: (9, {})} | custom-call | flops 2617245696 | tf_op jit(solution)/shard_map/pallas_call | solution.py:369
  19.3 0.8 collective-permute-done.refs_0_.first
  20.2 11.2 %collective-permute-done.1.refs_1_.second = bf16[4,128,512]{2,1,0:T(8,128)(2,1)S(1)} collective-permute-done((bf16[4,128,512]{2,1,0:T(8,128)(2,1)S(1)}, bf16[4,128,512]{2,1,0:T(8,128)(2,1)S(1)}, u32[]{:S(2)}, u32[]{:S(2)}) %collective-permute-start.1) | collective-permute-done | bytes 524320 | tf_op jit(solution)/shard_map/ppermute | solution.py:20
  31.3 0.1 turn.1
  31.4 0.2 collective-permute-start.6
  31.6 1.9 %collective-permute-start.7 = (bf16[2,4,128,128]{3,2,1,0:T(8,128)(2,1)S(1)}, bf16[2,4,128,128]{3,2,1,0:T(8,128)(2,1)S(1)}, u32[]{:S(2)}, u32[]{:S(2)}) collective-permute-start(bf16[2,4,128,128]{3,2,1,0:T(8,128)(2,1)S(1)} %get-tuple-element.44), channel_id=1, source_target_pairs={{1,2},{3,4},{5,6},{2,1},{4,3},{6,5},{9,10},{11,12},{13,14},{10,9},... | collective-permute-start | bytes 786440 | tf_op jit(solution)/shard_map/ppermute | solution.py:20
  33.5 6.2 %shard_map.75 = (bf16[4,768,768]{2,1,0:T(8,128)(2,1)S(1)}, f32[4,768,768]{2,1,0:T(8,128)S(1)}, bf16[4,128,256]{2,1,0:T(8,128)(2,1)S(1)}, bf16[4,128,256]{2,1,0:T(8,128)(2,1)S(1)}) custom-call(s32[2,12]{1,0:T(2,128)S(1)} %bitcast.3, s32[1]{0:T(128)S(6)} %copy.24.counts, ...), custom_call_target="tpu_custom_call", output_to_operand_aliasing={{0}: (8, {}), {1}: (9, {})} | custom-call | flops 2617245696 | tf_op jit(solution)/shard_map/pallas_call | solution.py:369
  39.7 0.0 collective-permute-done.6.refs_0_
  39.8 0.0 collective-permute-done.7.refs_1_
  39.8 5.0 %shard_map.76 = (bf16[4,768,768]{2,1,0:T(8,128)(2,1)S(1)}, f32[4,768,768]{2,1,0:T(8,128)S(1)}, bf16[2,4,128,128]{3,2,1,0:T(8,128)(2,1)S(1)}, bf16[2,4,128,128]{3...) custom-call(s32[2,12]{1,0:T(2,128)S(1)} %bitcast.4, ...), custom_call_target="tpu_custom_call", output_to_operand_aliasing={{0}: (8, {}), {1}: (9, {})} | custom-call | flops 2617245696 | tf_op jit(solution)/shard_map/pallas_call | solution.py:369
  44.7 0.2 sides.1
  44.9 0.1 collective-permute-start.12
  45.0 0.5 collective-permute-start.8
  45.5 4.5 %collective-permute-start.9 = (bf16[2,4,128,128]{3,2,1,0:T(8,128)(2,1)S(1)}, bf16[2,4,128,128]{3,2,1,0:T(8,128)(2,1)S(1)}, u32[]{:S(2)}, u32[]{:S(2)}) collective-permute-start(bf16[2,4,128,128]{3,2,1,0:T(8,128)(2,1)S(1)} %get-tuple-element.49), channel_id=1, source_target_pairs={{1,2},{3,4},{5,6},{2,1},{4,3},{6,5},{9,10},{11,12},{13,14},{10,9},... | collective-permute-start | bytes 786440 | tf_op jit(solution)/shard_map/ppermute | solution.py:20
  49.9 1.9 %collective-permute-start.13 = (bf16[4,512,128]{2,1,0:T(8,128)(2,1)S(1)}, bf16[4,512,128]{2,1,0:T(8,128)(2,1)S(1)}, u32[]{:S(2)}, u32[]{:S(2)}) collective-permute-start(bf16[4,512,128]{2,1,0:T(8,128)(2,1)S(1)} %get-tuple-element.54), channel_id=1, source_target_pairs={{1,2},{3,4},{5,6},{2,1},{4,3},{6,5},{9,10},{11,12},{13,14},{10,9},... | collective-permute-start | bytes 1572872 | tf_op jit(solution)/shard_map/ppermute | solution.py:20
  51.9 0.1 collective-permute-start.4
  51.9 0.0 collective-permute-done.8.first
  51.9 6.8 %collective-permute-start.5 = (bf16[4,128,256]{2,1,0:T(8,128)(2,1)S(1)}, bf16[4,128,256]{2,1,0:T(8,128)(2,1)S(1)}, u32[]{:S(2)}, u32[]{:S(2)}) collective-permute-start(bf16[4,128,256]{2,1,0:T(8,128)(2,1)S(1)} %get-tuple-element.41), channel_id=1, source_target_pairs={{8,16},{16,8},{9,17},{17,9},{10,18},{18,10},{11,19},{19,11},{12,20... | collective-permute-start | bytes 786440 | tf_op jit(solution)/shard_map/ppermute | solution.py:20
  58.8 0.0 collective-permute-done.9.second
  58.8 0.1 join.1
  58.9 0.1 collective-permute-start.10
  59.0 0.0 collective-permute-done.12.first
  59.0 2.6 %collective-permute-start.11 = (bf16[2,4,128,128]{3,2,1,0:T(8,128)(2,1)S(1)}, bf16[2,4,128,128]{3,2,1,0:T(8,128)(2,1)S(1)}, u32[]{:S(2)}, u32[]{:S(2)}) collective-permute-start(bf16[2,4,128,128]{3,2,1,0:T(8,128)(2,1)S(1)} %get-tuple-element.51), channel_id=1, source_target_pairs={{8,16},{16,8},{9,17},{17,9},{10,18},{18,10},{11,19},{19,11},{12,20... | collective-permute-start | bytes 786440 | tf_op jit(solution)/shard_map/ppermute | solution.py:20
  61.6 0.0 collective-permute-done.13.second
  61.7 1.6 %settle.1 = (f32[4,768,768]{2,1,0:T(8,128)S(1)}, f32[4,512,512]{2,1,0:T(8,128)}) custom-call(bf16[4,512,128]{2,1,0:T(8,128)(2,1)S(1)} %collective-permute-done.12.first, bf16[4,512,128]{2,1,0:T(8,128)(2,1)S(1)} %collective-permute-done.13.second, f32[4,768,768]{2,1,0:T(8,128)S(1)} %get-tuple-element.52.total.total_in), custom_call_target="tpu_custom_call", output_to_operand_aliasing={{0}: (2, {})} | custom-call | tf_op jit(solution)/shard_map/settle/pallas_call | solution.py:455
  63.3 0.0 collective-permute-done.4.core_0
  63.3 6.3 %collective-permute-done.5.core_1 = bf16[4,128,256]{2,1,0:T(8,128)(2,1)S(1)} collective-permute-done((bf16[4,128,256]{2,1,0:T(8,128)(2,1)S(1)}, bf16[4,128,256]{2,1,0:T(8,128)(2,1)S(1)}, u32[]{:S(2)}, u32[]{:S(2)}) %collective-permute-start.5) | collective-permute-done | bytes 262176 | tf_op jit(solution)/shard_map/ppermute | solution.py:20
  69.6 1.5 %collective-permute-done.10.edge_0 = bf16[2,4,128,128]{3,2,1,0:T(8,128)(2,1)S(1)} collective-permute-done((bf16[2,4,128,128]{3,2,1,0:T(8,128)(2,1)S(1)}, bf16[2,4,128,128]{3,2,1,0:T(8,128)(2,1)S(1)}, u32[]{:S(2)}, u32[]{:S(2)}) %collective-permute-start.10) | collective-permute-done | bytes 262176 | tf_op jit(solution)/shard_map/ppermute | solution.py:20
  71.1 9.2 %collective-permute-done.11.edge_1 = bf16[2,4,128,128]{3,2,1,0:T(8,128)(2,1)S(1)} collective-permute-done((bf16[2,4,128,128]{3,2,1,0:T(8,128)(2,1)S(1)}, bf16[2,4,128,128]{3,2,1,0:T(8,128)(2,1)S(1)}, u32[]{:S(2)}, u32[]{:S(2)}) %collective-permute-start.11) | collective-permute-done | bytes 262176 | tf_op jit(solution)/shard_map/ppermute | solution.py:20
  80.2 1.4 %finish.1 = f32[4,512,512]{2,1,0:T(8,128)} custom-call(bf16[4,128,256]{2,1,0:T(8,128)(2,1)S(1)} %collective-permute-done.4.core_0, bf16[4,128,256]{2,1,0:T(8,128)(2,1)S(1)} %collective-permute-done.5.core_1, bf16[2,4,128,128]{3,2,1,0:T(8,128)(2,1)S(1)} %collective-permute-done.10.edge_0, ...), custom_call_target="tpu_custom_call", output_to_operand_aliasing={{}: (5, {})} | custom-call | tf_op jit(solution)/shard_map/finish/pallas_call | solution.py:498
  (2 shorter events, 0.0 us)
Async XLA Ops:
  0.0 10.1 %copy-start.1 = (bf16[6,256,256]{2,1,0:T(8,128)(2,1)S(1)}, bf16[6,256,256]{2,1,0:T(8,128)(2,1)}, u32[]{:S(2)}) copy-start(bf16[6,256,256]{2,1,0:T(8,128)(2,1)} %constant.2.clone.tab) | copy-start | bytes 2359300
  0.0 10.1 %copy-start = (bf16[12,256,256]{2,1,0:T(8,128)(2,1)S(1)}, bf16[12,256,256]{2,1,0:T(8,128)(2,1)}, u32[]{:S(2)}) copy-start(bf16[12,256,256]{2,1,0:T(8,128)(2,1)} %measured.7) | copy-start | bytes 4718596
  0.0 10.1 %copy-start.2 = (f32[2,256,256]{2,1,0:T(8,128)S(1)}, f32[2,256,256]{2,1,0:T(8,128)}, u32[]{:S(2)}) copy-start(f32[2,256,256]{2,1,0:T(8,128)} %light.7) | copy-start | bytes 1572868
  0.0 10.1 %copy-start.3 = (s32[12,2]{0,1:T(2,128)S(1)}, s32[12,2]{0,1:T(2,128)}, u32[]{:S(2)}) copy-start(s32[12,2]{0,1:T(2,128)} %param.11) | copy-start | bytes 292
  0.0 2.3 %copy-start.4 = (f32[4,512,512]{2,1,0:T(8,128)S(1)}, f32[4,512,512]{2,1,0:T(8,128)}, u32[]{:S(2)}) copy-start(f32[4,512,512]{2,1,0:T(8,128)} %objects.1) | copy-start | bytes 12582916
  2.4 7.7 %copy-start.5 = (f32[256,256]{1,0:T(8,128)S(1)}, f32[256,256]{1,0:T(8,128)}, u32[]{:S(2)}) copy-start(f32[256,256]{1,0:T(8,128)} %spread.1) | copy-start | bytes 786436
  2.9 9.7 %collective-permute-start.2 = (bf16[4,512,128]{2,1,0:T(8,128)(2,1)S(1)}, bf16[4,512,128]{2,1,0:T(8,128)(2,1)S(1)}, u32[]{:S(2)}, u32[]{:S(2)}) collective-permute-start(bf16[4,512,128]{2,1,0:T(8,128)(2,1)S(1)} %get-tuple-element.35), channel_id=1, source_target_pairs={{0,1},{2,3},{4,5},{6,7},{1,0},{3,2},{5,4},{7,6},{8,9},{10,11},{12,... | collective-permute-start | bytes 1572872 | tf_op jit(solution)/shard_map/ppermute | solution.py:20
  3.0 10.5 %collective-permute-start.3 = (bf16[4,512,128]{2,1,0:T(8,128)(2,1)S(1)}, bf16[4,512,128]{2,1,0:T(8,128)(2,1)S(1)}, u32[]{:S(2)}, u32[]{:S(2)}) collective-permute-start(bf16[4,512,128]{2,1,0:T(8,128)(2,1)S(1)} %get-tuple-element.36), channel_id=1, source_target_pairs={{1,2},{3,4},{5,6},{2,1},{4,3},{6,5},{9,10},{11,12},{13,14},{10,9},... | collective-permute-start | bytes 1572872 | tf_op jit(solution)/shard_map/ppermute | solution.py:20
  5.5 14.7 %collective-permute-start = (bf16[4,128,512]{2,1,0:T(8,128)(2,1)S(1)}, bf16[4,128,512]{2,1,0:T(8,128)(2,1)S(1)}, u32[]{:S(2)}, u32[]{:S(2)}) collective-permute-start(bf16[4,128,512]{2,1,0:T(8,128)(2,1)S(1)} %get-tuple-element.33), channel_id=1, source_target_pairs={{0,8},{16,24},{8,0},{24,16},{1,9},{17,25},{9,1},{25,17},{2,10},{18... | collective-permute-start | bytes 1572872 | tf_op jit(solution)/shard_map/ppermute | solution.py:20
  7.0 24.3 %collective-permute-start.1 = (bf16[4,128,512]{2,1,0:T(8,128)(2,1)S(1)}, bf16[4,128,512]{2,1,0:T(8,128)(2,1)S(1)}, u32[]{:S(2)}, u32[]{:S(2)}) collective-permute-start(bf16[4,128,512]{2,1,0:T(8,128)(2,1)S(1)} %get-tuple-element.34), channel_id=1, source_target_pairs={{8,16},{16,8},{9,17},{17,9},{10,18},{18,10},{11,19},{19,11},{12,20... | collective-permute-start | bytes 1572872 | tf_op jit(solution)/shard_map/ppermute | solution.py:20
  31.4 8.3 %collective-permute-start.6 = (bf16[2,4,128,128]{3,2,1,0:T(8,128)(2,1)S(1)}, bf16[2,4,128,128]{3,2,1,0:T(8,128)(2,1)S(1)}, u32[]{:S(2)}, u32[]{:S(2)}) collective-permute-start(bf16[2,4,128,128]{3,2,1,0:T(8,128)(2,1)S(1)} %get-tuple-element.43), channel_id=1, source_target_pairs={{0,1},{2,3},{4,5},{6,7},{1,0},{3,2},{5,4},{7,6},{8,9},{10,11},{12,... | collective-permute-start | bytes 786440 | tf_op jit(solution)/shard_map/ppermute | solution.py:20
  31.6 8.1 %collective-permute-start.7 = (bf16[2,4,128,128]{3,2,1,0:T(8,128)(2,1)S(1)}, bf16[2,4,128,128]{3,2,1,0:T(8,128)(2,1)S(1)}, u32[]{:S(2)}, u32[]{:S(2)}) collective-permute-start(bf16[2,4,128,128]{3,2,1,0:T(8,128)(2,1)S(1)} %get-tuple-element.44), channel_id=1, source_target_pairs={{1,2},{3,4},{5,6},{2,1},{4,3},{6,5},{9,10},{11,12},{13,14},{10,9},... | collective-permute-start | bytes 786440 | tf_op jit(solution)/shard_map/ppermute | solution.py:20
  44.9 14.1 %collective-permute-start.12 = (bf16[4,512,128]{2,1,0:T(8,128)(2,1)S(1)}, bf16[4,512,128]{2,1,0:T(8,128)(2,1)S(1)}, u32[]{:S(2)}, u32[]{:S(2)}) collective-permute-start(bf16[4,512,128]{2,1,0:T(8,128)(2,1)S(1)} %get-tuple-element.53), channel_id=1, source_target_pairs={{0,1},{2,3},{4,5},{6,7},{1,0},{3,2},{5,4},{7,6},{8,9},{10,11},{12,... | collective-permute-start | bytes 1572872 | tf_op jit(solution)/shard_map/ppermute | solution.py:20
  45.0 7.0 %collective-permute-start.8 = (bf16[2,4,128,128]{3,2,1,0:T(8,128)(2,1)S(1)}, bf16[2,4,128,128]{3,2,1,0:T(8,128)(2,1)S(1)}, u32[]{:S(2)}, u32[]{:S(2)}) collective-permute-start(bf16[2,4,128,128]{3,2,1,0:T(8,128)(2,1)S(1)} %get-tuple-element.48), channel_id=1, source_target_pairs={{0,1},{2,3},{4,5},{6,7},{1,0},{3,2},{5,4},{7,6},{8,9},{10,11},{12,... | collective-permute-start | bytes 786440 | tf_op jit(solution)/shard_map/ppermute | solution.py:20
  45.5 13.3 %collective-permute-start.9 = (bf16[2,4,128,128]{3,2,1,0:T(8,128)(2,1)S(1)}, bf16[2,4,128,128]{3,2,1,0:T(8,128)(2,1)S(1)}, u32[]{:S(2)}, u32[]{:S(2)}) collective-permute-start(bf16[2,4,128,128]{3,2,1,0:T(8,128)(2,1)S(1)} %get-tuple-element.49), channel_id=1, source_target_pairs={{1,2},{3,4},{5,6},{2,1},{4,3},{6,5},{9,10},{11,12},{13,14},{10,9},... | collective-permute-start | bytes 786440 | tf_op jit(solution)/shard_map/ppermute | solution.py:20
  49.9 11.7 %collective-permute-start.13 = (bf16[4,512,128]{2,1,0:T(8,128)(2,1)S(1)}, bf16[4,512,128]{2,1,0:T(8,128)(2,1)S(1)}, u32[]{:S(2)}, u32[]{:S(2)}) collective-permute-start(bf16[4,512,128]{2,1,0:T(8,128)(2,1)S(1)} %get-tuple-element.54), channel_id=1, source_target_pairs={{1,2},{3,4},{5,6},{2,1},{4,3},{6,5},{9,10},{11,12},{13,14},{10,9},... | collective-permute-start | bytes 1572872 | tf_op jit(solution)/shard_map/ppermute | solution.py:20
  51.9 11.4 %collective-permute-start.4 = (bf16[4,128,256]{2,1,0:T(8,128)(2,1)S(1)}, bf16[4,128,256]{2,1,0:T(8,128)(2,1)S(1)}, u32[]{:S(2)}, u32[]{:S(2)}) collective-permute-start(bf16[4,128,256]{2,1,0:T(8,128)(2,1)S(1)} %get-tuple-element.40), channel_id=1, source_target_pairs={{0,8},{16,24},{8,0},{24,16},{1,9},{17,25},{9,1},{25,17},{2,10},{18... | collective-permute-start | bytes 786440 | tf_op jit(solution)/shard_map/ppermute | solution.py:20
  51.9 17.7 %collective-permute-start.5 = (bf16[4,128,256]{2,1,0:T(8,128)(2,1)S(1)}, bf16[4,128,256]{2,1,0:T(8,128)(2,1)S(1)}, u32[]{:S(2)}, u32[]{:S(2)}) collective-permute-start(bf16[4,128,256]{2,1,0:T(8,128)(2,1)S(1)} %get-tuple-element.41), channel_id=1, source_target_pairs={{8,16},{16,8},{9,17},{17,9},{10,18},{18,10},{11,19},{19,11},{12,20... | collective-permute-start | bytes 786440 | tf_op jit(solution)/shard_map/ppermute | solution.py:20
  58.9 12.2 %collective-permute-start.10 = (bf16[2,4,128,128]{3,2,1,0:T(8,128)(2,1)S(1)}, bf16[2,4,128,128]{3,2,1,0:T(8,128)(2,1)S(1)}, u32[]{:S(2)}, u32[]{:S(2)}) collective-permute-start(bf16[2,4,128,128]{3,2,1,0:T(8,128)(2,1)S(1)} %get-tuple-element.50), channel_id=1, source_target_pairs={{0,8},{16,24},{8,0},{24,16},{1,9},{17,25},{9,1},{25,17},{2,10},{18... | collective-permute-start | bytes 786440 | tf_op jit(solution)/shard_map/ppermute | solution.py:20
  59.0 21.2 %collective-permute-start.11 = (bf16[2,4,128,128]{3,2,1,0:T(8,128)(2,1)S(1)}, bf16[2,4,128,128]{3,2,1,0:T(8,128)(2,1)S(1)}, u32[]{:S(2)}, u32[]{:S(2)}) collective-permute-start(bf16[2,4,128,128]{3,2,1,0:T(8,128)(2,1)S(1)} %get-tuple-element.51), channel_id=1, source_target_pairs={{8,16},{16,8},{9,17},{17,9},{10,18},{18,10},{11,19},{19,11},{12,20... | collective-permute-start | bytes 786440 | tf_op jit(solution)/shard_map/ppermute | solution.py:20

commit v4 on v3

--- a/solution.py
+++ b/solution.py
@@ -221,7 +221,8 @@
     if mode == INSIDE:
         window, total, spread_out = refs[:3]
     else:
-        sources, (window, total), outs = refs[:2], refs[4:6], refs[6:-1]
+        m = {BESIDE: 3, OVER: 1, CORNER: 2}[mode]
+        sources, (window, total), outs = refs[:m], refs[m + 2 : m + 4], refs[m + 4 : -1]
     tile = window.shape[1] - 2 * n
     inner = pl.ds(n, tile)
     row_halo = [pick(ahead("row", turn), 0, n + tile, n) for turn in range(2)]
@@ -242,8 +243,9 @@
     else:
         if mode == BESIDE:
             moves = [(sources[turn], (inner, col_halo[turn])) for turn in range(2)]
+            moves += [(sources[2], (row_halo[0], inner))]
         elif mode == OVER:
-            moves = [(sources[turn], (row_halo[turn], inner)) for turn in range(2)]
+            moves = [(sources[0], (row_halo[1], inner))]
         else:
             moves = [
                 (sources[turn].at[d], (row_halo[d], col_halo[turn]))
@@ -258,31 +260,29 @@
         return (at >= 0) & ((at + 2) * n <= tile)
 
     def listed(kind, found):
-        def choose(j, found):
-            row_in, col_in = inside(offsets[0, j]), inside(offsets[1, j])
+        for j in range(slot_count):
+            row, col = offsets[0, j], offsets[1, j]
+            early = inside(row) | ((row < 0) == (ahead("row", 0) == 1))
             wanted = j < counts[0]
-            wanted &= row_in if kind in (INSIDE, BESIDE) else jnp.logical_not(row_in)
-            wanted &= col_in if kind in (INSIDE, OVER) else jnp.logical_not(col_in)
-
-            @pl.when(wanted)
-            def _():
-                order[found] = j
-
-            return found + wanted.astype(jnp.int32)
-
-        return lax.fori_loop(0, slot_count, choose, found)
-
-    group = 2 if mode == CORNER else 3
+            if kind == INSIDE:
+                wanted &= inside(row) & inside(col)
+            elif kind == BESIDE:
+                wanted &= (inside(row) != inside(col)) & early
+            elif kind == OVER:
+                wanted &= jnp.logical_not(early) & inside(col)
+            else:
+                wanted &= jnp.logical_not(inside(row) | inside(col))
+            order[found] = j
+            found = found + wanted.astype(jnp.int32)
+        return found
+
+    group = 3 if mode in (INSIDE, BESIDE) else 2
     found = jnp.int32(0)
-    for kind in range(mode if mode != CORNER else 0):
-        found = listed(kind, found)
+    if mode == BESIDE:
+        found = listed(INSIDE, found)
         left = found % group
         for i in range(group - 1):
-
-            @pl.when(i < left)
-            def _():
-                order[i] = order[found - left + i]
-
+            order[i] = order[jnp.maximum(found - left + i, 0)]
         found = left
     found = listed(mode, found)
 
@@ -299,7 +299,7 @@
             def put(k, pair, here=(pl.ds(row, extent), pl.ds(col, extent)), i=i):
                 for part in range(2):
                     value = pair[part]
-                    if mode == OVER and i == size - 1 and size > 1:
+                    if mode == BESIDE and i == size - 1 and size > 1:
                         value = jnp.where(at + i < found, value, 0.0)
                     total[(k + part, *here)] += value
 
@@ -320,20 +320,18 @@
         run(group * i, group)
         return carry
 
-    spare = 1 if mode == OVER else 0
+    spare = 1 if mode == BESIDE else 0
     lax.fori_loop(0, (found + spare) // group, several, 0)
-    if mode in (OVER, CORNER):
+    if mode != INSIDE:
 
         @pl.when(found % group == 1)
         def _():
             run(found - 1, 1)
 
-    if mode == BESIDE:
-        outs[0][...] = total[0, :8, :128]
-    if mode == OVER:
-        for turn in range(2):
-            for k in range(4):
-                outs[turn][k] = total[k, row_halo[turn], pl.ds(2 * n, tile - 2 * n)].astype(HALF)
+    if mode in (BESIDE, OVER):
+        rows = row_halo[0 if mode == BESIDE else 1]
+        for k in range(4):
+            outs[0][k] = total[k, rows, pl.ds(2 * n, tile - 2 * n)].astype(HALF)
     if mode == CORNER:
         ends, edge = outs[:2], outs[2]
         for turn in range(2):
@@ -351,8 +349,8 @@
     square = (4, n, n)
     outs = {
         INSIDE: [(window.shape, FULL), ((2, extent, extent), FULL)],
-        BESIDE: [((8, 128), FULL)],
-        OVER: [((4, n, tile - 2 * n), HALF)] * 2,
+        BESIDE: [((4, n, tile - 2 * n), HALF)],
+        OVER: [((4, n, tile - 2 * n), HALF)],
         CORNER: [((2, *square), HALF)] * 2 + [((2, 2, *square), FULL)],
     }[mode]
     operands = [*scalars, *constants]
@@ -363,15 +361,15 @@
         specs += [VMEM]
     else:
         operands += [*sources, window, total]
-        specs += [VMEM] * 4
-        aliases = {8: 0, 9: 1}
+        specs += [VMEM] * (len(sources) + 2)
+        aliases = {6 + len(sources): 0, 7 + len(sources): 1}
         outs = [(window.shape, HALF), (total.shape, FULL)] + outs
     return pl.pallas_call(
         functools.partial(slots_kernel, mode),
         out_shape=[jax.ShapeDtypeStruct(*out) for out in outs],
         in_specs=specs,
         out_specs=[VMEM] * len(outs),
-        scratch_shapes=[pltpu.SMEM((slot_count,), jnp.int32)],
+        scratch_shapes=[pltpu.SMEM((slot_count + 3,), jnp.int32)],
         input_output_aliases=aliases,
         compiler_params=pltpu.CompilerParams(vmem_limit_bytes=24 << 20),
         cost_estimate=pl.CostEstimate(
@@ -523,10 +521,11 @@
     beside = both(strips[2:], "col")
     constants = [jnp.asarray(half_tables(extent)), illumination, propagator_phase, intensity]
     total, constants[2] = run_slots(INSIDE, scalars, constants, window)
-    window, total, token = run_slots(BESIDE, scalars, constants, window, total, beside)
-    corner = both(turn_ends(*over, token), "col")
-    window, total, *cores = run_slots(OVER, scalars, constants, window, total, over)
-    cores = both(cores, "row")
+    window, total, core = run_slots(BESIDE, scalars, constants, window, total, (*beside, over[0]))
+    cores = [exchange(core, "row", 0)]
+    corner = both(turn_ends(*over, core), "col")
+    window, total, core = run_slots(OVER, scalars, constants, window, total, over[1:])
+    cores += [exchange(core, "row", 1)]
     _, total, *ends, edge = run_slots(CORNER, scalars, constants, window, total, corner)
     ends = both(ends, "col")
     outer = both(sides(total, n), "col")

time: 82.9 us -> 82 us (0.989)
  waiting for transfers between devices: 29.9 us -> 29 us
    ppermute x14, waiting for transfers between devices: 29.9 us -> 29 us  [exchange(): return lax.ppermute(x, axis, pairs + [(j, i) for i, j in pairs])]
  transfers between devices with their start and end apart: 14 -> 14, of which waited for: 6 -> 7; matrix products, arithmetic and copies ran while one was open for 0% -> 0% of each run, Pallas kernels for 20% -> 20%
where the time goes in v4:
time: 82 us; the launch traced here: 81.7 us
  waiting for transfers between devices  29 us (35%)
  starting transfers between devices  25.6 us (31%)
  Pallas kernels  23.7 us (29%)
  local copies, waits for them, and re-layouts  2.35 us (3%)
  between operations  1.09 us (1%)
    ppermute x14, waiting for transfers between devices, exchange(): return lax.ppermute(x, axis, pairs + [(j, i) for i, j in pairs])  29 us
    ppermute x14, starting transfers between devices, exchange(): return lax.ppermute(x, axis, pairs + [(j, i) for i, j in pairs])  25.6 us
    pallas_call x4, Pallas kernels, run_slots(): pl.pallas_call(functools.partial(slots_kernel, mode), out_shape=[jax.Shap...  19.8 us
    unnamed x12, local copies, waits for them, and re-layouts  2.35 us
  transfers between devices with their start and end apart: 14, of which 7 were waited for; matrix products, arithmetic and copies ran while one was open for 0% of the time, Pallas kernels for 20%

profile of v4, /device:TPU:20, one launch (start us, length us, event | category | flops | bytes accessed | tf_op | source)
XLA Modules:
  0.0 81.7 jit_solution(6298874546062588596)
XLA Ops:
  0.0 0.0 copy-start.1
  0.0 0.0 copy-start
  0.0 0.0 copy-start.3
  0.0 0.0 copy-start.4
  0.0 2.3 %copy-done.4 = f32[4,512,512]{2,1,0:T(8,128)S(1)} copy-done((f32[4,512,512]{2,1,0:T(8,128)S(1)}, f32[4,512,512]{2,1,0:T(8,128)}, u32[]{:S(2)}) %copy-start.4) | copy-done | bytes 4194328
  2.4 0.6 prepare.1
  2.9 0.1 collective-permute-start
  3.0 2.4 %collective-permute-start.1 = (bf16[4,512,128]{2,1,0:T(8,128)(2,1)S(1)}, bf16[4,512,128]{2,1,0:T(8,128)(2,1)S(1)}, u32[]{:S(2)}, u32[]{:S(2)}) collective-permute-start(bf16[4,512,128]{2,1,0:T(8,128)(2,1)S(1)} %get-tuple-element.33), channel_id=1, source_target_pairs={{1,2},{3,4},{5,6},{2,1},{4,3},{6,5},{9,10},{11,12},{13,14},{10,9},... | collective-permute-start | bytes 1572872 | tf_op jit(solution)/shard_map/ppermute | solution.py:20
  5.5 1.6 %collective-permute-start.2 = (bf16[4,128,512]{2,1,0:T(8,128)(2,1)S(1)}, bf16[4,128,512]{2,1,0:T(8,128)(2,1)S(1)}, u32[]{:S(2)}, u32[]{:S(2)}) collective-permute-start(bf16[4,128,512]{2,1,0:T(8,128)(2,1)S(1)} %get-tuple-element.34), channel_id=1, source_target_pairs={{0,8},{16,24},{8,0},{24,16},{1,9},{17,25},{9,1},{25,17},{2,10},{18... | collective-permute-start | bytes 1572872 | tf_op jit(solution)/shard_map/ppermute | solution.py:20
  7.0 2.4 %collective-permute-start.4 = (bf16[4,128,512]{2,1,0:T(8,128)(2,1)S(1)}, bf16[4,128,512]{2,1,0:T(8,128)(2,1)S(1)}, u32[]{:S(2)}, u32[]{:S(2)}) collective-permute-start(bf16[4,128,512]{2,1,0:T(8,128)(2,1)S(1)} %get-tuple-element.37), channel_id=1, source_target_pairs={{8,16},{16,8},{9,17},{17,9},{10,18},{18,10},{11,19},{19,11},{12,20... | collective-permute-start | bytes 1572872 | tf_op jit(solution)/shard_map/ppermute | solution.py:20
  10.1 0.0 copy-done.1
  10.1 0.0 copy-done
  10.1 0.0 copy-done.2
  10.1 0.0 copy-done.3
  10.1 0.0 copy-done.5
  10.1 2.3 %shard_map.73 = (f32[4,768,768]{2,1,0:T(8,128)S(1)}, f32[2,256,256]{2,1,0:T(8,128)S(1)}) custom-call(s32[2,12]{1,0:T(2,128)S(1)} %bitcast.1, s32[1]{0:T(128)S(6)} %copy.24.counts, bf16[6,256,256]{2,1,0:T(8,128)(2,1)S(1)} %copy-done.1, f32[2,256,256]{2,1,0:T(8,128)S(1)} %copy-done.2, f32[256,256]{1,0:T(8,128)S(1)} %copy-done.5, ...), custom_call_target="tpu_custom_call" | custom-call | flops 2617245696 | tf_op jit(solution)/shard_map/pallas_call | solution.py:367
  12.4 0.0 collective-permute-done.refs_0_
  12.4 1.1 %collective-permute-done.1.refs_1_ = bf16[4,512,128]{2,1,0:T(8,128)(2,1)S(1)} collective-permute-done((bf16[4,512,128]{2,1,0:T(8,128)(2,1)S(1)}, bf16[4,512,128]{2,1,0:T(8,128)(2,1)S(1)}, u32[]{:S(2)}, u32[]{:S(2)}) %collective-permute-start.1) | collective-permute-done | bytes 524320 | tf_op jit(solution)/shard_map/ppermute | solution.py:20
  13.5 6.6 %collective-permute-done.2.refs_2_.first = bf16[4,128,512]{2,1,0:T(8,128)(2,1)S(1)} collective-permute-done((bf16[4,128,512]{2,1,0:T(8,128)(2,1)S(1)}, bf16[4,128,512]{2,1,0:T(8,128)(2,1)S(1)}, u32[]{:S(2)}, u32[]{:S(2)}) %collective-permute-start.2) | collective-permute-done | bytes 524320 | tf_op jit(solution)/shard_map/ppermute | solution.py:20
  20.2 8.9 %shard_map.74 = (bf16[4,768,768]{2,1,0:T(8,128)(2,1)S(1)}, f32[4,768,768]{2,1,0:T(8,128)S(1)}, bf16[4,128,256]{2,1,0:T(8,128)(2,1)S(1)}) custom-call(s32[2,12]{1,0:T(2,128)S(1)} %bitcast.2, s32[1]{0:T(128)S(6)} %copy.24.counts, bf16[6,256,256]{2,1,0:T(8,128)(2,1)S(1)} %copy-done.1, ...), custom_call_target="tpu_custom_call", output_to_operand_aliasing={{0}: (9, {}), {1}: (10, {})} | custom-call | flops 2617245696 | tf_op jit(solution)/shard_map/pallas_call | solution.py:367
  29.1 2.3 %collective-permute-done.4.refs_0_.second = bf16[4,128,512]{2,1,0:T(8,128)(2,1)S(1)} collective-permute-done((bf16[4,128,512]{2,1,0:T(8,128)(2,1)S(1)}, bf16[4,128,512]{2,1,0:T(8,128)(2,1)S(1)}, u32[]{:S(2)}, u32[]{:S(2)}) %collective-permute-start.4) | collective-permute-done | bytes 524320 | tf_op jit(solution)/shard_map/ppermute | solution.py:20
  31.3 0.1 turn.1
  31.4 0.2 collective-permute-start.6
  31.6 1.9 %collective-permute-start.7 = (bf16[2,4,128,128]{3,2,1,0:T(8,128)(2,1)S(1)}, bf16[2,4,128,128]{3,2,1,0:T(8,128)(2,1)S(1)}, u32[]{:S(2)}, u32[]{:S(2)}) collective-permute-start(bf16[2,4,128,128]{3,2,1,0:T(8,128)(2,1)S(1)} %get-tuple-element.42), channel_id=1, source_target_pairs={{1,2},{3,4},{5,6},{2,1},{4,3},{6,5},{9,10},{11,12},{13,14},{10,9},... | collective-permute-start | bytes 786440 | tf_op jit(solution)/shard_map/ppermute | solution.py:20
  33.5 3.8 %shard_map.75 = (bf16[4,768,768]{2,1,0:T(8,128)(2,1)S(1)}, f32[4,768,768]{2,1,0:T(8,128)S(1)}, bf16[4,128,256]{2,1,0:T(8,128)(2,1)S(1)}) custom-call(s32[2,12]{1,0:T(2,128)S(1)} %bitcast.3, s32[1]{0:T(128)S(6)} %copy.24.counts, bf16[6,256,256]{2,1,0:T(8,128)(2,1)S(1)} %copy-done.1, ...), custom_call_target="tpu_custom_call", output_to_operand_aliasing={{0}: (7, {}), {1}: (8, {})} | custom-call | flops 2617245696 | tf_op jit(solution)/shard_map/pallas_call | solution.py:367
  37.3 0.0 collective-permute-done.6.refs_0_
  37.3 2.0 %collective-permute-done.7.refs_1_ = bf16[2,4,128,128]{3,2,1,0:T(8,128)(2,1)S(1)} collective-permute-done((bf16[2,4,128,128]{3,2,1,0:T(8,128)(2,1)S(1)}, bf16[2,4,128,128]{3,2,1,0:T(8,128)(2,1)S(1)}, u32[]{:S(2)}, u32[]{:S(2)}) %collective-permute-start.7) | collective-permute-done | bytes 262176 | tf_op jit(solution)/shard_map/ppermute | solution.py:20
  39.3 4.8 %shard_map.76 = (bf16[4,768,768]{2,1,0:T(8,128)(2,1)S(1)}, f32[4,768,768]{2,1,0:T(8,128)S(1)}, bf16[2,4,128,128]{3,2,1,0:T(8,128)(2,1)S(1)}, bf16[2,4,128,128]{3...) custom-call(s32[2,12]{1,0:T(2,128)S(1)} %bitcast.4, ...), custom_call_target="tpu_custom_call", output_to_operand_aliasing={{0}: (8, {}), {1}: (9, {})} | custom-call | flops 2617245696 | tf_op jit(solution)/shard_map/pallas_call | solution.py:367
  44.1 0.2 sides.1
  44.3 0.1 collective-permute-start.12
  44.4 0.5 collective-permute-start.8
  44.9 1.9 %collective-permute-start.9 = (bf16[2,4,128,128]{3,2,1,0:T(8,128)(2,1)S(1)}, bf16[2,4,128,128]{3,2,1,0:T(8,128)(2,1)S(1)}, u32[]{:S(2)}, u32[]{:S(2)}) collective-permute-start(bf16[2,4,128,128]{3,2,1,0:T(8,128)(2,1)S(1)} %get-tuple-element.47), channel_id=1, source_target_pairs={{1,2},{3,4},{5,6},{2,1},{4,3},{6,5},{9,10},{11,12},{13,14},{10,9},... | collective-permute-start | bytes 786440 | tf_op jit(solution)/shard_map/ppermute | solution.py:20
  46.8 3.6 %collective-permute-start.13 = (bf16[4,512,128]{2,1,0:T(8,128)(2,1)S(1)}, bf16[4,512,128]{2,1,0:T(8,128)(2,1)S(1)}, u32[]{:S(2)}, u32[]{:S(2)}) collective-permute-start(bf16[4,512,128]{2,1,0:T(8,128)(2,1)S(1)} %get-tuple-element.52), channel_id=1, source_target_pairs={{1,2},{3,4},{5,6},{2,1},{4,3},{6,5},{9,10},{11,12},{13,14},{10,9},... | collective-permute-start | bytes 1572872 | tf_op jit(solution)/shard_map/ppermute | solution.py:20
  50.4 0.1 collective-permute-start.3
  50.5 0.0 collective-permute-done.8.first
  50.5 8.1 %collective-permute-start.5 = (bf16[4,128,256]{2,1,0:T(8,128)(2,1)S(1)}, bf16[4,128,256]{2,1,0:T(8,128)(2,1)S(1)}, u32[]{:S(2)}, u32[]{:S(2)}) collective-permute-start(bf16[4,128,256]{2,1,0:T(8,128)(2,1)S(1)} %get-tuple-element.40), channel_id=1, source_target_pairs={{8,16},{16,8},{9,17},{17,9},{10,18},{18,10},{11,19},{19,11},{12,20... | collective-permute-start | bytes 786440 | tf_op jit(solution)/shard_map/ppermute | solution.py:20
  58.7 0.0 collective-permute-done.9.second
  58.7 0.1 join.1
  58.8 0.1 collective-permute-start.10
  58.9 0.0 collective-permute-done.12.first
  58.9 2.6 %collective-permute-start.11 = (bf16[2,4,128,128]{3,2,1,0:T(8,128)(2,1)S(1)}, bf16[2,4,128,128]{3,2,1,0:T(8,128)(2,1)S(1)}, u32[]{:S(2)}, u32[]{:S(2)}) collective-permute-start(bf16[2,4,128,128]{3,2,1,0:T(8,128)(2,1)S(1)} %get-tuple-element.49), channel_id=1, source_target_pairs={{8,16},{16,8},{9,17},{17,9},{10,18},{18,10},{11,19},{19,11},{12,20... | collective-permute-start | bytes 786440 | tf_op jit(solution)/shard_map/ppermute | solution.py:20
  61.5 0.0 collective-permute-done.13.second
  61.5 1.6 %settle.1 = (f32[4,768,768]{2,1,0:T(8,128)S(1)}, f32[4,512,512]{2,1,0:T(8,128)}) custom-call(bf16[4,512,128]{2,1,0:T(8,128)(2,1)S(1)} %collective-permute-done.12.first, bf16[4,512,128]{2,1,0:T(8,128)(2,1)S(1)} %collective-permute-done.13.second, f32[4,768,768]{2,1,0:T(8,128)S(1)} %get-tuple-element.50.total.total_in), custom_call_target="tpu_custom_call", output_to_operand_aliasing={{0}: (2, {})} | custom-call | tf_op jit(solution)/shard_map/settle/pallas_call | solution.py:453
  63.1 6.4 %collective-permute-done.5.core_1 = bf16[4,128,256]{2,1,0:T(8,128)(2,1)S(1)} collective-permute-done((bf16[4,128,256]{2,1,0:T(8,128)(2,1)S(1)}, bf16[4,128,256]{2,1,0:T(8,128)(2,1)S(1)}, u32[]{:S(2)}, u32[]{:S(2)}) %collective-permute-start.5) | collective-permute-done | bytes 262176 | tf_op jit(solution)/shard_map/ppermute | solution.py:20
  69.5 0.0 collective-permute-done.3.core_0
  69.5 1.5 %collective-permute-done.10.edge_0 = bf16[2,4,128,128]{3,2,1,0:T(8,128)(2,1)S(1)} collective-permute-done((bf16[2,4,128,128]{3,2,1,0:T(8,128)(2,1)S(1)}, bf16[2,4,128,128]{3,2,1,0:T(8,128)(2,1)S(1)}, u32[]{:S(2)}, u32[]{:S(2)}) %collective-permute-start.10) | collective-permute-done | bytes 262176 | tf_op jit(solution)/shard_map/ppermute | solution.py:20
  71.0 9.2 %collective-permute-done.11.edge_1 = bf16[2,4,128,128]{3,2,1,0:T(8,128)(2,1)S(1)} collective-permute-done((bf16[2,4,128,128]{3,2,1,0:T(8,128)(2,1)S(1)}, bf16[2,4,128,128]{3,2,1,0:T(8,128)(2,1)S(1)}, u32[]{:S(2)}, u32[]{:S(2)}) %collective-permute-start.11) | collective-permute-done | bytes 262176 | tf_op jit(solution)/shard_map/ppermute | solution.py:20
  80.1 1.4 %finish.1 = f32[4,512,512]{2,1,0:T(8,128)} custom-call(bf16[4,128,256]{2,1,0:T(8,128)(2,1)S(1)} %collective-permute-done.3.core_0, bf16[4,128,256]{2,1,0:T(8,128)(2,1)S(1)} %collective-permute-done.5.core_1, bf16[2,4,128,128]{3,2,1,0:T(8,128)(2,1)S(1)} %collective-permute-done.10.edge_0, ...), custom_call_target="tpu_custom_call", output_to_operand_aliasing={{}: (5, {})} | custom-call | tf_op jit(solution)/shard_map/finish/pallas_call | solution.py:496
  (2 shorter events, 0.0 us)
Async XLA Ops:
  0.0 10.1 %copy-start.1 = (bf16[6,256,256]{2,1,0:T(8,128)(2,1)S(1)}, bf16[6,256,256]{2,1,0:T(8,128)(2,1)}, u32[]{:S(2)}) copy-start(bf16[6,256,256]{2,1,0:T(8,128)(2,1)} %constant.2.clone.tab) | copy-start | bytes 2359300
  0.0 10.1 %copy-start = (bf16[12,256,256]{2,1,0:T(8,128)(2,1)S(1)}, bf16[12,256,256]{2,1,0:T(8,128)(2,1)}, u32[]{:S(2)}) copy-start(bf16[12,256,256]{2,1,0:T(8,128)(2,1)} %measured.7) | copy-start | bytes 4718596
  0.0 10.1 %copy-start.2 = (f32[2,256,256]{2,1,0:T(8,128)S(1)}, f32[2,256,256]{2,1,0:T(8,128)}, u32[]{:S(2)}) copy-start(f32[2,256,256]{2,1,0:T(8,128)} %light.7) | copy-start | bytes 1572868
  0.0 10.1 %copy-start.3 = (s32[12,2]{0,1:T(2,128)S(1)}, s32[12,2]{0,1:T(2,128)}, u32[]{:S(2)}) copy-start(s32[12,2]{0,1:T(2,128)} %param.11) | copy-start | bytes 292
  0.0 2.3 %copy-start.4 = (f32[4,512,512]{2,1,0:T(8,128)S(1)}, f32[4,512,512]{2,1,0:T(8,128)}, u32[]{:S(2)}) copy-start(f32[4,512,512]{2,1,0:T(8,128)} %objects.1) | copy-start | bytes 12582916
  2.4 7.7 %copy-start.5 = (f32[256,256]{1,0:T(8,128)S(1)}, f32[256,256]{1,0:T(8,128)}, u32[]{:S(2)}) copy-start(f32[256,256]{1,0:T(8,128)} %spread.1) | copy-start | bytes 786436
  2.9 9.5 %collective-permute-start = (bf16[4,512,128]{2,1,0:T(8,128)(2,1)S(1)}, bf16[4,512,128]{2,1,0:T(8,128)(2,1)S(1)}, u32[]{:S(2)}, u32[]{:S(2)}) collective-permute-start(bf16[4,512,128]{2,1,0:T(8,128)(2,1)S(1)} %get-tuple-element.32), channel_id=1, source_target_pairs={{0,1},{2,3},{4,5},{6,7},{1,0},{3,2},{5,4},{7,6},{8,9},{10,11},{12,... | collective-permute-start | bytes 1572872 | tf_op jit(solution)/shard_map/ppermute | solution.py:20
  3.0 10.5 %collective-permute-start.1 = (bf16[4,512,128]{2,1,0:T(8,128)(2,1)S(1)}, bf16[4,512,128]{2,1,0:T(8,128)(2,1)S(1)}, u32[]{:S(2)}, u32[]{:S(2)}) collective-permute-start(bf16[4,512,128]{2,1,0:T(8,128)(2,1)S(1)} %get-tuple-element.33), channel_id=1, source_target_pairs={{1,2},{3,4},{5,6},{2,1},{4,3},{6,5},{9,10},{11,12},{13,14},{10,9},... | collective-permute-start | bytes 1572872 | tf_op jit(solution)/shard_map/ppermute | solution.py:20
  5.5 14.7 %collective-permute-start.2 = (bf16[4,128,512]{2,1,0:T(8,128)(2,1)S(1)}, bf16[4,128,512]{2,1,0:T(8,128)(2,1)S(1)}, u32[]{:S(2)}, u32[]{:S(2)}) collective-permute-start(bf16[4,128,512]{2,1,0:T(8,128)(2,1)S(1)} %get-tuple-element.34), channel_id=1, source_target_pairs={{0,8},{16,24},{8,0},{24,16},{1,9},{17,25},{9,1},{25,17},{2,10},{18... | collective-permute-start | bytes 1572872 | tf_op jit(solution)/shard_map/ppermute | solution.py:20
  7.0 24.3 %collective-permute-start.4 = (bf16[4,128,512]{2,1,0:T(8,128)(2,1)S(1)}, bf16[4,128,512]{2,1,0:T(8,128)(2,1)S(1)}, u32[]{:S(2)}, u32[]{:S(2)}) collective-permute-start(bf16[4,128,512]{2,1,0:T(8,128)(2,1)S(1)} %get-tuple-element.37), channel_id=1, source_target_pairs={{8,16},{16,8},{9,17},{17,9},{10,18},{18,10},{11,19},{19,11},{12,20... | collective-permute-start | bytes 1572872 | tf_op jit(solution)/shard_map/ppermute | solution.py:20
  31.4 5.9 %collective-permute-start.6 = (bf16[2,4,128,128]{3,2,1,0:T(8,128)(2,1)S(1)}, bf16[2,4,128,128]{3,2,1,0:T(8,128)(2,1)S(1)}, u32[]{:S(2)}, u32[]{:S(2)}) collective-permute-start(bf16[2,4,128,128]{3,2,1,0:T(8,128)(2,1)S(1)} %get-tuple-element.41), channel_id=1, source_target_pairs={{0,1},{2,3},{4,5},{6,7},{1,0},{3,2},{5,4},{7,6},{8,9},{10,11},{12,... | collective-permute-start | bytes 786440 | tf_op jit(solution)/shard_map/ppermute | solution.py:20
  31.6 7.7 %collective-permute-start.7 = (bf16[2,4,128,128]{3,2,1,0:T(8,128)(2,1)S(1)}, bf16[2,4,128,128]{3,2,1,0:T(8,128)(2,1)S(1)}, u32[]{:S(2)}, u32[]{:S(2)}) collective-permute-start(bf16[2,4,128,128]{3,2,1,0:T(8,128)(2,1)S(1)} %get-tuple-element.42), channel_id=1, source_target_pairs={{1,2},{3,4},{5,6},{2,1},{4,3},{6,5},{9,10},{11,12},{13,14},{10,9},... | collective-permute-start | bytes 786440 | tf_op jit(solution)/shard_map/ppermute | solution.py:20
  44.3 14.6 %collective-permute-start.12 = (bf16[4,512,128]{2,1,0:T(8,128)(2,1)S(1)}, bf16[4,512,128]{2,1,0:T(8,128)(2,1)S(1)}, u32[]{:S(2)}, u32[]{:S(2)}) collective-permute-start(bf16[4,512,128]{2,1,0:T(8,128)(2,1)S(1)} %get-tuple-element.51), channel_id=1, source_target_pairs={{0,1},{2,3},{4,5},{6,7},{1,0},{3,2},{5,4},{7,6},{8,9},{10,11},{12,... | collective-permute-start | bytes 1572872 | tf_op jit(solution)/shard_map/ppermute | solution.py:20
  44.4 6.1 %collective-permute-start.8 = (bf16[2,4,128,128]{3,2,1,0:T(8,128)(2,1)S(1)}, bf16[2,4,128,128]{3,2,1,0:T(8,128)(2,1)S(1)}, u32[]{:S(2)}, u32[]{:S(2)}) collective-permute-start(bf16[2,4,128,128]{3,2,1,0:T(8,128)(2,1)S(1)} %get-tuple-element.46), channel_id=1, source_target_pairs={{0,1},{2,3},{4,5},{6,7},{1,0},{3,2},{5,4},{7,6},{8,9},{10,11},{12,... | collective-permute-start | bytes 786440 | tf_op jit(solution)/shard_map/ppermute | solution.py:20
  44.9 13.8 %collective-permute-start.9 = (bf16[2,4,128,128]{3,2,1,0:T(8,128)(2,1)S(1)}, bf16[2,4,128,128]{3,2,1,0:T(8,128)(2,1)S(1)}, u32[]{:S(2)}, u32[]{:S(2)}) collective-permute-start(bf16[2,4,128,128]{3,2,1,0:T(8,128)(2,1)S(1)} %get-tuple-element.47), channel_id=1, source_target_pairs={{1,2},{3,4},{5,6},{2,1},{4,3},{6,5},{9,10},{11,12},{13,14},{10,9},... | collective-permute-start | bytes 786440 | tf_op jit(solution)/shard_map/ppermute | solution.py:20
  46.8 14.7 %collective-permute-start.13 = (bf16[4,512,128]{2,1,0:T(8,128)(2,1)S(1)}, bf16[4,512,128]{2,1,0:T(8,128)(2,1)S(1)}, u32[]{:S(2)}, u32[]{:S(2)}) collective-permute-start(bf16[4,512,128]{2,1,0:T(8,128)(2,1)S(1)} %get-tuple-element.52), channel_id=1, source_target_pairs={{1,2},{3,4},{5,6},{2,1},{4,3},{6,5},{9,10},{11,12},{13,14},{10,9},... | collective-permute-start | bytes 1572872 | tf_op jit(solution)/shard_map/ppermute | solution.py:20
  50.4 19.1 %collective-permute-start.3 = (bf16[4,128,256]{2,1,0:T(8,128)(2,1)S(1)}, bf16[4,128,256]{2,1,0:T(8,128)(2,1)S(1)}, u32[]{:S(2)}, u32[]{:S(2)}) collective-permute-start(bf16[4,128,256]{2,1,0:T(8,128)(2,1)S(1)} %get-tuple-element.36.token), channel_id=1, source_target_pairs={{0,8},{16,24},{8,0},{24,16},{1,9},{17,25},{9,1},{25,17},{2,10},{18... | collective-permute-start | bytes 786440 | tf_op jit(solution)/shard_map/ppermute | solution.py:20
  50.5 19.0 %collective-permute-start.5 = (bf16[4,128,256]{2,1,0:T(8,128)(2,1)S(1)}, bf16[4,128,256]{2,1,0:T(8,128)(2,1)S(1)}, u32[]{:S(2)}, u32[]{:S(2)}) collective-permute-start(bf16[4,128,256]{2,1,0:T(8,128)(2,1)S(1)} %get-tuple-element.40), channel_id=1, source_target_pairs={{8,16},{16,8},{9,17},{17,9},{10,18},{18,10},{11,19},{19,11},{12,20... | collective-permute-start | bytes 786440 | tf_op jit(solution)/shard_map/ppermute | solution.py:20
  58.8 12.2 %collective-permute-start.10 = (bf16[2,4,128,128]{3,2,1,0:T(8,128)(2,1)S(1)}, bf16[2,4,128,128]{3,2,1,0:T(8,128)(2,1)S(1)}, u32[]{:S(2)}, u32[]{:S(2)}) collective-permute-start(bf16[2,4,128,128]{3,2,1,0:T(8,128)(2,1)S(1)} %get-tuple-element.48), channel_id=1, source_target_pairs={{0,8},{16,24},{8,0},{24,16},{1,9},{17,25},{9,1},{25,17},{2,10},{18... | collective-permute-start | bytes 786440 | tf_op jit(solution)/shard_map/ppermute | solution.py:20
  58.9 21.2 %collective-permute-start.11 = (bf16[2,4,128,128]{3,2,1,0:T(8,128)(2,1)S(1)}, bf16[2,4,128,128]{3,2,1,0:T(8,128)(2,1)S(1)}, u32[]{:S(2)}, u32[]{:S(2)}) collective-permute-start(bf16[2,4,128,128]{3,2,1,0:T(8,128)(2,1)S(1)} %get-tuple-element.49), channel_id=1, source_target_pairs={{8,16},{16,8},{9,17},{17,9},{10,18},{18,10},{11,19},{19,11},{12,20... | collective-permute-start | bytes 786440 | tf_op jit(solution)/shard_map/ppermute | solution.py:20

commit v5 on v4

--- a/solution.py
+++ b/solution.py
@@ -438,74 +438,67 @@
     )(edge, first, second)
 
 
-def settle_kernel(n, first, second, total_in, total, out, sems):
-    tile = out.shape[1]
-    for turn, side in enumerate((first, second)):
+def settle_kernel(n, side_0, side_1, core_0, core_1, total_in, total, out, sems):
+    planes, tile = out.shape[:2]
+    inner, middle = pl.ds(n, tile), pl.ds(2 * n, tile - 2 * n)
+    for turn, (side, core) in enumerate(((side_0, core_0), (side_1, core_1))):
         cols = pick(ahead("col", turn), n, tile, n)
-        for k in range(out.shape[0]):
-            total[k, pl.ds(n, tile), cols] += side[k].astype(FULL)
-    rows = tile - 2 * n
-    run_copies([(total.at[:, pl.ds(2 * n, rows), pl.ds(n, tile)], out.at[:, pl.ds(n, rows)])], sems)
-
-
-def settle(total, first, second, n):
-    planes, tile = first.shape[:2]
+        rows = pick(ahead("row", turn), n, tile, n)
+        for k in range(planes):
+            total[k, inner, cols] += side[k].astype(FULL)
+            total[k, rows, middle] += core[k].astype(FULL)
+    moves = [(total.at[:, middle, inner], out.at[:, pl.ds(n, tile - 2 * n)])]
+    for at in (0, tile - n):
+        band = total.at[:, pl.ds(n + at, n), middle]
+        moves.append((band, out.at[:, pl.ds(at, n), pl.ds(n, tile - 2 * n)]))
+    run_copies(moves, sems)
+
+
+def settle(total, sides, cores, n):
+    planes, tile = sides[0].shape[:2]
     return pl.pallas_call(
         functools.partial(settle_kernel, n),
         out_shape=[
             jax.ShapeDtypeStruct(total.shape, FULL),
             jax.ShapeDtypeStruct((planes, tile, tile), FULL),
         ],
-        in_specs=[VMEM] * 3,
+        in_specs=[VMEM] * 5,
         out_specs=[VMEM, ANYWHERE],
-        scratch_shapes=[pltpu.SemaphoreType.DMA((1,))],
-        input_output_aliases={2: 0},
+        scratch_shapes=[pltpu.SemaphoreType.DMA((3,))],
+        input_output_aliases={4: 0},
         compiler_params=pltpu.CompilerParams(vmem_limit_bytes=16 << 20),
         name="settle",
-    )(first, second, total)
-
-
-def finish_kernel(n, core_0, core_1, edge_0, edge_1, total, out_in, out, band, sems):
+    )(*sides, *cores, total)
+
+
+def finish_kernel(n, edge_0, edge_1, total, out_in, out, block, sems):
     planes, tile = out.shape[:2]
     copies = []
-    for turn, (core, edge) in enumerate(((core_0, edge_0), (core_1, edge_1))):
-        side = ahead("row", turn)
-        rows = pick(side, n, tile, n)
-        to = pick(side, 0, tile - n, n)
-        for k in range(planes):
-            band[turn, k, :, pl.ds(n, tile - 2 * n)] = total[
-                k, rows, pl.ds(2 * n, tile - 2 * n)
-            ] + core[k].astype(FULL)
-            for e in range(2):
-                at = ahead("col", e)
-                band[turn, k, :, pick(at, 0, tile - n, n)] = total[
-                    k, rows, pick(at, n, tile, n)
-                ] + edge[e, k].astype(FULL)
-            copies.append(
-                pltpu.make_async_copy(
-                    band.at[turn, k], out.at[k, to], sems.at[turn * planes + k]
-                )
-            )
+    for turn, edge in enumerate((edge_0, edge_1)):
+        for e in range(2):
+            row, col = ahead("row", turn), ahead("col", e)
+            rows, cols = pick(row, n, tile, n), pick(col, n, tile, n)
+            for k in range(planes):
+                block[turn, e, k] = total[k, rows, cols] + edge[e, k].astype(FULL)
+            target = out.at[:, pick(row, 0, tile - n, n), pick(col, 0, tile - n, n)]
+            copies.append(pltpu.make_async_copy(block.at[turn, e], target, sems.at[2 * turn + e]))
             copies[-1].start()
     for copy in copies:
         copy.wait()
 
 
-def finish(total, out, cores, edges, n):
-    planes, tile = out.shape[:2]
+def finish(total, out, edges, n):
+    planes = out.shape[0]
     return pl.pallas_call(
         functools.partial(finish_kernel, n),
         out_shape=jax.ShapeDtypeStruct(out.shape, FULL),
-        in_specs=[VMEM] * 5 + [ANYWHERE],
+        in_specs=[VMEM] * 3 + [ANYWHERE],
         out_specs=ANYWHERE,
-        scratch_shapes=[
-            pltpu.VMEM((2, planes, n, tile), FULL),
-            pltpu.SemaphoreType.DMA((2 * planes,)),
-        ],
-        input_output_aliases={5: 0},
+        scratch_shapes=[pltpu.VMEM((2, 2, planes, n, n), FULL), pltpu.SemaphoreType.DMA((4,))],
+        input_output_aliases={3: 0},
         compiler_params=pltpu.CompilerParams(vmem_limit_bytes=16 << 20),
         name="finish",
-    )(*cores, *edges, total, out)
+    )(*edges, total, out)
 
 
 def both(parts, axis):
@@ -530,8 +523,8 @@
     ends = both(ends, "col")
     outer = both(sides(total, n), "col")
     edges = both(join(edge, *ends), "row")
-    total, out = settle(total, *outer, n)
-    return finish(total, out, cores, edges, n)
+    total, out = settle(total, outer, cores, n)
+    return finish(total, out, edges, n)
 
 
 def solution(mesh):

time: 82 us -> 81 us (0.988); the launches traced: 81.7 us -> 79.6 us
  waiting for transfers between devices: 29 us -> 22.6 us
  starting transfers between devices: 25.6 us -> 29.7 us
    ppermute x14, waiting for transfers between devices: 29 us -> 22.6 us  [exchange(): return lax.ppermute(x, axis, pairs + [(j, i) for i, j in pairs])]
    ppermute x14, starting transfers between devices: 25.6 us -> 29.7 us  [exchange(): return lax.ppermute(x, axis, pairs + [(j, i) for i, j in pairs])]
  transfers between devices with their start and end apart: 14 -> 14, of which waited for: 7 -> 7; matrix products, arithmetic and copies ran while one was open for 0% -> 0% of each run, Pallas kernels for 20% -> 22%
where the time goes in v5:
time: 81 us; the launch traced here: 79.6 us
  starting transfers between devices  29.7 us (37%)
  Pallas kernels  23.9 us (30%)
  waiting for transfers between devices  22.6 us (28%)
  local copies, waits for them, and re-layouts  2.35 us (3%)
  between operations  1.06 us (1%)
    ppermute x14, starting transfers between devices, exchange(): return lax.ppermute(x, axis, pairs + [(j, i) for i, j in pairs])  29.7 us
    ppermute x14, waiting for transfers between devices, exchange(): return lax.ppermute(x, axis, pairs + [(j, i) for i, j in pairs])  22.6 us
    pallas_call x4, Pallas kernels, run_slots(): pl.pallas_call(functools.partial(slots_kernel, mode), out_shape=[jax.Shap...  19.8 us
    unnamed x12, local copies, waits for them, and re-layouts  2.35 us
    pallas_call x1, Pallas kernels, settle(): pl.pallas_call(functools.partial(settle_kernel, n), out_shape=[jax.ShapeD...  2.18 us
  transfers between devices with their start and end apart: 14, of which 7 were waited for; matrix products, arithmetic and copies ran while one was open for 0% of the time, Pallas kernels for 22%

profile of v5, /device:TPU:20, one launch (start us, length us, event | category | flops | bytes accessed | tf_op | source)
XLA Modules:
  0.0 79.6 jit_solution(12798653369698949557)
XLA Ops:
  0.0 0.0 copy-start.1
  0.0 0.0 copy-start
  0.0 0.0 copy-start.3
  0.0 0.0 copy-start.4
  0.0 2.3 %copy-done.4 = f32[4,512,512]{2,1,0:T(8,128)S(1)} copy-done((f32[4,512,512]{2,1,0:T(8,128)S(1)}, f32[4,512,512]{2,1,0:T(8,128)}, u32[]{:S(2)}) %copy-start.4) | copy-done | bytes 4194328
  2.4 0.6 prepare.1
  2.9 1.6 %collective-permute-start = (bf16[4,128,512]{2,1,0:T(8,128)(2,1)S(1)}, bf16[4,128,512]{2,1,0:T(8,128)(2,1)S(1)}, u32[]{:S(2)}, u32[]{:S(2)}) collective-permute-start(bf16[4,128,512]{2,1,0:T(8,128)(2,1)S(1)} %get-tuple-element.32), channel_id=1, source_target_pairs={{0,8},{16,24},{8,0},{24,16},{1,9},{17,25},{9,1},{25,17},{2,10},{18... | collective-permute-start | bytes 1572872 | tf_op jit(solution)/shard_map/ppermute | solution.py:20
  4.5 0.0 collective-permute-start.2
  4.5 2.5 %collective-permute-start.3 = (bf16[4,512,128]{2,1,0:T(8,128)(2,1)S(1)}, bf16[4,512,128]{2,1,0:T(8,128)(2,1)S(1)}, u32[]{:S(2)}, u32[]{:S(2)}) collective-permute-start(bf16[4,512,128]{2,1,0:T(8,128)(2,1)S(1)} %get-tuple-element.35), channel_id=1, source_target_pairs={{1,2},{3,4},{5,6},{2,1},{4,3},{6,5},{9,10},{11,12},{13,14},{10,9},... | collective-permute-start | bytes 1572872 | tf_op jit(solution)/shard_map/ppermute | solution.py:20
  7.0 2.4 %collective-permute-start.1 = (bf16[4,128,512]{2,1,0:T(8,128)(2,1)S(1)}, bf16[4,128,512]{2,1,0:T(8,128)(2,1)S(1)}, u32[]{:S(2)}, u32[]{:S(2)}) collective-permute-start(bf16[4,128,512]{2,1,0:T(8,128)(2,1)S(1)} %get-tuple-element.33), channel_id=1, source_target_pairs={{8,16},{16,8},{9,17},{17,9},{10,18},{18,10},{11,19},{19,11},{12,20... | collective-permute-start | bytes 1572872 | tf_op jit(solution)/shard_map/ppermute | solution.py:20
  10.0 0.0 copy-done.1
  10.0 0.0 copy-done
  10.0 0.0 copy-done.2
  10.0 0.0 copy-done.3
  10.0 0.0 copy-done.5
  10.1 2.3 %shard_map.73 = (f32[4,768,768]{2,1,0:T(8,128)S(1)}, f32[2,256,256]{2,1,0:T(8,128)S(1)}) custom-call(s32[2,12]{1,0:T(2,128)S(1)} %bitcast.1, s32[1]{0:T(128)S(6)} %copy.24.counts, bf16[6,256,256]{2,1,0:T(8,128)(2,1)S(1)} %copy-done.1, f32[2,256,256]{2,1,0:T(8,128)S(1)} %copy-done.2, f32[256,256]{1,0:T(8,128)S(1)} %copy-done.5, ...), custom_call_target="tpu_custom_call" | custom-call | flops 2617245696 | tf_op jit(solution)/shard_map/pallas_call | solution.py:367
  12.3 4.5 %collective-permute-done.refs_2_.first = bf16[4,128,512]{2,1,0:T(8,128)(2,1)S(1)} collective-permute-done((bf16[4,128,512]{2,1,0:T(8,128)(2,1)S(1)}, bf16[4,128,512]{2,1,0:T(8,128)(2,1)S(1)}, u32[]{:S(2)}, u32[]{:S(2)}) %collective-permute-start) | collective-permute-done | bytes 524320 | tf_op jit(solution)/shard_map/ppermute | solution.py:20
  16.8 0.0 collective-permute-done.2.refs_0_
  16.8 0.0 collective-permute-done.3.refs_1_
  16.8 8.9 %shard_map.74 = (bf16[4,768,768]{2,1,0:T(8,128)(2,1)S(1)}, f32[4,768,768]{2,1,0:T(8,128)S(1)}, bf16[4,128,256]{2,1,0:T(8,128)(2,1)S(1)}) custom-call(s32[2,12]{1,0:T(2,128)S(1)} %bitcast.2, s32[1]{0:T(128)S(6)} %copy.24.counts, bf16[6,256,256]{2,1,0:T(8,128)(2,1)S(1)} %copy-done.1, ...), custom_call_target="tpu_custom_call", output_to_operand_aliasing={{0}: (9, {}), {1}: (10, {})} | custom-call | flops 2617245696 | tf_op jit(solution)/shard_map/pallas_call | solution.py:367
  25.7 2.1 %collective-permute-done.1.second.refs_0_ = bf16[4,128,512]{2,1,0:T(8,128)(2,1)S(1)} collective-permute-done((bf16[4,128,512]{2,1,0:T(8,128)(2,1)S(1)}, bf16[4,128,512]{2,1,0:T(8,128)(2,1)S(1)}, u32[]{:S(2)}, u32[]{:S(2)}) %collective-permute-start.1) | collective-permute-done | bytes 524320 | tf_op jit(solution)/shard_map/ppermute | solution.py:20
  27.8 0.1 turn.1
  27.9 0.1 collective-permute-start.4
  28.0 2.4 %collective-permute-start.5 = (bf16[2,4,128,128]{3,2,1,0:T(8,128)(2,1)S(1)}, bf16[2,4,128,128]{3,2,1,0:T(8,128)(2,1)S(1)}, u32[]{:S(2)}, u32[]{:S(2)}) collective-permute-start(bf16[2,4,128,128]{3,2,1,0:T(8,128)(2,1)S(1)} %get-tuple-element.39), channel_id=1, source_target_pairs={{1,2},{3,4},{5,6},{2,1},{4,3},{6,5},{9,10},{11,12},{13,14},{10,9},... | collective-permute-start | bytes 786440 | tf_op jit(solution)/shard_map/ppermute | solution.py:20
  30.5 3.8 %shard_map.75 = (bf16[4,768,768]{2,1,0:T(8,128)(2,1)S(1)}, f32[4,768,768]{2,1,0:T(8,128)S(1)}, bf16[4,128,256]{2,1,0:T(8,128)(2,1)S(1)}) custom-call(s32[2,12]{1,0:T(2,128)S(1)} %bitcast.3, s32[1]{0:T(128)S(6)} %copy.24.counts, bf16[6,256,256]{2,1,0:T(8,128)(2,1)S(1)} %copy-done.1, ...), custom_call_target="tpu_custom_call", output_to_operand_aliasing={{0}: (7, {}), {1}: (8, {})} | custom-call | flops 2617245696 | tf_op jit(solution)/shard_map/pallas_call | solution.py:367
  34.2 0.0 collective-permute-done.4.refs_0_
  34.2 1.5 %collective-permute-done.5.refs_1_ = bf16[2,4,128,128]{3,2,1,0:T(8,128)(2,1)S(1)} collective-permute-done((bf16[2,4,128,128]{3,2,1,0:T(8,128)(2,1)S(1)}, bf16[2,4,128,128]{3,2,1,0:T(8,128)(2,1)S(1)}, u32[]{:S(2)}, u32[]{:S(2)}) %collective-permute-start.5) | collective-permute-done | bytes 262176 | tf_op jit(solution)/shard_map/ppermute | solution.py:20
  35.7 4.9 %shard_map.76 = (bf16[4,768,768]{2,1,0:T(8,128)(2,1)S(1)}, f32[4,768,768]{2,1,0:T(8,128)S(1)}, bf16[2,4,128,128]{3,2,1,0:T(8,128)(2,1)S(1)}, bf16[2,4,128,128]{3...) custom-call(s32[2,12]{1,0:T(2,128)S(1)} %bitcast.4, ...), custom_call_target="tpu_custom_call", output_to_operand_aliasing={{0}: (8, {}), {1}: (9, {})} | custom-call | flops 2617245696 | tf_op jit(solution)/shard_map/pallas_call | solution.py:367
  40.6 0.1 collective-permute-start.6
  40.6 2.4 %collective-permute-start.7 = (bf16[2,4,128,128]{3,2,1,0:T(8,128)(2,1)S(1)}, bf16[2,4,128,128]{3,2,1,0:T(8,128)(2,1)S(1)}, u32[]{:S(2)}, u32[]{:S(2)}) collective-permute-start(bf16[2,4,128,128]{3,2,1,0:T(8,128)(2,1)S(1)} %get-tuple-element.46), channel_id=1, source_target_pairs={{1,2},{3,4},{5,6},{2,1},{4,3},{6,5},{9,10},{11,12},{13,14},{10,9},... | collective-permute-start | bytes 786440 | tf_op jit(solution)/shard_map/ppermute | solution.py:20
  43.1 0.2 sides.1
  43.3 0.5 collective-permute-start.10
  43.8 2.7 %collective-permute-start.11 = (bf16[4,512,128]{2,1,0:T(8,128)(2,1)S(1)}, bf16[4,512,128]{2,1,0:T(8,128)(2,1)S(1)}, u32[]{:S(2)}, u32[]{:S(2)}) collective-permute-start(bf16[4,512,128]{2,1,0:T(8,128)(2,1)S(1)} %get-tuple-element.51), channel_id=1, source_target_pairs={{1,2},{3,4},{5,6},{2,1},{4,3},{6,5},{9,10},{11,12},{13,14},{10,9},... | collective-permute-start | bytes 1572872 | tf_op jit(solution)/shard_map/ppermute | solution.py:20
  46.5 8.1 %collective-permute-start.13 = (bf16[4,128,256]{2,1,0:T(8,128)(2,1)S(1)}, bf16[4,128,256]{2,1,0:T(8,128)(2,1)S(1)}, u32[]{:S(2)}, u32[]{:S(2)}) collective-permute-start(bf16[4,128,256]{2,1,0:T(8,128)(2,1)S(1)} %get-tuple-element.52), channel_id=1, source_target_pairs={{8,16},{16,8},{9,17},{17,9},{10,18},{18,10},{11,19},{19,11},{12,20... | collective-permute-start | bytes 786440 | tf_op jit(solution)/shard_map/ppermute | solution.py:20
  54.6 0.0 collective-permute-done.6.first
  54.6 0.1 collective-permute-start.12
  54.7 0.0 collective-permute-done.7.second
  54.7 0.1 join.1
  54.8 2.1 %collective-permute-start.8 = (bf16[2,4,128,128]{3,2,1,0:T(8,128)(2,1)S(1)}, bf16[2,4,128,128]{3,2,1,0:T(8,128)(2,1)S(1)}, u32[]{:S(2)}, u32[]{:S(2)}) collective-permute-start(bf16[2,4,128,128]{3,2,1,0:T(8,128)(2,1)S(1)} %get-tuple-element.47), channel_id=1, source_target_pairs={{0,8},{16,24},{8,0},{24,16},{1,9},{17,25},{9,1},{25,17},{2,10},{18... | collective-permute-start | bytes 786440 | tf_op jit(solution)/shard_map/ppermute | solution.py:20
  56.9 4.9 %collective-permute-done.13.core_1 = bf16[4,128,256]{2,1,0:T(8,128)(2,1)S(1)} collective-permute-done((bf16[4,128,256]{2,1,0:T(8,128)(2,1)S(1)}, bf16[4,128,256]{2,1,0:T(8,128)(2,1)S(1)}, u32[]{:S(2)}, u32[]{:S(2)}) %collective-permute-start.13) | collective-permute-done | bytes 262176 | tf_op jit(solution)/shard_map/ppermute | solution.py:20
  61.7 4.8 %collective-permute-start.9 = (bf16[2,4,128,128]{3,2,1,0:T(8,128)(2,1)S(1)}, bf16[2,4,128,128]{3,2,1,0:T(8,128)(2,1)S(1)}, u32[]{:S(2)}, u32[]{:S(2)}) collective-permute-start(bf16[2,4,128,128]{3,2,1,0:T(8,128)(2,1)S(1)} %get-tuple-element.48), channel_id=1, source_target_pairs={{8,16},{16,8},{9,17},{17,9},{10,18},{18,10},{11,19},{19,11},{12,20... | collective-permute-start | bytes 786440 | tf_op jit(solution)/shard_map/ppermute | solution.py:20
  66.5 0.3 collective-permute-done.12.core_0
  66.9 0.0 collective-permute-done.10.side_0
  66.9 0.0 collective-permute-done.11.side_1
  66.9 2.2 %settle.1 = (f32[4,768,768]{2,1,0:T(8,128)S(1)}, f32[4,512,512]{2,1,0:T(8,128)}) custom-call(bf16[4,512,128]{2,1,0:T(8,128)(2,1)S(1)} %collective-permute-done.10.side_0, bf16[4,512,128]{2,1,0:T(8,128)(2,1)S(1)} %collective-permute-done.11.side_1, bf16[4,128,256]{2,1,0:T(8,128)(2,1)S(1)} %collective-permute-done.12.core_0, ...), custom_call_target="tpu_custom_call", output_to_operand_aliasing={{0}: (4, {})} | custom-call | tf_op jit(solution)/shard_map/settle/pallas_call | solution.py:459
  69.1 3.4 %collective-permute-done.8.edge_0 = bf16[2,4,128,128]{3,2,1,0:T(8,128)(2,1)S(1)} collective-permute-done((bf16[2,4,128,128]{3,2,1,0:T(8,128)(2,1)S(1)}, bf16[2,4,128,128]{3,2,1,0:T(8,128)(2,1)S(1)}, u32[]{:S(2)}, u32[]{:S(2)}) %collective-permute-start.8) | collective-permute-done | bytes 262176 | tf_op jit(solution)/shard_map/ppermute | solution.py:20
  72.5 5.9 %collective-permute-done.9.edge_1 = bf16[2,4,128,128]{3,2,1,0:T(8,128)(2,1)S(1)} collective-permute-done((bf16[2,4,128,128]{3,2,1,0:T(8,128)(2,1)S(1)}, bf16[2,4,128,128]{3,2,1,0:T(8,128)(2,1)S(1)}, u32[]{:S(2)}, u32[]{:S(2)}) %collective-permute-start.9) | collective-permute-done | bytes 262176 | tf_op jit(solution)/shard_map/ppermute | solution.py:20
  78.4 1.0 %finish.1 = f32[4,512,512]{2,1,0:T(8,128)} custom-call(bf16[2,4,128,128]{3,2,1,0:T(8,128)(2,1)S(1)} %collective-permute-done.8.edge_0, bf16[2,4,128,128]{3,2,1,0:T(8,128)(2,1)S(1)} %collective-permute-done.9.edge_1, f32[4,768,768]{2,1,0:T(8,128)S(1)} %get-tuple-element.53.total, f32[4,512,512]{2,1,0:T(8,128)} %get-tuple-element.54.out_in), custom_call_target="tpu_custom_call", output_to_operand_aliasing={{}: (3, {})} | custom-call | tf_op jit(solution)/shard_map/finish/pallas_call | solution.py:492
  (2 shorter events, 0.0 us)
Async XLA Ops:
  0.0 10.0 %copy-start.1 = (bf16[6,256,256]{2,1,0:T(8,128)(2,1)S(1)}, bf16[6,256,256]{2,1,0:T(8,128)(2,1)}, u32[]{:S(2)}) copy-start(bf16[6,256,256]{2,1,0:T(8,128)(2,1)} %constant.2.clone.tab) | copy-start | bytes 2359300
  0.0 10.0 %copy-start = (bf16[12,256,256]{2,1,0:T(8,128)(2,1)S(1)}, bf16[12,256,256]{2,1,0:T(8,128)(2,1)}, u32[]{:S(2)}) copy-start(bf16[12,256,256]{2,1,0:T(8,128)(2,1)} %measured.7) | copy-start | bytes 4718596
  0.0 10.0 %copy-start.2 = (f32[2,256,256]{2,1,0:T(8,128)S(1)}, f32[2,256,256]{2,1,0:T(8,128)}, u32[]{:S(2)}) copy-start(f32[2,256,256]{2,1,0:T(8,128)} %light.7) | copy-start | bytes 1572868
  0.0 10.0 %copy-start.3 = (s32[12,2]{0,1:T(2,128)S(1)}, s32[12,2]{0,1:T(2,128)}, u32[]{:S(2)}) copy-start(s32[12,2]{0,1:T(2,128)} %param.11) | copy-start | bytes 292
  0.0 2.3 %copy-start.4 = (f32[4,512,512]{2,1,0:T(8,128)S(1)}, f32[4,512,512]{2,1,0:T(8,128)}, u32[]{:S(2)}) copy-start(f32[4,512,512]{2,1,0:T(8,128)} %objects.1) | copy-start | bytes 12582916
  2.4 7.7 %copy-start.5 = (f32[256,256]{1,0:T(8,128)S(1)}, f32[256,256]{1,0:T(8,128)}, u32[]{:S(2)}) copy-start(f32[256,256]{1,0:T(8,128)} %spread.1) | copy-start | bytes 786436
  2.9 13.9 %collective-permute-start = (bf16[4,128,512]{2,1,0:T(8,128)(2,1)S(1)}, bf16[4,128,512]{2,1,0:T(8,128)(2,1)S(1)}, u32[]{:S(2)}, u32[]{:S(2)}) collective-permute-start(bf16[4,128,512]{2,1,0:T(8,128)(2,1)S(1)} %get-tuple-element.32), channel_id=1, source_target_pairs={{0,8},{16,24},{8,0},{24,16},{1,9},{17,25},{9,1},{25,17},{2,10},{18... | collective-permute-start | bytes 1572872 | tf_op jit(solution)/shard_map/ppermute | solution.py:20
  4.5 12.3 %collective-permute-start.2 = (bf16[4,512,128]{2,1,0:T(8,128)(2,1)S(1)}, bf16[4,512,128]{2,1,0:T(8,128)(2,1)S(1)}, u32[]{:S(2)}, u32[]{:S(2)}) collective-permute-start(bf16[4,512,128]{2,1,0:T(8,128)(2,1)S(1)} %get-tuple-element.34), channel_id=1, source_target_pairs={{0,1},{2,3},{4,5},{6,7},{1,0},{3,2},{5,4},{7,6},{8,9},{10,11},{12,... | collective-permute-start | bytes 1572872 | tf_op jit(solution)/shard_map/ppermute | solution.py:20
  4.5 12.3 %collective-permute-start.3 = (bf16[4,512,128]{2,1,0:T(8,128)(2,1)S(1)}, bf16[4,512,128]{2,1,0:T(8,128)(2,1)S(1)}, u32[]{:S(2)}, u32[]{:S(2)}) collective-permute-start(bf16[4,512,128]{2,1,0:T(8,128)(2,1)S(1)} %get-tuple-element.35), channel_id=1, source_target_pairs={{1,2},{3,4},{5,6},{2,1},{4,3},{6,5},{9,10},{11,12},{13,14},{10,9},... | collective-permute-start | bytes 1572872 | tf_op jit(solution)/shard_map/ppermute | solution.py:20
  7.0 20.9 %collective-permute-start.1 = (bf16[4,128,512]{2,1,0:T(8,128)(2,1)S(1)}, bf16[4,128,512]{2,1,0:T(8,128)(2,1)S(1)}, u32[]{:S(2)}, u32[]{:S(2)}) collective-permute-start(bf16[4,128,512]{2,1,0:T(8,128)(2,1)S(1)} %get-tuple-element.33), channel_id=1, source_target_pairs={{8,16},{16,8},{9,17},{17,9},{10,18},{18,10},{11,19},{19,11},{12,20... | collective-permute-start | bytes 1572872 | tf_op jit(solution)/shard_map/ppermute | solution.py:20
  27.9 6.3 %collective-permute-start.4 = (bf16[2,4,128,128]{3,2,1,0:T(8,128)(2,1)S(1)}, bf16[2,4,128,128]{3,2,1,0:T(8,128)(2,1)S(1)}, u32[]{:S(2)}, u32[]{:S(2)}) collective-permute-start(bf16[2,4,128,128]{3,2,1,0:T(8,128)(2,1)S(1)} %get-tuple-element.38), channel_id=1, source_target_pairs={{0,1},{2,3},{4,5},{6,7},{1,0},{3,2},{5,4},{7,6},{8,9},{10,11},{12,... | collective-permute-start | bytes 786440 | tf_op jit(solution)/shard_map/ppermute | solution.py:20
  28.0 7.7 %collective-permute-start.5 = (bf16[2,4,128,128]{3,2,1,0:T(8,128)(2,1)S(1)}, bf16[2,4,128,128]{3,2,1,0:T(8,128)(2,1)S(1)}, u32[]{:S(2)}, u32[]{:S(2)}) collective-permute-start(bf16[2,4,128,128]{3,2,1,0:T(8,128)(2,1)S(1)} %get-tuple-element.39), channel_id=1, source_target_pairs={{1,2},{3,4},{5,6},{2,1},{4,3},{6,5},{9,10},{11,12},{13,14},{10,9},... | collective-permute-start | bytes 786440 | tf_op jit(solution)/shard_map/ppermute | solution.py:20
  40.6 14.0 %collective-permute-start.6 = (bf16[2,4,128,128]{3,2,1,0:T(8,128)(2,1)S(1)}, bf16[2,4,128,128]{3,2,1,0:T(8,128)(2,1)S(1)}, u32[]{:S(2)}, u32[]{:S(2)}) collective-permute-start(bf16[2,4,128,128]{3,2,1,0:T(8,128)(2,1)S(1)} %get-tuple-element.45), channel_id=1, source_target_pairs={{0,1},{2,3},{4,5},{6,7},{1,0},{3,2},{5,4},{7,6},{8,9},{10,11},{12,... | collective-permute-start | bytes 786440 | tf_op jit(solution)/shard_map/ppermute | solution.py:20
  40.6 14.0 %collective-permute-start.7 = (bf16[2,4,128,128]{3,2,1,0:T(8,128)(2,1)S(1)}, bf16[2,4,128,128]{3,2,1,0:T(8,128)(2,1)S(1)}, u32[]{:S(2)}, u32[]{:S(2)}) collective-permute-start(bf16[2,4,128,128]{3,2,1,0:T(8,128)(2,1)S(1)} %get-tuple-element.46), channel_id=1, source_target_pairs={{1,2},{3,4},{5,6},{2,1},{4,3},{6,5},{9,10},{11,12},{13,14},{10,9},... | collective-permute-start | bytes 786440 | tf_op jit(solution)/shard_map/ppermute | solution.py:20
  43.3 23.6 %collective-permute-start.10 = (bf16[4,512,128]{2,1,0:T(8,128)(2,1)S(1)}, bf16[4,512,128]{2,1,0:T(8,128)(2,1)S(1)}, u32[]{:S(2)}, u32[]{:S(2)}) collective-permute-start(bf16[4,512,128]{2,1,0:T(8,128)(2,1)S(1)} %get-tuple-element.50), channel_id=1, source_target_pairs={{0,1},{2,3},{4,5},{6,7},{1,0},{3,2},{5,4},{7,6},{8,9},{10,11},{12,... | collective-permute-start | bytes 1572872 | tf_op jit(solution)/shard_map/ppermute | solution.py:20
  43.8 23.1 %collective-permute-start.11 = (bf16[4,512,128]{2,1,0:T(8,128)(2,1)S(1)}, bf16[4,512,128]{2,1,0:T(8,128)(2,1)S(1)}, u32[]{:S(2)}, u32[]{:S(2)}) collective-permute-start(bf16[4,512,128]{2,1,0:T(8,128)(2,1)S(1)} %get-tuple-element.51), channel_id=1, source_target_pairs={{1,2},{3,4},{5,6},{2,1},{4,3},{6,5},{9,10},{11,12},{13,14},{10,9},... | collective-permute-start | bytes 1572872 | tf_op jit(solution)/shard_map/ppermute | solution.py:20
  46.5 15.3 %collective-permute-start.13 = (bf16[4,128,256]{2,1,0:T(8,128)(2,1)S(1)}, bf16[4,128,256]{2,1,0:T(8,128)(2,1)S(1)}, u32[]{:S(2)}, u32[]{:S(2)}) collective-permute-start(bf16[4,128,256]{2,1,0:T(8,128)(2,1)S(1)} %get-tuple-element.52), channel_id=1, source_target_pairs={{8,16},{16,8},{9,17},{17,9},{10,18},{18,10},{11,19},{19,11},{12,20... | collective-permute-start | bytes 786440 | tf_op jit(solution)/shard_map/ppermute | solution.py:20
  54.6 12.3 %collective-permute-start.12 = (bf16[4,128,256]{2,1,0:T(8,128)(2,1)S(1)}, bf16[4,128,256]{2,1,0:T(8,128)(2,1)S(1)}, u32[]{:S(2)}, u32[]{:S(2)}) collective-permute-start(bf16[4,128,256]{2,1,0:T(8,128)(2,1)S(1)} %get-tuple-element.37.token), channel_id=1, source_target_pairs={{0,8},{16,24},{8,0},{24,16},{1,9},{17,25},{9,1},{25,17},{2,10},{18... | collective-permute-start | bytes 786440 | tf_op jit(solution)/shard_map/ppermute | solution.py:20
  54.8 17.7 %collective-permute-start.8 = (bf16[2,4,128,128]{3,2,1,0:T(8,128)(2,1)S(1)}, bf16[2,4,128,128]{3,2,1,0:T(8,128)(2,1)S(1)}, u32[]{:S(2)}, u32[]{:S(2)}) collective-permute-start(bf16[2,4,128,128]{3,2,1,0:T(8,128)(2,1)S(1)} %get-tuple-element.47), channel_id=1, source_target_pairs={{0,8},{16,24},{8,0},{24,16},{1,9},{17,25},{9,1},{25,17},{2,10},{18... | collective-permute-start | bytes 786440 | tf_op jit(solution)/shard_map/ppermute | solution.py:20
  61.7 16.6 %collective-permute-start.9 = (bf16[2,4,128,128]{3,2,1,0:T(8,128)(2,1)S(1)}, bf16[2,4,128,128]{3,2,1,0:T(8,128)(2,1)S(1)}, u32[]{:S(2)}, u32[]{:S(2)}) collective-permute-start(bf16[2,4,128,128]{3,2,1,0:T(8,128)(2,1)S(1)} %get-tuple-element.48), channel_id=1, source_target_pairs={{8,16},{16,8},{9,17},{17,9},{10,18},{18,10},{11,19},{19,11},{12,20... | collective-permute-start | bytes 786440 | tf_op jit(solution)/shard_map/ppermute | solution.py:20

commit v6 on v5

--- a/solution.py
+++ b/solution.py
@@ -280,7 +280,7 @@
     found = jnp.int32(0)
     if mode == BESIDE:
         found = listed(INSIDE, found)
-        left = found % group
+        left = jnp.where(found < group, 0, found % group)
         for i in range(group - 1):
             order[i] = order[jnp.maximum(found - left + i, 0)]
         found = left
@@ -299,7 +299,7 @@
             def put(k, pair, here=(pl.ds(row, extent), pl.ds(col, extent)), i=i):
                 for part in range(2):
                     value = pair[part]
-                    if mode == BESIDE and i == size - 1 and size > 1:
+                    if i >= {INSIDE: 1, BESIDE: 2}.get(mode, size):
                         value = jnp.where(at + i < found, value, 0.0)
                     total[(k + part, *here)] += value
 
@@ -320,8 +320,10 @@
         run(group * i, group)
         return carry
 
-    spare = 1 if mode == BESIDE else 0
-    lax.fori_loop(0, (found + spare) // group, several, 0)
+    groups = (found + (1 if mode == BESIDE else 0)) // group
+    if mode == INSIDE:
+        groups = jnp.maximum(groups, jnp.minimum(found, 1))
+    lax.fori_loop(0, groups, several, 0)
     if mode != INSIDE:
 
         @pl.when(found % group == 1)

time: 81 us -> 81 us (level)
  waiting for transfers between devices: 22.6 us -> 20.8 us
  Pallas kernels: 23.9 us -> 25.6 us
    ppermute x14, waiting for transfers between devices: 22.6 us -> 20.8 us  [exchange(): return lax.ppermute(x, axis, pairs + [(j, i) for i, j in pairs])]
    pallas_call x4, Pallas kernels: 19.8 us -> 21.5 us  [run_slots(): pl.pallas_call(functools.partial(slots_kernel, mode), out_shape=[jax.Shap...]
  transfers between devices with their start and end apart: 14 -> 14, of which waited for: 7 -> 6; matrix products, arithmetic and copies ran while one was open for 0% -> 0% of each run, Pallas kernels for 22% -> 24%
where the time goes in v6:
time: 81 us; the launch traced here: 79.6 us
  starting transfers between devices  29.7 us (37%)
  Pallas kernels  25.6 us (32%)
  waiting for transfers between devices  20.8 us (26%)
  local copies, waits for them, and re-layouts  2.35 us (3%)
  between operations  1.08 us (1%)
    ppermute x14, starting transfers between devices, exchange(): return lax.ppermute(x, axis, pairs + [(j, i) for i, j in pairs])  29.7 us
    pallas_call x4, Pallas kernels, run_slots(): pl.pallas_call(functools.partial(slots_kernel, mode), out_shape=[jax.Shap...  21.5 us
    ppermute x14, waiting for transfers between devices, exchange(): return lax.ppermute(x, axis, pairs + [(j, i) for i, j in pairs])  20.8 us
    unnamed x12, local copies, waits for them, and re-layouts  2.35 us
    pallas_call x1, Pallas kernels, settle(): pl.pallas_call(functools.partial(settle_kernel, n), out_shape=[jax.ShapeD...  2.18 us
  transfers between devices with their start and end apart: 14, of which 6 were waited for; matrix products, arithmetic and copies ran while one was open for 0% of the time, Pallas kernels for 24%

profile of v6, /device:TPU:20, one launch (start us, length us, event | category | flops | bytes accessed | tf_op | source)
XLA Modules:
  0.0 79.6 jit_solution(39576922021733827)
XLA Ops:
  0.0 0.0 copy-start.1
  0.0 0.0 copy-start
  0.0 0.0 copy-start.3
  0.0 0.0 copy-start.4
  0.0 2.3 %copy-done.4 = f32[4,512,512]{2,1,0:T(8,128)S(1)} copy-done((f32[4,512,512]{2,1,0:T(8,128)S(1)}, f32[4,512,512]{2,1,0:T(8,128)}, u32[]{:S(2)}) %copy-start.4) | copy-done | bytes 4194328
  2.4 0.6 prepare.1
  2.9 1.6 %collective-permute-start = (bf16[4,128,512]{2,1,0:T(8,128)(2,1)S(1)}, bf16[4,128,512]{2,1,0:T(8,128)(2,1)S(1)}, u32[]{:S(2)}, u32[]{:S(2)}) collective-permute-start(bf16[4,128,512]{2,1,0:T(8,128)(2,1)S(1)} %get-tuple-element.32), channel_id=1, source_target_pairs={{0,8},{16,24},{8,0},{24,16},{1,9},{17,25},{9,1},{25,17},{2,10},{18... | collective-permute-start | bytes 1572872 | tf_op jit(solution)/shard_map/ppermute | solution.py:20
  4.5 0.0 collective-permute-start.2
  4.5 2.5 %collective-permute-start.3 = (bf16[4,512,128]{2,1,0:T(8,128)(2,1)S(1)}, bf16[4,512,128]{2,1,0:T(8,128)(2,1)S(1)}, u32[]{:S(2)}, u32[]{:S(2)}) collective-permute-start(bf16[4,512,128]{2,1,0:T(8,128)(2,1)S(1)} %get-tuple-element.35), channel_id=1, source_target_pairs={{1,2},{3,4},{5,6},{2,1},{4,3},{6,5},{9,10},{11,12},{13,14},{10,9},... | collective-permute-start | bytes 1572872 | tf_op jit(solution)/shard_map/ppermute | solution.py:20
  7.0 2.4 %collective-permute-start.1 = (bf16[4,128,512]{2,1,0:T(8,128)(2,1)S(1)}, bf16[4,128,512]{2,1,0:T(8,128)(2,1)S(1)}, u32[]{:S(2)}, u32[]{:S(2)}) collective-permute-start(bf16[4,128,512]{2,1,0:T(8,128)(2,1)S(1)} %get-tuple-element.33), channel_id=1, source_target_pairs={{8,16},{16,8},{9,17},{17,9},{10,18},{18,10},{11,19},{19,11},{12,20... | collective-permute-start | bytes 1572872 | tf_op jit(solution)/shard_map/ppermute | solution.py:20
  10.0 0.0 copy-done.1
  10.0 0.0 copy-done
  10.0 0.0 copy-done.2
  10.0 0.0 copy-done.3
  10.0 0.0 copy-done.5
  10.1 7.0 %shard_map.73 = (f32[4,768,768]{2,1,0:T(8,128)S(1)}, f32[2,256,256]{2,1,0:T(8,128)S(1)}) custom-call(s32[2,12]{1,0:T(2,128)S(1)} %bitcast.1, s32[1]{0:T(128)S(6)} %copy.24.counts, bf16[6,256,256]{2,1,0:T(8,128)(2,1)S(1)} %copy-done.1, f32[2,256,256]{2,1,0:T(8,128)S(1)} %copy-done.2, f32[256,256]{1,0:T(8,128)S(1)} %copy-done.5, ...), custom_call_target="tpu_custom_call" | custom-call | flops 2617245696 | tf_op jit(solution)/shard_map/pallas_call | solution.py:369
  17.1 0.0 collective-permute-done.refs_2_.first
  17.1 0.0 collective-permute-done.2.refs_0_
  17.1 0.0 collective-permute-done.3.refs_1_
  17.1 5.9 %shard_map.74 = (bf16[4,768,768]{2,1,0:T(8,128)(2,1)S(1)}, f32[4,768,768]{2,1,0:T(8,128)S(1)}, bf16[4,128,256]{2,1,0:T(8,128)(2,1)S(1)}) custom-call(s32[2,12]{1,0:T(2,128)S(1)} %bitcast.2, s32[1]{0:T(128)S(6)} %copy.24.counts, bf16[6,256,256]{2,1,0:T(8,128)(2,1)S(1)} %copy-done.1, ...), custom_call_target="tpu_custom_call", output_to_operand_aliasing={{0}: (9, {}), {1}: (10, {})} | custom-call | flops 2617245696 | tf_op jit(solution)/shard_map/pallas_call | solution.py:369
  23.0 4.8 %collective-permute-done.1.second.refs_0_ = bf16[4,128,512]{2,1,0:T(8,128)(2,1)S(1)} collective-permute-done((bf16[4,128,512]{2,1,0:T(8,128)(2,1)S(1)}, bf16[4,128,512]{2,1,0:T(8,128)(2,1)S(1)}, u32[]{:S(2)}, u32[]{:S(2)}) %collective-permute-start.1) | collective-permute-done | bytes 524320 | tf_op jit(solution)/shard_map/ppermute | solution.py:20
  27.8 0.1 turn.1
  27.9 0.1 collective-permute-start.4
  28.0 2.4 %collective-permute-start.5 = (bf16[2,4,128,128]{3,2,1,0:T(8,128)(2,1)S(1)}, bf16[2,4,128,128]{3,2,1,0:T(8,128)(2,1)S(1)}, u32[]{:S(2)}, u32[]{:S(2)}) collective-permute-start(bf16[2,4,128,128]{3,2,1,0:T(8,128)(2,1)S(1)} %get-tuple-element.39), channel_id=1, source_target_pairs={{1,2},{3,4},{5,6},{2,1},{4,3},{6,5},{9,10},{11,12},{13,14},{10,9},... | collective-permute-start | bytes 786440 | tf_op jit(solution)/shard_map/ppermute | solution.py:20
  30.5 3.8 %shard_map.75 = (bf16[4,768,768]{2,1,0:T(8,128)(2,1)S(1)}, f32[4,768,768]{2,1,0:T(8,128)S(1)}, bf16[4,128,256]{2,1,0:T(8,128)(2,1)S(1)}) custom-call(s32[2,12]{1,0:T(2,128)S(1)} %bitcast.3, s32[1]{0:T(128)S(6)} %copy.24.counts, bf16[6,256,256]{2,1,0:T(8,128)(2,1)S(1)} %copy-done.1, ...), custom_call_target="tpu_custom_call", output_to_operand_aliasing={{0}: (7, {}), {1}: (8, {})} | custom-call | flops 2617245696 | tf_op jit(solution)/shard_map/pallas_call | solution.py:369
  34.2 0.0 collective-permute-done.4.refs_0_
  34.2 1.5 %collective-permute-done.5.refs_1_ = bf16[2,4,128,128]{3,2,1,0:T(8,128)(2,1)S(1)} collective-permute-done((bf16[2,4,128,128]{3,2,1,0:T(8,128)(2,1)S(1)}, bf16[2,4,128,128]{3,2,1,0:T(8,128)(2,1)S(1)}, u32[]{:S(2)}, u32[]{:S(2)}) %collective-permute-start.5) | collective-permute-done | bytes 262176 | tf_op jit(solution)/shard_map/ppermute | solution.py:20
  35.7 4.9 %shard_map.76 = (bf16[4,768,768]{2,1,0:T(8,128)(2,1)S(1)}, f32[4,768,768]{2,1,0:T(8,128)S(1)}, bf16[2,4,128,128]{3,2,1,0:T(8,128)(2,1)S(1)}, bf16[2,4,128,128]{3...) custom-call(s32[2,12]{1,0:T(2,128)S(1)} %bitcast.4, ...), custom_call_target="tpu_custom_call", output_to_operand_aliasing={{0}: (8, {}), {1}: (9, {})} | custom-call | flops 2617245696 | tf_op jit(solution)/shard_map/pallas_call | solution.py:369
  40.6 0.1 collective-permute-start.6
  40.6 2.4 %collective-permute-start.7 = (bf16[2,4,128,128]{3,2,1,0:T(8,128)(2,1)S(1)}, bf16[2,4,128,128]{3,2,1,0:T(8,128)(2,1)S(1)}, u32[]{:S(2)}, u32[]{:S(2)}) collective-permute-start(bf16[2,4,128,128]{3,2,1,0:T(8,128)(2,1)S(1)} %get-tuple-element.46), channel_id=1, source_target_pairs={{1,2},{3,4},{5,6},{2,1},{4,3},{6,5},{9,10},{11,12},{13,14},{10,9},... | collective-permute-start | bytes 786440 | tf_op jit(solution)/shard_map/ppermute | solution.py:20
  43.1 0.2 sides.1
  43.3 0.5 collective-permute-start.10
  43.8 2.7 %collective-permute-start.11 = (bf16[4,512,128]{2,1,0:T(8,128)(2,1)S(1)}, bf16[4,512,128]{2,1,0:T(8,128)(2,1)S(1)}, u32[]{:S(2)}, u32[]{:S(2)}) collective-permute-start(bf16[4,512,128]{2,1,0:T(8,128)(2,1)S(1)} %get-tuple-element.51), channel_id=1, source_target_pairs={{1,2},{3,4},{5,6},{2,1},{4,3},{6,5},{9,10},{11,12},{13,14},{10,9},... | collective-permute-start | bytes 1572872 | tf_op jit(solution)/shard_map/ppermute | solution.py:20
  46.5 8.1 %collective-permute-start.13 = (bf16[4,128,256]{2,1,0:T(8,128)(2,1)S(1)}, bf16[4,128,256]{2,1,0:T(8,128)(2,1)S(1)}, u32[]{:S(2)}, u32[]{:S(2)}) collective-permute-start(bf16[4,128,256]{2,1,0:T(8,128)(2,1)S(1)} %get-tuple-element.52), channel_id=1, source_target_pairs={{8,16},{16,8},{9,17},{17,9},{10,18},{18,10},{11,19},{19,11},{12,20... | collective-permute-start | bytes 786440 | tf_op jit(solution)/shard_map/ppermute | solution.py:20
  54.6 0.0 collective-permute-done.6.first
  54.6 0.1 collective-permute-start.12
  54.7 0.0 collective-permute-done.7.second
  54.7 0.1 join.1
  54.8 2.1 %collective-permute-start.8 = (bf16[2,4,128,128]{3,2,1,0:T(8,128)(2,1)S(1)}, bf16[2,4,128,128]{3,2,1,0:T(8,128)(2,1)S(1)}, u32[]{:S(2)}, u32[]{:S(2)}) collective-permute-start(bf16[2,4,128,128]{3,2,1,0:T(8,128)(2,1)S(1)} %get-tuple-element.47), channel_id=1, source_target_pairs={{0,8},{16,24},{8,0},{24,16},{1,9},{17,25},{9,1},{25,17},{2,10},{18... | collective-permute-start | bytes 786440 | tf_op jit(solution)/shard_map/ppermute | solution.py:20
  56.9 4.9 %collective-permute-done.13.core_1 = bf16[4,128,256]{2,1,0:T(8,128)(2,1)S(1)} collective-permute-done((bf16[4,128,256]{2,1,0:T(8,128)(2,1)S(1)}, bf16[4,128,256]{2,1,0:T(8,128)(2,1)S(1)}, u32[]{:S(2)}, u32[]{:S(2)}) %collective-permute-start.13) | collective-permute-done | bytes 262176 | tf_op jit(solution)/shard_map/ppermute | solution.py:20
  61.7 4.8 %collective-permute-start.9 = (bf16[2,4,128,128]{3,2,1,0:T(8,128)(2,1)S(1)}, bf16[2,4,128,128]{3,2,1,0:T(8,128)(2,1)S(1)}, u32[]{:S(2)}, u32[]{:S(2)}) collective-permute-start(bf16[2,4,128,128]{3,2,1,0:T(8,128)(2,1)S(1)} %get-tuple-element.48), channel_id=1, source_target_pairs={{8,16},{16,8},{9,17},{17,9},{10,18},{18,10},{11,19},{19,11},{12,20... | collective-permute-start | bytes 786440 | tf_op jit(solution)/shard_map/ppermute | solution.py:20
  66.5 0.3 collective-permute-done.12.core_0
  66.9 0.0 collective-permute-done.10.side_0
  66.9 0.0 collective-permute-done.11.side_1
  66.9 2.2 %settle.1 = (f32[4,768,768]{2,1,0:T(8,128)S(1)}, f32[4,512,512]{2,1,0:T(8,128)}) custom-call(bf16[4,512,128]{2,1,0:T(8,128)(2,1)S(1)} %collective-permute-done.10.side_0, bf16[4,512,128]{2,1,0:T(8,128)(2,1)S(1)} %collective-permute-done.11.side_1, bf16[4,128,256]{2,1,0:T(8,128)(2,1)S(1)} %collective-permute-done.12.core_0, ...), custom_call_target="tpu_custom_call", output_to_operand_aliasing={{0}: (4, {})} | custom-call | tf_op jit(solution)/shard_map/settle/pallas_call | solution.py:461
  69.1 3.4 %collective-permute-done.8.edge_0 = bf16[2,4,128,128]{3,2,1,0:T(8,128)(2,1)S(1)} collective-permute-done((bf16[2,4,128,128]{3,2,1,0:T(8,128)(2,1)S(1)}, bf16[2,4,128,128]{3,2,1,0:T(8,128)(2,1)S(1)}, u32[]{:S(2)}, u32[]{:S(2)}) %collective-permute-start.8) | collective-permute-done | bytes 262176 | tf_op jit(solution)/shard_map/ppermute | solution.py:20
  72.5 5.9 %collective-permute-done.9.edge_1 = bf16[2,4,128,128]{3,2,1,0:T(8,128)(2,1)S(1)} collective-permute-done((bf16[2,4,128,128]{3,2,1,0:T(8,128)(2,1)S(1)}, bf16[2,4,128,128]{3,2,1,0:T(8,128)(2,1)S(1)}, u32[]{:S(2)}, u32[]{:S(2)}) %collective-permute-start.9) | collective-permute-done | bytes 262176 | tf_op jit(solution)/shard_map/ppermute | solution.py:20
  78.4 1.0 %finish.1 = f32[4,512,512]{2,1,0:T(8,128)} custom-call(bf16[2,4,128,128]{3,2,1,0:T(8,128)(2,1)S(1)} %collective-permute-done.8.edge_0, bf16[2,4,128,128]{3,2,1,0:T(8,128)(2,1)S(1)} %collective-permute-done.9.edge_1, f32[4,768,768]{2,1,0:T(8,128)S(1)} %get-tuple-element.53.total, f32[4,512,512]{2,1,0:T(8,128)} %get-tuple-element.54.out_in), custom_call_target="tpu_custom_call", output_to_operand_aliasing={{}: (3, {})} | custom-call | tf_op jit(solution)/shard_map/finish/pallas_call | solution.py:494
  (2 shorter events, 0.0 us)
Async XLA Ops:
  0.0 10.0 %copy-start.1 = (bf16[6,256,256]{2,1,0:T(8,128)(2,1)S(1)}, bf16[6,256,256]{2,1,0:T(8,128)(2,1)}, u32[]{:S(2)}) copy-start(bf16[6,256,256]{2,1,0:T(8,128)(2,1)} %constant.2.clone.tab) | copy-start | bytes 2359300
  0.0 10.0 %copy-start = (bf16[12,256,256]{2,1,0:T(8,128)(2,1)S(1)}, bf16[12,256,256]{2,1,0:T(8,128)(2,1)}, u32[]{:S(2)}) copy-start(bf16[12,256,256]{2,1,0:T(8,128)(2,1)} %measured.7) | copy-start | bytes 4718596
  0.0 10.0 %copy-start.2 = (f32[2,256,256]{2,1,0:T(8,128)S(1)}, f32[2,256,256]{2,1,0:T(8,128)}, u32[]{:S(2)}) copy-start(f32[2,256,256]{2,1,0:T(8,128)} %light.7) | copy-start | bytes 1572868
  0.0 10.0 %copy-start.3 = (s32[12,2]{0,1:T(2,128)S(1)}, s32[12,2]{0,1:T(2,128)}, u32[]{:S(2)}) copy-start(s32[12,2]{0,1:T(2,128)} %param.11) | copy-start | bytes 292
  0.0 2.3 %copy-start.4 = (f32[4,512,512]{2,1,0:T(8,128)S(1)}, f32[4,512,512]{2,1,0:T(8,128)}, u32[]{:S(2)}) copy-start(f32[4,512,512]{2,1,0:T(8,128)} %objects.1) | copy-start | bytes 12582916
  2.4 7.7 %copy-start.5 = (f32[256,256]{1,0:T(8,128)S(1)}, f32[256,256]{1,0:T(8,128)}, u32[]{:S(2)}) copy-start(f32[256,256]{1,0:T(8,128)} %spread.1) | copy-start | bytes 786436
  2.9 14.1 %collective-permute-start = (bf16[4,128,512]{2,1,0:T(8,128)(2,1)S(1)}, bf16[4,128,512]{2,1,0:T(8,128)(2,1)S(1)}, u32[]{:S(2)}, u32[]{:S(2)}) collective-permute-start(bf16[4,128,512]{2,1,0:T(8,128)(2,1)S(1)} %get-tuple-element.32), channel_id=1, source_target_pairs={{0,8},{16,24},{8,0},{24,16},{1,9},{17,25},{9,1},{25,17},{2,10},{18... | collective-permute-start | bytes 1572872 | tf_op jit(solution)/shard_map/ppermute | solution.py:20
  4.5 12.6 %collective-permute-start.2 = (bf16[4,512,128]{2,1,0:T(8,128)(2,1)S(1)}, bf16[4,512,128]{2,1,0:T(8,128)(2,1)S(1)}, u32[]{:S(2)}, u32[]{:S(2)}) collective-permute-start(bf16[4,512,128]{2,1,0:T(8,128)(2,1)S(1)} %get-tuple-element.34), channel_id=1, source_target_pairs={{0,1},{2,3},{4,5},{6,7},{1,0},{3,2},{5,4},{7,6},{8,9},{10,11},{12,... | collective-permute-start | bytes 1572872 | tf_op jit(solution)/shard_map/ppermute | solution.py:20
  4.5 12.6 %collective-permute-start.3 = (bf16[4,512,128]{2,1,0:T(8,128)(2,1)S(1)}, bf16[4,512,128]{2,1,0:T(8,128)(2,1)S(1)}, u32[]{:S(2)}, u32[]{:S(2)}) collective-permute-start(bf16[4,512,128]{2,1,0:T(8,128)(2,1)S(1)} %get-tuple-element.35), channel_id=1, source_target_pairs={{1,2},{3,4},{5,6},{2,1},{4,3},{6,5},{9,10},{11,12},{13,14},{10,9},... | collective-permute-start | bytes 1572872 | tf_op jit(solution)/shard_map/ppermute | solution.py:20
  7.0 20.9 %collective-permute-start.1 = (bf16[4,128,512]{2,1,0:T(8,128)(2,1)S(1)}, bf16[4,128,512]{2,1,0:T(8,128)(2,1)S(1)}, u32[]{:S(2)}, u32[]{:S(2)}) collective-permute-start(bf16[4,128,512]{2,1,0:T(8,128)(2,1)S(1)} %get-tuple-element.33), channel_id=1, source_target_pairs={{8,16},{16,8},{9,17},{17,9},{10,18},{18,10},{11,19},{19,11},{12,20... | collective-permute-start | bytes 1572872 | tf_op jit(solution)/shard_map/ppermute | solution.py:20
  27.9 6.3 %collective-permute-start.4 = (bf16[2,4,128,128]{3,2,1,0:T(8,128)(2,1)S(1)}, bf16[2,4,128,128]{3,2,1,0:T(8,128)(2,1)S(1)}, u32[]{:S(2)}, u32[]{:S(2)}) collective-permute-start(bf16[2,4,128,128]{3,2,1,0:T(8,128)(2,1)S(1)} %get-tuple-element.38), channel_id=1, source_target_pairs={{0,1},{2,3},{4,5},{6,7},{1,0},{3,2},{5,4},{7,6},{8,9},{10,11},{12,... | collective-permute-start | bytes 786440 | tf_op jit(solution)/shard_map/ppermute | solution.py:20
  28.0 7.7 %collective-permute-start.5 = (bf16[2,4,128,128]{3,2,1,0:T(8,128)(2,1)S(1)}, bf16[2,4,128,128]{3,2,1,0:T(8,128)(2,1)S(1)}, u32[]{:S(2)}, u32[]{:S(2)}) collective-permute-start(bf16[2,4,128,128]{3,2,1,0:T(8,128)(2,1)S(1)} %get-tuple-element.39), channel_id=1, source_target_pairs={{1,2},{3,4},{5,6},{2,1},{4,3},{6,5},{9,10},{11,12},{13,14},{10,9},... | collective-permute-start | bytes 786440 | tf_op jit(solution)/shard_map/ppermute | solution.py:20
  40.6 14.0 %collective-permute-start.6 = (bf16[2,4,128,128]{3,2,1,0:T(8,128)(2,1)S(1)}, bf16[2,4,128,128]{3,2,1,0:T(8,128)(2,1)S(1)}, u32[]{:S(2)}, u32[]{:S(2)}) collective-permute-start(bf16[2,4,128,128]{3,2,1,0:T(8,128)(2,1)S(1)} %get-tuple-element.45), channel_id=1, source_target_pairs={{0,1},{2,3},{4,5},{6,7},{1,0},{3,2},{5,4},{7,6},{8,9},{10,11},{12,... | collective-permute-start | bytes 786440 | tf_op jit(solution)/shard_map/ppermute | solution.py:20
  40.6 14.0 %collective-permute-start.7 = (bf16[2,4,128,128]{3,2,1,0:T(8,128)(2,1)S(1)}, bf16[2,4,128,128]{3,2,1,0:T(8,128)(2,1)S(1)}, u32[]{:S(2)}, u32[]{:S(2)}) collective-permute-start(bf16[2,4,128,128]{3,2,1,0:T(8,128)(2,1)S(1)} %get-tuple-element.46), channel_id=1, source_target_pairs={{1,2},{3,4},{5,6},{2,1},{4,3},{6,5},{9,10},{11,12},{13,14},{10,9},... | collective-permute-start | bytes 786440 | tf_op jit(solution)/shard_map/ppermute | solution.py:20
  43.3 23.6 %collective-permute-start.10 = (bf16[4,512,128]{2,1,0:T(8,128)(2,1)S(1)}, bf16[4,512,128]{2,1,0:T(8,128)(2,1)S(1)}, u32[]{:S(2)}, u32[]{:S(2)}) collective-permute-start(bf16[4,512,128]{2,1,0:T(8,128)(2,1)S(1)} %get-tuple-element.50), channel_id=1, source_target_pairs={{0,1},{2,3},{4,5},{6,7},{1,0},{3,2},{5,4},{7,6},{8,9},{10,11},{12,... | collective-permute-start | bytes 1572872 | tf_op jit(solution)/shard_map/ppermute | solution.py:20
  43.8 23.1 %collective-permute-start.11 = (bf16[4,512,128]{2,1,0:T(8,128)(2,1)S(1)}, bf16[4,512,128]{2,1,0:T(8,128)(2,1)S(1)}, u32[]{:S(2)}, u32[]{:S(2)}) collective-permute-start(bf16[4,512,128]{2,1,0:T(8,128)(2,1)S(1)} %get-tuple-element.51), channel_id=1, source_target_pairs={{1,2},{3,4},{5,6},{2,1},{4,3},{6,5},{9,10},{11,12},{13,14},{10,9},... | collective-permute-start | bytes 1572872 | tf_op jit(solution)/shard_map/ppermute | solution.py:20
  46.5 15.3 %collective-permute-start.13 = (bf16[4,128,256]{2,1,0:T(8,128)(2,1)S(1)}, bf16[4,128,256]{2,1,0:T(8,128)(2,1)S(1)}, u32[]{:S(2)}, u32[]{:S(2)}) collective-permute-start(bf16[4,128,256]{2,1,0:T(8,128)(2,1)S(1)} %get-tuple-element.52), channel_id=1, source_target_pairs={{8,16},{16,8},{9,17},{17,9},{10,18},{18,10},{11,19},{19,11},{12,20... | collective-permute-start | bytes 786440 | tf_op jit(solution)/shard_map/ppermute | solution.py:20
  54.6 12.3 %collective-permute-start.12 = (bf16[4,128,256]{2,1,0:T(8,128)(2,1)S(1)}, bf16[4,128,256]{2,1,0:T(8,128)(2,1)S(1)}, u32[]{:S(2)}, u32[]{:S(2)}) collective-permute-start(bf16[4,128,256]{2,1,0:T(8,128)(2,1)S(1)} %get-tuple-element.37.token), channel_id=1, source_target_pairs={{0,8},{16,24},{8,0},{24,16},{1,9},{17,25},{9,1},{25,17},{2,10},{18... | collective-permute-start | bytes 786440 | tf_op jit(solution)/shard_map/ppermute | solution.py:20
  54.8 17.7 %collective-permute-start.8 = (bf16[2,4,128,128]{3,2,1,0:T(8,128)(2,1)S(1)}, bf16[2,4,128,128]{3,2,1,0:T(8,128)(2,1)S(1)}, u32[]{:S(2)}, u32[]{:S(2)}) collective-permute-start(bf16[2,4,128,128]{3,2,1,0:T(8,128)(2,1)S(1)} %get-tuple-element.47), channel_id=1, source_target_pairs={{0,8},{16,24},{8,0},{24,16},{1,9},{17,25},{9,1},{25,17},{2,10},{18... | collective-permute-start | bytes 786440 | tf_op jit(solution)/shard_map/ppermute | solution.py:20
  61.7 16.6 %collective-permute-start.9 = (bf16[2,4,128,128]{3,2,1,0:T(8,128)(2,1)S(1)}, bf16[2,4,128,128]{3,2,1,0:T(8,128)(2,1)S(1)}, u32[]{:S(2)}, u32[]{:S(2)}) collective-permute-start(bf16[2,4,128,128]{3,2,1,0:T(8,128)(2,1)S(1)} %get-tuple-element.48), channel_id=1, source_target_pairs={{8,16},{16,8},{9,17},{17,9},{10,18},{18,10},{11,19},{19,11},{12,20... | collective-permute-start | bytes 786440 | tf_op jit(solution)/shard_map/ppermute | solution.py:20
